TPU v7x, 32 devices: a whole 2x2x4 slice. The times are simulated.
32 devices in a mesh: grp: 4 (over x, core), dev: 8 (over z, y).
Axes of the slice: x: 2, y: 2, z: 4, core: 2. Of those that a mesh axis runs over, the one named last changes fastest.
Arguments:
- positions: float32 [3, 32768], P(None, ('grp', 'dev')), may hold values from -6 to 6
- rotations: float32 [9, 32768], P(None, ('grp', 'dev')), may hold values from -1 to 1, as said below
- clump_kind: int32 [32768], P(('grp', 'dev')), may hold values from 0 to 7
- sub_offsets: int32 [8, 3, 64], replicated, may hold values from -8 to 8
- pair_blocks: int32 [2, 32768], P(None, ('grp', 'dev')), may hold values from 0 to 16383, as said below
- pair_count: int32 [32], P(('grp', 'dev')), may hold values from 1 to 1024, as said below
Outputs:
- clump_force: float32 [3, 32768], P(None, ('grp', 'dev'))
- clump_torque: float32 [3, 32768], P(None, ('grp', 'dev'))
Inputs may be any that keep to these rules, and one draw needn't show every extreme that they name: `rotations`: each column is a proper rotation matrix in row-major order. `pair_blocks`: the two blocks of a slot differ. A slot on a device of group g names as its first block one of group g's blocks (g * 4096 to (g + 1) * 4096 - 1) and as its second one of group g's blocks or of the 128 nearest blocks of groups g - 1 and g + 1, that is a block from g * 4096 - 128 to (g + 1) * 4096 + 127. `pair_count`: each device has at least one live slot.
All inputs are finite; a program needn't handle non-finite values.
Results may differ from a plain program's by a relative error of at most 0.0003.
Values sent between devices are 32-bit elements; how exact they have to be, the bound alone decides.
No kernel may reach another device: no remote copies, remote signals or barrier semaphores. Data moves between devices by JAX's collectives and lax.ppermute only.
A program may use at most 128 MiB of HBM per device.

v0:
```python
import functools

import jax
import jax.numpy as jnp
from jax import lax
from jax.experimental import pallas as pl
from jax.experimental.pallas import tpu as pltpu
from jax.sharding import PartitionSpec as P

RIM = 128
LANES = 128
OFFSET_UNIT = 0.125
REACH_SQUARED = 4.0
STIFFNESS = 1.0 / 256.0
CHUNK = 64
COMPS = 12
DEPTH = 2


def cross_axis(left_vec, right_vec):
    return jnp.stack(
        [
            left_vec[1] * right_vec[2] - left_vec[2] * right_vec[1],
            left_vec[2] * right_vec[0] - left_vec[0] * right_vec[2],
            left_vec[0] * right_vec[1] - left_vec[1] * right_vec[0],
        ],
        0,
    )


def split3(value):
    high = value.astype(jnp.bfloat16).astype(jnp.float32)
    rest = value - high
    middle = rest.astype(jnp.bfloat16).astype(jnp.float32)
    return high, middle, rest - middle


def pair_kernel(members, slots, head_row, place_ref, *refs):
    piece_count = members // 2
    pieces = refs[:piece_count]
    (rim_ref, off_ref, inner_ref, edge_ref, table, word_ref, words, gathered,
     parts, reach_ref, sums_ref, folded_ref, acc_near, acc_far, sem) = refs[piece_count:]
    along_z, along_y = place_ref[0], place_ref[1]
    own_rows = pieces[0].shape[1] - head_row
    inner_blocks = members * own_rows * 4
    slot_rows = head_row // 2

    owners = []
    for k in range(piece_count):
        for side in range(2):
            owners.append(
                lax.rem(along_z - k + piece_count, piece_count) * 2
                + (along_y if side == 0 else 1 - along_y)
            )
    before = [jnp.int32(0)]
    for member in range(members):
        before.append(before[-1] + place_ref[2 + member])
    total = before[-1]
    me = along_z * 2 + along_y
    begin = (total * me) // members
    finish = (total * (me + 1)) // members
    number = finish - begin

    flat = lax.broadcasted_iota(jnp.int32, (slot_rows, LANES), 0) * LANES
    column = lax.broadcasted_iota(jnp.int32, (slot_rows, LANES), 1)
    flat = flat + column
    near_list = jnp.zeros((slot_rows, LANES), jnp.float32)
    far_list = jnp.zeros((slot_rows, LANES), jnp.float32)
    for k in range(piece_count):
        for side in range(2):
            member = owners[2 * k + side]
            start = jnp.int32(0)
            for other in range(members):
                start = start + jnp.where(other < member, place_ref[2 + other], 0)
            low = jnp.maximum(start, begin) - begin
            high = jnp.minimum(start + place_ref[2 + member], finish) - begin
            shift = jnp.bitwise_and(start - begin, slots - 1)
            wanted = (flat >= low) & (flat < high)

            def moved(rows):
                turned = pltpu.roll(rows, shift & (LANES - 1), axis=1)
                same = pltpu.roll(turned, shift >> 7, axis=0)
                following = pltpu.roll(turned, (shift >> 7) + 1, axis=0)
                return jnp.where(column < (shift & (LANES - 1)), following, same)

            near_list = jnp.where(wanted, moved(pieces[k][side, pl.ds(0, slot_rows), :]), near_list)
            far_list = jnp.where(
                wanted, moved(pieces[k][side, pl.ds(slot_rows, slot_rows), :]), far_list
            )
    word_ref[pl.ds(0, slot_rows), :] = near_list.astype(jnp.int32)
    word_ref[pl.ds(slot_rows, slot_rows), :] = far_list.astype(jnp.int32)
    copy = pltpu.make_async_copy(word_ref, words, sem)
    copy.start()

    def unpack(source, row, first):
        rows = source[pl.ds(row, 32), :]
        for sub in range(4):
            shifted = rows if sub == 0 else pltpu.roll(rows, LANES - 32 * sub, axis=1)
            table[pl.ds(pl.multiple_of(first + sub * 32, 32), 32), :] = shifted

    for k in range(piece_count):
        for side in range(2):
            base = owners[2 * k + side] * (own_rows * 4)

            def take(part, carry, k=k, side=side, base=base):
                unpack(
                    pieces[k].at[side],
                    pl.multiple_of(head_row + part * 32, 8),
                    base + part * LANES,
                )
                return carry

            lax.fori_loop(0, own_rows // 32, take, 0)
    for end in range(2):
        unpack(rim_ref, end * 32, inner_blocks + end * LANES)

    def clear(turn, carry):
        acc_near[pl.ds(pl.multiple_of(turn * 48, 8), 48), :] = jnp.zeros((48, LANES), jnp.float32)
        acc_far[pl.ds(pl.multiple_of(turn * 96, 8), 96), :] = jnp.zeros((96, LANES), jnp.float32)
        return carry

    lax.fori_loop(0, acc_near.shape[0] // 48, clear, 0)

    copy.wait()

    lane = lax.broadcasted_iota(jnp.int32, (2 * CHUNK, LANES), 1)
    column_of = jnp.where(lane < LANES // 2, 0, 16)
    lane_f = (lane & 7).astype(jnp.float32)
    pick_low = lane < 8
    pick_all = lane < 16
    lane24 = lax.broadcasted_iota(jnp.int32, (24, LANES), 1)
    row8 = lax.broadcasted_iota(jnp.int32, (8, LANES), 0)
    lane8 = lax.broadcasted_iota(jnp.int32, (8, LANES), 1)
    row_first = (row8 & 3) == 0
    row_second = (row8 & 3) == 1
    half8 = (row8 < 4) == (lane8 < LANES // 2)
    ones_half = jnp.where(half8, 1.0, 0.0)
    row_sum = lax.broadcasted_iota(jnp.int32, (2 * LANES, 2 * LANES), 0)
    col_sum = lax.broadcasted_iota(jnp.int32, (2 * LANES, 2 * LANES), 1)
    halves = jnp.where(
        ((row_sum & (LANES - 1)) >= LANES // 2) == (col_sum >= LANES), 1.0, 0.0
    ).astype(jnp.bfloat16)
    row16 = lax.broadcasted_iota(jnp.int32, (16, LANES), 0)
    keeps = [jnp.where((row16 & 7) == sub, 1.0, 0.0).astype(jnp.bfloat16) for sub in range(8)]

    def fetch(first):
        def step(turn, carry):
            row = (first + turn * 8) >> 7
            base = (first + turn * 8) & (LANES - 1)
            for sub in range(8):
                index = turn * 8 + sub
                near = words[row, base + sub]
                far = words[slot_rows + row, base + sub]
                gathered[pl.ds(index, 1), :] = table[pl.ds(near, 1), :]
                gathered[pl.ds(CHUNK + index, 1), :] = table[pl.ds(far, 1), :]
            return carry

        lax.fori_loop(0, CHUNK // 8, step, 0)

    def arrange(first):
        def keep_part(slot, value):
            parts[pl.ds(pl.multiple_of(slot * slots + first, 8), CHUNK), :] = value

        packed = gathered[...]

        def spread(column):
            return jnp.take_along_axis(
                packed, column_of + column, axis=1, mode="promise_in_bounds"
            )

        kind_low = jnp.take_along_axis(
            packed, jnp.where(pick_low, 12, 28), axis=1, mode="promise_in_bounds"
        )
        pick = jnp.where(pick_all & (kind_low == lane_f), 1.0, 0.0).astype(jnp.bfloat16)
        offsets = jnp.dot(pick, off_ref[...], preferred_element_type=jnp.float32)
        where_at = []
        for axis in range(3):
            value = spread(axis)
            for mode in range(3):
                value = value + spread(3 + 3 * axis + mode) * offsets[:, mode * LANES : (mode + 1) * LANES]
            where_at.append(value)
        near = [value[:CHUNK] for value in where_at]
        far = [value[CHUNK:] for value in where_at]
        near_sq = near[0] * near[0] + near[1] * near[1] + near[2] * near[2]
        far_sq = far[0] * far[0] + far[1] * far[1] + far[2] * far[2]
        for axis, value in enumerate(near + [REACH_SQUARED - near_sq]):
            for part, piece in enumerate(split3(value)):
                keep_part(4 * part + axis, piece)
        for axis, value in enumerate([2.0 * value for value in far] + [-far_sq]):
            for part, piece in enumerate(split3(value)):
                keep_part(12 + 4 * part + axis, piece)
        for axis in range(3):
            keep_part(24 + axis, far[axis])

    one8 = jnp.ones((8, LANES), jnp.float32)

    def choose(first, second, third):
        return jnp.where(row_first, first, jnp.where(row_second, second, third))

    def prepare(base):
        def part(slot):
            return parts[pl.ds(slot * slots + base, 8), :]

        near = [[part(4 * which + axis) for axis in range(4)] for which in range(3)]
        far = [[part(12 + 4 * which + axis) for axis in range(4)] for which in range(3)]
        rows_a, rows_b = [], []
        for a, b, a_last, b_last in (
            (0, 0, near[0][3], one8),
            (0, 1, one8, far[1][3]),
            (1, 0, near[1][3], one8),
            (1, 1, one8, far[0][3]),
            (0, 2, one8, far[2][3]),
            (2, 0, near[2][3], one8),
        ):
            rows_a += near[a][:3] + [a_last]
            rows_b += far[b][:3] + [b_last]
        all_a = jnp.concatenate(rows_a, 0).astype(jnp.bfloat16)
        tiles_b = [
            jnp.concatenate(rows_b[2 * tile : 2 * tile + 2], 0).astype(jnp.bfloat16)
            for tile in range(12)
        ]
        return all_a, tiles_b

    def reach_of(all_a, tiles_b, pair):
        side_b = jnp.concatenate(
            [jnp.concatenate([tile * keeps[sub] for tile in tiles_b], 0) for sub in pair], 1
        )
        return lax.dot_general(
            all_a, side_b, (((0,), (0,)), ((), ())), preferred_element_type=jnp.float32
        )

    def sums_of(reach, base, pair):
        weight = jnp.maximum(reach, 0.0)
        weight_high = weight.astype(jnp.bfloat16)
        weight_low = (weight - weight_high.astype(jnp.float32)).astype(jnp.bfloat16)
        side_c = []
        for sub in pair:
            for which in range(3):
                row = choose(
                    *[
                        parts[pl.ds((4 * which + axis) * slots + base + sub, 8, stride=0), :]
                        for axis in range(3)
                    ]
                )
                side_c.append(jnp.where(half8, row, 0.0))
            side_c.append(ones_half)
        side_c = jnp.concatenate(side_c, 0).astype(jnp.bfloat16)
        return jnp.dot(
            jnp.concatenate([side_c, side_c], 1),
            jnp.concatenate([weight_high, weight_low], 0),
            preferred_element_type=jnp.float32,
        )

    def terms_of(sums, base, pair):
        terms = []
        for place, sub in enumerate(pair):
            mine = sums[32 * place : 32 * place + 32, LANES * place : LANES * place + LANES]
            axes = [
                parts[pl.ds((24 + axis) * slots + base + sub, 8, stride=0), :] for axis in range(3)
            ]
            force = mine[24:32] * choose(*axes) - (mine[0:8] + mine[8:16] + mine[16:24])
            terms += [
                force,
                force * choose(axes[1], axes[2], axes[0]),
                force * choose(axes[2], axes[0], axes[1]),
            ]
        terms = jnp.concatenate(terms, 0)
        terms_high = terms.astype(jnp.bfloat16)
        terms_low = (terms - terms_high.astype(jnp.float32)).astype(jnp.bfloat16)
        return jnp.concatenate([terms_high, terms_low], 1)

    def scatter(group):
        base = jnp.clip(group, 0, groups - 1) * 8
        row = base >> 7
        spot = base & (LANES - 1)
        for sub in range(8):
            lower = folded_ref[pl.ds(24 * sub, 24), :LANES]
            upper = folded_ref[pl.ds(24 * sub, 24), LANES:]
            live = (group >= 0) & (group * 8 + sub < number)
            block = words[row, spot + sub]
            here = lane24 == jnp.where(live, block & (LANES - 1), -1)
            at = pl.ds(pl.multiple_of((block >> 7) * 24, 8), 24)
            acc_near[at, :] += jnp.where(here, lower + upper, 0.0)
            block = words[slot_rows + row, spot + sub]
            here = lane24 == jnp.where(live, block & (LANES - 1), -1)
            at = pl.ds(pl.multiple_of((block >> 7) * 48, 8), 48)
            acc_far[at, :] += jnp.concatenate(
                [jnp.where(here, lower, 0.0), jnp.where(here, upper, 0.0)], 0
            )

    def chunk(turn, carry):
        first = pl.multiple_of(turn * CHUNK, CHUNK)
        fetch(first)
        arrange(first)
        return carry

    lax.fori_loop(0, (number + CHUNK - 1) // CHUNK, chunk, 0)

    groups = (number + 7) // 8
    pairs = [(2 * couple, 2 * couple + 1) for couple in range(4)]

    def octet(turn, slot):
        fresh = 4 * LANES * slot
        stale = 4 * LANES * (1 - slot)
        scatter(turn - 3)
        base = jnp.clip(turn - 2, 0, groups - 1) * 8
        terms = [
            terms_of(sums_ref[pl.ds(64 * couple, 64), :], base, pair)
            for couple, pair in enumerate(pairs)
        ]
        folded_ref[...] = jnp.dot(
            jnp.concatenate(terms, 0), halves, preferred_element_type=jnp.float32
        )
        ready = prepare(pl.multiple_of(jnp.minimum(turn, groups - 1) * 8, 8))
        for couple, pair in enumerate(pairs):
            reach_ref[pl.ds(fresh + LANES * couple, LANES), :] = reach_of(*ready, pair)
        base = jnp.clip(turn - 1, 0, groups - 1) * 8
        for couple, pair in enumerate(pairs):
            sums_ref[pl.ds(64 * couple, 64), :] = sums_of(
                reach_ref[pl.ds(stale + LANES * couple, LANES), :], base, pair
            )

    def octet_pair(turn, carry):
        for sub in range(DEPTH):
            octet(DEPTH * turn + sub, sub % 2)
        return carry

    lax.fori_loop(0, (groups + 2 + DEPTH) // DEPTH, octet_pair, 0)

    def total_of(row, half, tiles, start):
        line = (row // 3) * 8 + row % 3
        mine = acc_near[pl.ds(start * 24 + line + 4 * half, tiles, stride=24), :]
        line += 24 * half
        other = (
            acc_far[pl.ds(start * 48 + line, tiles, stride=48), :]
            + acc_far[pl.ds(start * 48 + line + 4, tiles, stride=48), :]
        )
        return (other - mine) * STIFFNESS

    for tiles, start, out in ((inner_blocks // LANES, 0, inner_ref), (2, inner_blocks // LANES, edge_ref)):
        for half in range(2):
            rows = [total_of(row, half, tiles, start) for row in range(9)]
            results = rows[0:3] + [rows[6 + (axis + 2) % 3] - rows[3 + (axis + 1) % 3] for axis in range(3)]
            for axis in range(6):
                out[pl.ds(6 * half + axis, tiles, stride=COMPS), :] = results[axis]


def neighbour_swap(rows_low, rows_high, axis):
    count = lax.axis_size(axis)
    index = lax.axis_index(axis)
    even = index % 2 == 0
    inside = [(i, i ^ 1) for i in range(count)]
    across = [(i, (i + 1) % count if i % 2 else (i - 1) % count) for i in range(count)]
    got_across = lax.ppermute(jnp.where(even, rows_low, rows_high), axis, across)
    got_inside = lax.ppermute(jnp.where(even, rows_high, rows_low), axis, inside)
    from_below = jnp.where(even, got_across, got_inside)
    from_above = jnp.where(even, got_inside, got_across)
    return from_below, from_above


def shards(positions, rotations, clump_kind, sub_offsets, pair_blocks, pair_count):
    members = lax.axis_size("dev")
    groups = lax.axis_size("grp")
    group = lax.axis_index("grp")
    me = lax.axis_index("dev")
    along_z, along_y = me // 2, me % 2
    rings = members // 2
    clumps = positions.shape[1]
    slots = pair_blocks.shape[1]
    own_blocks = clumps // 2
    kinds, _, subs = sub_offsets.shape
    head_row = 2 * slots // LANES

    values = jnp.concatenate(
        [
            positions,
            rotations,
            clump_kind.astype(jnp.float32)[None],
            jnp.zeros((3, clumps), jnp.float32),
        ],
        0,
    )
    values = values.T.reshape(own_blocks, 32)
    lane = lax.broadcasted_iota(jnp.int32, values.shape, 1)
    values = jnp.where(lane == 15, pair_count[0].astype(jnp.float32), values)
    packed = (
        values.reshape(own_blocks // LANES, 4, 32, 32)
        .transpose(0, 2, 1, 3)
        .reshape(own_blocks // 4, LANES)
    )
    inner_blocks = own_blocks * members
    blocks = pair_blocks - group * inner_blocks
    blocks = jnp.where(
        blocks < 0,
        blocks + inner_blocks + RIM,
        jnp.where(blocks >= inner_blocks, blocks + RIM, blocks),
    )
    payload = jnp.concatenate([blocks.astype(jnp.float32).reshape(head_row, LANES), packed], 0)

    pair_y = [(i, i ^ 1) for i in range(members)]
    both = jnp.stack([payload, lax.ppermute(payload, "dev", pair_y)])
    pieces = [both]
    for k in range(1, rings):
        pieces.append(
            lax.ppermute(both, "dev", [(i, (i + 2 * k) % members) for i in range(members)])
        )

    def piece_rows(member, start, count):
        z, y = member // 2, member % 2
        found = None
        for k in range(rings):
            rows = lax.dynamic_slice_in_dim(pieces[k], start, count, 1)
            side = jnp.where(along_y == y, rows[0], rows[1])
            hit = (along_z - k + rings) % rings == z
            found = side if found is None else jnp.where(hit, side, found)
        return found

    rim_rows = RIM // 4
    first_rows = piece_rows(0, head_row, rim_rows)
    last_rows = piece_rows(members - 1, head_row + packed.shape[0] - rim_rows, rim_rows)
    from_below, from_above = neighbour_swap(first_rows, last_rows, "grp")
    rims = jnp.concatenate([from_below, from_above], 0)

    offset_table = sub_offsets.astype(jnp.float32) * OFFSET_UNIT
    blank = jnp.zeros_like(offset_table)
    offset_rows = jnp.concatenate(
        [
            jnp.concatenate([offset_table, blank], 2).reshape(kinds, -1),
            jnp.concatenate([blank, offset_table], 2).reshape(kinds, -1),
        ],
        0,
    )
    offset_rows = jnp.concatenate(
        [offset_rows, jnp.zeros((LANES - 2 * kinds, offset_rows.shape[1]), jnp.float32)], 0
    ).astype(jnp.bfloat16)

    counts = jnp.zeros((members,), jnp.float32)
    for k in range(rings):
        for side in range(2):
            member = (along_z - k + rings) % rings * 2 + (along_y if side == 0 else 1 - along_y)
            counts = counts + jnp.where(
                jnp.arange(members) == member, pieces[k][side, head_row, 15], 0.0
            )
    place = jnp.concatenate(
        [jnp.stack([along_z, along_y]).astype(jnp.int32), counts.astype(jnp.int32)]
    )
    tiles = inner_blocks // LANES
    vmem = pl.BlockSpec(memory_space=pltpu.VMEM)
    inner, edge = pl.pallas_call(
        functools.partial(pair_kernel, members, slots, head_row),
        out_shape=(
            jax.ShapeDtypeStruct((tiles * COMPS, LANES), jnp.float32),
            jax.ShapeDtypeStruct((2 * COMPS, LANES), jnp.float32),
        ),
        in_specs=[pl.BlockSpec(memory_space=pltpu.SMEM)] + [vmem] * (rings + 2),
        out_specs=(vmem, vmem),
        scratch_shapes=[
            pltpu.VMEM((inner_blocks + 2 * RIM, LANES), jnp.float32),
            pltpu.VMEM((head_row, LANES), jnp.int32),
            pltpu.SMEM((head_row, LANES), jnp.int32),
            pltpu.VMEM((2 * CHUNK, LANES), jnp.float32),
            pltpu.VMEM((27 * slots, LANES), jnp.float32),
            pltpu.VMEM((8 * LANES, 2 * LANES), jnp.float32),
            pltpu.VMEM((4 * 64, 2 * LANES), jnp.float32),
            pltpu.VMEM((192, 2 * LANES), jnp.float32),
            pltpu.VMEM(((tiles + 2) * 24, LANES), jnp.float32),
            pltpu.VMEM(((tiles + 2) * 48, LANES), jnp.float32),
            pltpu.SemaphoreType.DMA,
        ],
        name="pair_kernel",
    )(place, *pieces, rims, offset_rows)

    below, above = neighbour_swap(edge[:COMPS], edge[COMPS:], "grp")
    below = jnp.where(group > 0, below, 0.0)
    above = jnp.where(group < groups - 1, above, 0.0)
    inner = inner + jnp.concatenate(
        [below, jnp.zeros(((tiles - 2) * COMPS, LANES), jnp.float32), above], 0
    )

    own_rows = tiles * COMPS // members
    ranks = inner.reshape(rings, 2, own_rows, LANES)
    mine = lax.dynamic_index_in_dim(ranks, along_y, 1, False)
    other = lax.dynamic_index_in_dim(ranks, 1 - along_y, 1, False)
    column = mine + lax.ppermute(other, "dev", pair_y)
    summed = lax.dynamic_index_in_dim(column, along_z, 0, False)
    for k in range(1, rings):
        part = lax.dynamic_index_in_dim(column, (along_z + k) % rings, 0, False)
        summed = summed + lax.ppermute(
            part, "dev", [(i, (i + 2 * k) % members) for i in range(members)]
        )
    summed = summed.reshape(own_blocks // LANES, 2, 6, LANES).transpose(2, 0, 3, 1).reshape(6, clumps)
    clump_force = summed[0:3]
    clump_torque = summed[3:6] - cross_axis(positions, clump_force)
    return (clump_force, clump_torque)


def solution(mesh):
    placed = (
        P(None, ("grp", "dev")),
        P(None, ("grp", "dev")),
        P(("grp", "dev")),
        P(),
        P(None, ("grp", "dev")),
        P(("grp", "dev")),
    )
    return jax.shard_map(
        shards,
        mesh=mesh,
        in_specs=placed,
        out_specs=(P(None, ("grp", "dev")), P(None, ("grp", "dev"))),
        check_vma=False,
    )
```

profile of v0, /device:TPU:0, one launch (start us, length us, event | category | flops | bytes accessed | tf_op | source)
XLA Modules:
  0.0 83.3 jit_solution(17017626586398065097)
XLA Ops:
  0.6 0.0 copy-start.7
  0.7 0.7 copy-done.7
  1.4 0.7 convert_element_type.22
  2.1 0.1 pad.23.clone
  2.1 0.0 copy-done.4
  2.1 0.8 maximum_bitcast_fusion
  2.9 0.2 copy.8
  3.1 0.1 reshape.78
  4.0 0.2 copy.9
  4.1 0.2 reshape.79
  4.3 3.1 %collective-permute-start = (f32[144,128]{1,0:T(8,128)S(1)}, f32[144,128]{1,0:T(8,128)S(1)}, u32[]{:S(2)}, u32[]{:S(2)}) collective-permute-start(f32[144,128]{1,0:T(8,128)S(1)} %constant_dynamic-update-slice_fusion), channel_id=1, source_target_pairs={{0,1},{1,0},{2,3},{3,2},{4,5},{5,4},{6,7},{7,6},{8,9},{9,8},{10,11... | collective-permute-start | bytes 221192 | tf_op jit(solution)/shard_map/ppermute | solution.py:401
  7.4 0.6 slice.176
  8.0 0.1 copy-done.6
  8.1 0.1 pad.12.clone
  8.2 0.1 pad_bitcast_fusion.1
  8.3 1.5 %collective-permute-done = f32[144,128]{1,0:T(8,128)S(1)} collective-permute-done((f32[144,128]{1,0:T(8,128)S(1)}, f32[144,128]{1,0:T(8,128)S(1)}, u32[]{:S(2)}, u32[]{:S(2)}) %collective-permute-start) | collective-permute-done | bytes 73760 | tf_op jit(solution)/shard_map/ppermute | solution.py:401
  9.7 2.1 %collective-permute-start.1 = (f32[2,144,128]{2,1,0:T(8,128)S(1)}, f32[2,144,128]{2,1,0:T(8,128)S(1)}, u32[]{:S(2)}, u32[]{:S(2)}) collective-permute-start(f32[2,144,128]{2,1,0:T(8,128)S(1)} %pad_maximum_fusion.refs_0_), channel_id=1, source_target_pairs={{0,2},{1,3},{2,4},{3,5},{4,6},{5,7},{6,0},{7,1},{8,10},{9,11},{10,... | collective-permute-start | bytes 442376 | tf_op jit(solution)/shard_map/ppermute | solution.py:405
  11.9 2.6 %collective-permute-start.2 = (f32[2,144,128]{2,1,0:T(8,128)S(1)}, f32[2,144,128]{2,1,0:T(8,128)S(1)}, u32[]{:S(2)}, u32[]{:S(2)}) collective-permute-start(f32[2,144,128]{2,1,0:T(8,128)S(1)} %pad_maximum_fusion.refs_0_), channel_id=1, source_target_pairs={{0,4},{1,5},{2,6},{3,7},{4,0},{5,1},{6,2},{7,3},{8,12},{9,13},{10,... | collective-permute-start | bytes 442376 | tf_op jit(solution)/shard_map/ppermute | solution.py:405
  14.5 1.3 %collective-permute-start.3 = (f32[2,144,128]{2,1,0:T(8,128)S(1)}, f32[2,144,128]{2,1,0:T(8,128)S(1)}, u32[]{:S(2)}, u32[]{:S(2)}) collective-permute-start(f32[2,144,128]{2,1,0:T(8,128)S(1)} %pad_maximum_fusion.refs_0_), channel_id=1, source_target_pairs={{0,6},{1,7},{2,0},{3,1},{4,2},{5,3},{6,4},{7,5},{8,14},{9,15},{10,... | collective-permute-start | bytes 442376 | tf_op jit(solution)/shard_map/ppermute | solution.py:405
  15.8 0.7 maximum_maximum_fusion.refs_5_
  16.5 0.6 slice.177
  17.1 1.6 %collective-permute-done.1.refs_1_ = f32[2,144,128]{2,1,0:T(8,128)S(1)} collective-permute-done((f32[2,144,128]{2,1,0:T(8,128)S(1)}, f32[2,144,128]{2,1,0:T(8,128)S(1)}, u32[]{:S(2)}, u32[]{:S(2)}) %collective-permute-start.1) | collective-permute-done | bytes 147488 | tf_op jit(solution)/shard_map/ppermute | solution.py:405
  18.7 4.3 %collective-permute-done.2.refs_2_ = f32[2,144,128]{2,1,0:T(8,128)S(1)} collective-permute-done((f32[2,144,128]{2,1,0:T(8,128)S(1)}, f32[2,144,128]{2,1,0:T(8,128)S(1)}, u32[]{:S(2)}, u32[]{:S(2)}) %collective-permute-start.2) | collective-permute-done | bytes 147488 | tf_op jit(solution)/shard_map/ppermute | solution.py:405
  23.0 0.0 collective-permute-done.3.refs_3_
  23.0 0.0 copy-done
  23.1 0.1 collective-permute-start.5
  23.1 1.6 %collective-permute-start.4 = (f32[32,128]{1,0:T(8,128)S(1)}, f32[32,128]{1,0:T(8,128)S(1)}, u32[]{:S(2)}, u32[]{:S(2)}) collective-permute-start(f32[32,128]{1,0:T(8,128)S(1)} %get-tuple-element.6), channel_id=1, source_target_pairs={{0,24},{8,16},{16,8},{24,0},{1,25},{9,17},{17,9},{25,1},{2,26},{10... | collective-permute-start | bytes 49160 | tf_op jit(solution)/shard_map/ppermute | solution.py:354
  24.8 0.6 fusion.19
  25.4 0.0 copy-done.2
  25.4 0.7 fusion.20
  26.0 0.6 fusion.21
  26.6 5.0 %fusion.16 = s32[8]{0:T(128)S(1)} fusion(f32[]{:T(128)} %bitcast.15, s32[]{:T(128)S(6)} %add.187, f32[]{:T(128)} %bitcast.14, s32[]{:T(128)S(6)} %add.185, f32[]{:T(128)} %bitcast.13, s32[]{:T(128)S(6)} %add.181, f32[]{:T(128)} %bitcast.12, s32[]{:T(128)S(6)} %add.179, f32[]{:T(128)} %bitcast.11, s32[]{:T(128)S(6)} %add.175, f32[]{:T(128)} %bitcast.10, ...), kind=kLoop, calls=%fused_computation.64 | loop fusion | flops 192 | bytes 96 | tf_op jit(solution)/shard_map/convert_element_type | solution.py:445
  31.6 0.6 pad_add_fusion.place_ref
  32.2 0.0 collective-permute-done.5
  32.2 0.0 collective-permute-done.4
  32.2 0.6 pad_maximum_fusion.1.refs_4_
  32.8 22.8 %pair_kernel.1 = (f32[384,128]{1,0:T(8,128)}, f32[24,128]{1,0:T(8,128)}) custom-call(s32[10]{0:T(128)} %pad_add_fusion.place_ref, f32[2,144,128]{2,1,0:T(8,128)} %copy-done, f32[2,144,128]{2,1,0:T(8,128)} %copy-done.1, f32[2,144,128]{2,1,0:T(8,128)} %copy-done.2, f32[2,144,128]{2,1,0:T(8,128)} %copy-done.3, f32[64,128]{1,0:T(8,128)} %pad_maximum_fusion.1.refs_4_, ...), custom_call_target="tpu_custom_call" | custom-call | tf_op jit(solution)/shard_map/pair_kernel/pallas_call | solution.py:449
  55.6 0.8 slice_select_fusion.9
  56.4 3.2 %collective-permute-start.6 = (f32[12,128]{1,0:T(8,128)S(1)}, f32[12,128]{1,0:T(8,128)S(1)}, u32[]{:S(2)}, u32[]{:S(2)}) collective-permute-start(f32[12,128]{1,0:T(8,128)S(1)} %get-tuple-element.30), channel_id=1, source_target_pairs={{0,24},{8,16},{16,8},{24,0},{1,25},{9,17},{17,9},{25,1},{2,26},{10... | collective-permute-start | bytes 18440 | tf_op jit(solution)/shard_map/ppermute | solution.py:354
  59.6 0.0 collective-permute-start.7
  59.6 0.1 pad.8.clone
  59.7 1.3 %collective-permute-done.6 = f32[12,128]{1,0:T(8,128)S(1)} collective-permute-done((f32[12,128]{1,0:T(8,128)S(1)}, f32[12,128]{1,0:T(8,128)S(1)}, u32[]{:S(2)}, u32[]{:S(2)}) %collective-permute-start.6) | collective-permute-done | bytes 6176 | tf_op jit(solution)/shard_map/ppermute | solution.py:354
  61.0 0.0 collective-permute-done.7
  61.0 1.0 %maximum_add_fusion = f32[384,128]{1,0:T(8,128)S(1)} fusion(f32[384,128]{1,0:T(8,128)} %get-tuple-element.4, f32[12,128]{1,0:T(8,128)S(1)} %get-tuple-element.29, f32[12,128]{1,0:T(8,128)S(1)} %get-tuple-element.28, f32[384]{0:T(512)S(1)} %pad.8.clone), kind=kLoop, calls=%fused_computation.1 | loop fusion | flops 147456 | bytes 407040 | tf_op jit(solution)/shard_map/add | solution.py:476
  62.1 1.6 %collective-permute-start.8 = (f32[4,48,128]{2,1,0:T(8,128)S(1)}, f32[4,48,128]{2,1,0:T(8,128)S(1)}, u32[]{:S(2)}, u32[]{:S(2)}) collective-permute-start(f32[4,48,128]{2,1,0:T(8,128)S(1)} %dynamic-slice_bitcast_fusion), channel_id=1, source_target_pairs={{0,1},{1,0},{2,3},{3,2},{4,5},{5,4},{6,7},{7,6},{8,9},{9,8},{10,11... | collective-permute-start | bytes 294920 | tf_op jit(solution)/shard_map/ppermute | solution.py:484
  63.7 4.1 %collective-permute-done.8 = f32[4,48,128]{2,1,0:T(8,128)S(1)} collective-permute-done((f32[4,48,128]{2,1,0:T(8,128)S(1)}, f32[4,48,128]{2,1,0:T(8,128)S(1)}, u32[]{:S(2)}, u32[]{:S(2)}) %collective-permute-start.8) | collective-permute-done | bytes 98336 | tf_op jit(solution)/shard_map/ppermute | solution.py:484
  67.8 2.6 %collective-permute-start.10 = (f32[48,128]{1,0:T(8,128)S(1)}, f32[48,128]{1,0:T(8,128)S(1)}, u32[]{:S(2)}, u32[]{:S(2)}) collective-permute-start(f32[48,128]{1,0:T(8,128)S(1)} %get-tuple-element.17), channel_id=1, source_target_pairs={{0,4},{1,5},{2,6},{3,7},{4,0},{5,1},{6,2},{7,3},{8,12},{9,13},{10,... | collective-permute-start | bytes 73736 | tf_op jit(solution)/shard_map/ppermute | solution.py:488
  70.4 3.4 %collective-permute-start.11 = (f32[48,128]{1,0:T(8,128)S(1)}, f32[48,128]{1,0:T(8,128)S(1)}, u32[]{:S(2)}, u32[]{:S(2)}) collective-permute-start(f32[48,128]{1,0:T(8,128)S(1)} %get-tuple-element.16), channel_id=1, source_target_pairs={{0,6},{1,7},{2,0},{3,1},{4,2},{5,3},{6,4},{7,5},{8,14},{9,15},{10,... | collective-permute-start | bytes 73736 | tf_op jit(solution)/shard_map/ppermute | solution.py:488
  73.8 0.0 collective-permute-start.9
  73.8 0.0 collective-permute-done.10
  73.8 1.5 %collective-permute-done.11 = f32[48,128]{1,0:T(8,128)S(1)} collective-permute-done((f32[48,128]{1,0:T(8,128)S(1)}, f32[48,128]{1,0:T(8,128)S(1)}, u32[]{:S(2)}, u32[]{:S(2)}) %collective-permute-start.11) | collective-permute-done | bytes 24608 | tf_op jit(solution)/shard_map/ppermute | solution.py:488
  75.4 4.1 %collective-permute-done.9 = f32[48,128]{1,0:T(8,128)S(1)} collective-permute-done((f32[48,128]{1,0:T(8,128)S(1)}, f32[48,128]{1,0:T(8,128)S(1)}, u32[]{:S(2)}, u32[]{:S(2)}) %collective-permute-start.9) | collective-permute-done | bytes 24608 | tf_op jit(solution)/shard_map/ppermute | solution.py:488
  79.5 0.1 copy.12
  79.7 0.2 squeeze.93
  79.9 0.1 copy.13
  80.0 0.2 squeeze.94
  80.2 0.1 copy.14
  80.4 0.2 squeeze.95
  80.5 0.3 copy.11
  80.8 0.5 slice.169
  81.3 0.3 copy.10
  81.6 0.0 copy-start.5
  81.6 1.1 %slice.167 = f32[3,1024]{1,0:T(4,128)} reshape(f32[3,4,128,2]{3,2,1,0:T(8,128)S(1)} %copy.10) | data formatting | bytes 24576 | tf_op jit(solution)/shard_map/slice | solution.py:492
  82.7 0.6 maximum_subtract_fusion
  (32 shorter events, 0.2 us)
Async XLA Ops:
  0.6 0.7 copy-start.7
  0.6 1.5 %copy-start.4 = (f32[9,1024]{1,0:T(8,128)S(1)}, f32[9,1024]{1,0:T(8,128)}, u32[]{:S(2)}) copy-start(f32[9,1024]{1,0:T(8,128)} %param.7) | copy-start | bytes 110596
  4.3 5.4 %collective-permute-start = (f32[144,128]{1,0:T(8,128)S(1)}, f32[144,128]{1,0:T(8,128)S(1)}, u32[]{:S(2)}, u32[]{:S(2)}) collective-permute-start(f32[144,128]{1,0:T(8,128)S(1)} %constant_dynamic-update-slice_fusion), channel_id=1, source_target_pairs={{0,1},{1,0},{2,3},{3,2},{4,5},{5,4},{6,7},{7,6},{8,9},{9,8},{10,11... | collective-permute-start | bytes 221192 | tf_op jit(solution)/shard_map/ppermute | solution.py:401
  7.4 0.7 copy-start.6
  9.7 13.3 %copy-start = (f32[2,144,128]{2,1,0:T(8,128)}, f32[2,144,128]{2,1,0:T(8,128)S(1)}, u32[]{:S(2)}) copy-start(f32[2,144,128]{2,1,0:T(8,128)S(1)} %pad_maximum_fusion.refs_0_) | copy-start | bytes 442372
  9.7 9.0 %collective-permute-start.1 = (f32[2,144,128]{2,1,0:T(8,128)S(1)}, f32[2,144,128]{2,1,0:T(8,128)S(1)}, u32[]{:S(2)}, u32[]{:S(2)}) collective-permute-start(f32[2,144,128]{2,1,0:T(8,128)S(1)} %pad_maximum_fusion.refs_0_), channel_id=1, source_target_pairs={{0,2},{1,3},{2,4},{3,5},{4,6},{5,7},{6,0},{7,1},{8,10},{9,11},{10,... | collective-permute-start | bytes 442376 | tf_op jit(solution)/shard_map/ppermute | solution.py:405
  11.9 11.1 %collective-permute-start.2 = (f32[2,144,128]{2,1,0:T(8,128)S(1)}, f32[2,144,128]{2,1,0:T(8,128)S(1)}, u32[]{:S(2)}, u32[]{:S(2)}) collective-permute-start(f32[2,144,128]{2,1,0:T(8,128)S(1)} %pad_maximum_fusion.refs_0_), channel_id=1, source_target_pairs={{0,4},{1,5},{2,6},{3,7},{4,0},{5,1},{6,2},{7,3},{8,12},{9,13},{10,... | collective-permute-start | bytes 442376 | tf_op jit(solution)/shard_map/ppermute | solution.py:405
  14.5 8.6 %collective-permute-start.3 = (f32[2,144,128]{2,1,0:T(8,128)S(1)}, f32[2,144,128]{2,1,0:T(8,128)S(1)}, u32[]{:S(2)}, u32[]{:S(2)}) collective-permute-start(f32[2,144,128]{2,1,0:T(8,128)S(1)} %pad_maximum_fusion.refs_0_), channel_id=1, source_target_pairs={{0,6},{1,7},{2,0},{3,1},{4,2},{5,3},{6,4},{7,5},{8,14},{9,15},{10,... | collective-permute-start | bytes 442376 | tf_op jit(solution)/shard_map/ppermute | solution.py:405
  18.7 6.0 %copy-start.1 = (f32[2,144,128]{2,1,0:T(8,128)}, f32[2,144,128]{2,1,0:T(8,128)S(1)}, u32[]{:S(2)}) copy-start(f32[2,144,128]{2,1,0:T(8,128)S(1)} %collective-permute-done.1.refs_1_) | copy-start | bytes 442372
  23.0 2.4 %copy-start.2 = (f32[2,144,128]{2,1,0:T(8,128)}, f32[2,144,128]{2,1,0:T(8,128)S(1)}, u32[]{:S(2)}) copy-start(f32[2,144,128]{2,1,0:T(8,128)S(1)} %collective-permute-done.2.refs_2_) | copy-start | bytes 442372
  23.0 9.8 %copy-start.3 = (f32[2,144,128]{2,1,0:T(8,128)}, f32[2,144,128]{2,1,0:T(8,128)S(1)}, u32[]{:S(2)}) copy-start(f32[2,144,128]{2,1,0:T(8,128)S(1)} %collective-permute-done.3.refs_3_) | copy-start | bytes 442372
  23.1 9.1 %collective-permute-start.5 = (f32[32,128]{1,0:T(8,128)S(1)}, f32[32,128]{1,0:T(8,128)S(1)}, u32[]{:S(2)}, u32[]{:S(2)}) collective-permute-start(f32[32,128]{1,0:T(8,128)S(1)} %select_bitcast_fusion.1), channel_id=1, source_target_pairs={{0,8},{8,0},{16,24},{24,16},{1,9},{9,1},{17,25},{25,17},{2,10},{10... | collective-permute-start | bytes 49160 | tf_op jit(solution)/shard_map/ppermute | solution.py:355
  23.1 9.0 %collective-permute-start.4 = (f32[32,128]{1,0:T(8,128)S(1)}, f32[32,128]{1,0:T(8,128)S(1)}, u32[]{:S(2)}, u32[]{:S(2)}) collective-permute-start(f32[32,128]{1,0:T(8,128)S(1)} %get-tuple-element.6), channel_id=1, source_target_pairs={{0,24},{8,16},{16,8},{24,0},{1,25},{9,17},{17,9},{25,1},{2,26},{10... | collective-permute-start | bytes 49160 | tf_op jit(solution)/shard_map/ppermute | solution.py:354
  56.4 4.6 %collective-permute-start.6 = (f32[12,128]{1,0:T(8,128)S(1)}, f32[12,128]{1,0:T(8,128)S(1)}, u32[]{:S(2)}, u32[]{:S(2)}) collective-permute-start(f32[12,128]{1,0:T(8,128)S(1)} %get-tuple-element.30), channel_id=1, source_target_pairs={{0,24},{8,16},{16,8},{24,0},{1,25},{9,17},{17,9},{25,1},{2,26},{10... | collective-permute-start | bytes 18440 | tf_op jit(solution)/shard_map/ppermute | solution.py:354
  59.6 1.4 %collective-permute-start.7 = (f32[12,128]{1,0:T(8,128)S(1)}, f32[12,128]{1,0:T(8,128)S(1)}, u32[]{:S(2)}, u32[]{:S(2)}) collective-permute-start(f32[12,128]{1,0:T(8,128)S(1)} %get-tuple-element.31), channel_id=1, source_target_pairs={{0,8},{8,0},{16,24},{24,16},{1,9},{9,1},{17,25},{25,17},{2,10},{10... | collective-permute-start | bytes 18440 | tf_op jit(solution)/shard_map/ppermute | solution.py:355
  62.1 5.7 %collective-permute-start.8 = (f32[4,48,128]{2,1,0:T(8,128)S(1)}, f32[4,48,128]{2,1,0:T(8,128)S(1)}, u32[]{:S(2)}, u32[]{:S(2)}) collective-permute-start(f32[4,48,128]{2,1,0:T(8,128)S(1)} %dynamic-slice_bitcast_fusion), channel_id=1, source_target_pairs={{0,1},{1,0},{2,3},{3,2},{4,5},{5,4},{6,7},{7,6},{8,9},{9,8},{10,11... | collective-permute-start | bytes 294920 | tf_op jit(solution)/shard_map/ppermute | solution.py:484
  67.8 6.1 %collective-permute-start.10 = (f32[48,128]{1,0:T(8,128)S(1)}, f32[48,128]{1,0:T(8,128)S(1)}, u32[]{:S(2)}, u32[]{:S(2)}) collective-permute-start(f32[48,128]{1,0:T(8,128)S(1)} %get-tuple-element.17), channel_id=1, source_target_pairs={{0,4},{1,5},{2,6},{3,7},{4,0},{5,1},{6,2},{7,3},{8,12},{9,13},{10,... | collective-permute-start | bytes 73736 | tf_op jit(solution)/shard_map/ppermute | solution.py:488
  70.4 4.9 %collective-permute-start.11 = (f32[48,128]{1,0:T(8,128)S(1)}, f32[48,128]{1,0:T(8,128)S(1)}, u32[]{:S(2)}, u32[]{:S(2)}) collective-permute-start(f32[48,128]{1,0:T(8,128)S(1)} %get-tuple-element.16), channel_id=1, source_target_pairs={{0,6},{1,7},{2,0},{3,1},{4,2},{5,3},{6,4},{7,5},{8,14},{9,15},{10,... | collective-permute-start | bytes 73736 | tf_op jit(solution)/shard_map/ppermute | solution.py:488
  73.8 5.6 %collective-permute-start.9 = (f32[48,128]{1,0:T(8,128)S(1)}, f32[48,128]{1,0:T(8,128)S(1)}, u32[]{:S(2)}, u32[]{:S(2)}) collective-permute-start(f32[48,128]{1,0:T(8,128)S(1)} %get-tuple-element.15), channel_id=1, source_target_pairs={{0,2},{1,3},{2,4},{3,5},{4,6},{5,7},{6,0},{7,1},{8,10},{9,11},{10,... | collective-permute-start | bytes 73736 | tf_op jit(solution)/shard_map/ppermute | solution.py:488
  81.6 1.1 %copy-start.5 = (f32[3,1024]{1,0:T(4,128)S(1)}, f32[3,1024]{1,0:T(4,128)}, u32[]{:S(2)}) copy-start(f32[3,1024]{1,0:T(4,128)} %param.6) | copy-start | bytes 36868
where the time goes:
time: 84.5 us; the launch traced here: 83.3 us
  Pallas kernels  22.8 us (27%)
  starting transfers between devices  21.7 us (26%)
  waiting for transfers between devices  18.3 us (22%)
  other arithmetic  11 us (13%)
  local copies, waits for them, and re-layouts  7.98 us (9%)
  between operations  1.58 us (2%)
    pallas_call x1, Pallas kernels, shards(): pl.pallas_call(functools.partial(pair_kernel, members, slots, head_row),...  22.8 us
    ppermute x3, starting transfers between devices, shards(): lax.ppermute(both, 'dev', [(i, (i + 2 * k) % members) for i in range(memb...  6.07 us
    ppermute x3, starting transfers between devices, shards(): lax.ppermute(part, 'dev', [(i, (i + 2 * k) % members) for i in range(memb...  6.05 us
    ppermute x3, waiting for transfers between devices, shards(): lax.ppermute(both, 'dev', [(i, (i + 2 * k) % members) for i in range(memb...  5.87 us
    ppermute x3, waiting for transfers between devices, shards(): lax.ppermute(part, 'dev', [(i, (i + 2 * k) % members) for i in range(memb...  5.62 us
    convert_element_type x1, other arithmetic, shards(): counts.astype(jnp.int32)  4.97 us
    ppermute x2, starting transfers between devices, neighbour_swap(): lax.ppermute(jnp.where(even, rows_low, rows_high), axis, across)  4.84 us
    ppermute x1, waiting for transfers between devices, shards(): column = mine + lax.ppermute(other, 'dev', pair_y)  4.09 us
  transfers between devices with their start and end apart: 12, of which 7 were waited for; matrix products, arithmetic and copies ran while one was open for 12% of the time, Pallas kernels for 0%

commit v1 on v0

--- a/solution.py
+++ b/solution.py
@@ -14,18 +14,9 @@
 STIFFNESS = 1.0 / 256.0
 CHUNK = 64
 COMPS = 12
+PARAMS = 10
+ROWS = 24
 DEPTH = 2
-
-
-def cross_axis(left_vec, right_vec):
-    return jnp.stack(
-        [
-            left_vec[1] * right_vec[2] - left_vec[2] * right_vec[1],
-            left_vec[2] * right_vec[0] - left_vec[0] * right_vec[2],
-            left_vec[0] * right_vec[1] - left_vec[1] * right_vec[0],
-        ],
-        0,
-    )
 
 
 def split3(value):
@@ -35,28 +26,135 @@
     return high, middle, rest - middle
 
 
-def pair_kernel(members, slots, head_row, place_ref, *refs):
+def payload_kernel(slots, members, position_ref, rotation_ref, kind_ref, pair_ref, count_ref, out_ref):
+    clumps = position_ref.shape[1]
+    blocks = clumps // 2
+    inner_blocks = blocks * members
+    wide = 2 * LANES
+    row = lax.broadcasted_iota(jnp.int32, (wide, wide), 0)
+    column = lax.broadcasted_iota(jnp.int32, (wide, wide), 1)
+    source = jnp.where(column < LANES, 2 * column, 2 * column - (wide - 1))
+    picked = jnp.where(row == source, 1.0, 0.0).astype(jnp.bfloat16)
+    parts = []
+    for turn in range(clumps // wide):
+        at = slice(turn * wide, (turn + 1) * wide)
+        kinds = kind_ref[2 * turn : 2 * turn + 2, :].astype(jnp.float32)
+        value = jnp.concatenate(
+            [
+                position_ref[:, at],
+                rotation_ref[0:6, at],
+                jnp.concatenate([kinds[0:1], kinds[1:2]], 1),
+                jnp.zeros((16 - PARAMS, wide), jnp.float32),
+            ],
+            0,
+        )
+        parts += [piece.astype(jnp.bfloat16) for piece in split3(value)]
+    sorted_parts = jnp.dot(
+        jnp.concatenate(parts, 0), picked, preferred_element_type=jnp.float32
+    )
+    for turn in range(clumps // wide):
+        high, middle, low = (sorted_parts[16 * (3 * turn + part) : 16 * (3 * turn + part) + 16] for part in range(3))
+        value = (high + middle) + low
+        at = slice(turn * LANES, (turn + 1) * LANES)
+        out_ref[0:PARAMS, at] = value[0:PARAMS, :LANES]
+        out_ref[PARAMS : 2 * PARAMS, at] = value[0:PARAMS, LANES:]
+    pairs = pair_ref[...] - lax.axis_index("grp") * inner_blocks
+    pairs = jnp.where(
+        pairs < 0,
+        pairs + inner_blocks + RIM,
+        jnp.where(pairs >= inner_blocks, pairs + RIM, pairs),
+    )
+    live = lax.broadcasted_iota(jnp.int32, pairs.shape, 1) < count_ref[0]
+    pairs = jnp.where(live, pairs, -1).astype(jnp.float32)
+    lists = slots // blocks
+    for which in range(2):
+        for part in range(lists):
+            out_ref[pl.ds(2 * PARAMS + which * lists + part, 1), :] = pairs[
+                which : which + 1, part * blocks : (part + 1) * blocks
+            ]
+
+
+def finish_kernel(own_ref, *refs):
+    parts = refs[:-4]
+    position_ref, force_ref, torque_ref, total_ref = refs[-4:]
+    total = own_ref[...]
+    for part in parts:
+        total = total + part[...]
+    total_ref[...] = total
+    tiles = own_ref.shape[0] // COMPS
+    wide = 2 * LANES
+    row = lax.broadcasted_iota(jnp.int32, (wide, wide), 0)
+    column = lax.broadcasted_iota(jnp.int32, (wide, wide), 1)
+    target = jnp.where(row < LANES, 2 * row, 2 * row - (wide - 1))
+    placed = jnp.where(column == target, 1.0, 0.0).astype(jnp.bfloat16)
+    halves = [
+        jnp.concatenate(
+            [total_ref[pl.ds(6 * half + comp, tiles, stride=COMPS), :] for comp in range(6)], 0
+        )
+        for half in range(2)
+    ]
+    value = jnp.concatenate(halves, 1)
+    rows = value.shape[0]
+    joined = jnp.dot(
+        jnp.concatenate([part.astype(jnp.bfloat16) for part in split3(value)], 0),
+        placed,
+        preferred_element_type=jnp.float32,
+    )
+    value = (joined[0:rows] + joined[rows : 2 * rows]) + joined[2 * rows : 3 * rows]
+    comps = [value[comp * tiles : (comp + 1) * tiles] for comp in range(6)]
+    centre = [
+        jnp.concatenate(
+            [position_ref[axis : axis + 1, tile * wide : (tile + 1) * wide] for tile in range(tiles)], 0
+        )
+        for axis in range(3)
+    ]
+    for axis in range(3):
+        after, last = (axis + 1) % 3, (axis + 2) % 3
+        torque = comps[3 + axis] - (centre[after] * comps[last] - centre[last] * comps[after])
+        for tile in range(tiles):
+            at = slice(tile * wide, (tile + 1) * wide)
+            force_ref[axis : axis + 1, at] = comps[axis][tile : tile + 1]
+            torque_ref[axis : axis + 1, at] = torque[tile : tile + 1]
+
+
+def pair_kernel(members, slots, *refs):
     piece_count = members // 2
     pieces = refs[:piece_count]
-    (rim_ref, off_ref, inner_ref, edge_ref, table, word_ref, words, gathered,
-     parts, reach_ref, sums_ref, folded_ref, acc_near, acc_far, sem) = refs[piece_count:]
-    along_z, along_y = place_ref[0], place_ref[1]
-    own_rows = pieces[0].shape[1] - head_row
-    inner_blocks = members * own_rows * 4
-    slot_rows = head_row // 2
+    (inside_ref, across_ref, off_ref, inner_ref, edge_in_ref, edge_over_ref, table, list_ref, word_ref,
+     words, gathered, parts, reach_ref, sums_ref, folded_ref, acc_near, acc_far, sem) = refs[piece_count:]
+    me = lax.axis_index("dev")
+    along_z, along_y = me // 2, lax.rem(me, 2)
+    even = lax.rem(lax.axis_index("grp"), 2) == 0
+    own_blocks = pieces[0].shape[2]
+    inner_blocks = members * own_blocks
+    slot_rows = slots // LANES
+    lists = slots // own_blocks
 
     owners = []
+    counts = []
     for k in range(piece_count):
         for side in range(2):
             owners.append(
                 lax.rem(along_z - k + piece_count, piece_count) * 2
                 + (along_y if side == 0 else 1 - along_y)
             )
-    before = [jnp.int32(0)]
-    for member in range(members):
-        before.append(before[-1] + place_ref[2 + member])
-    total = before[-1]
-    me = along_z * 2 + along_y
+            base = (2 * k + side) * 2 * slot_rows
+            for part in range(2 * slot_rows):
+                line, spot = part // (own_blocks // LANES), part % (own_blocks // LANES)
+                list_ref[pl.ds(base + part, 1), :] = pieces[k][
+                    side, pl.ds(2 * PARAMS + line, 1), spot * LANES : (spot + 1) * LANES
+                ]
+            found = jnp.where(list_ref[pl.ds(base, slot_rows), :] >= 0.0, 1.0, 0.0)
+            counts.append(jnp.sum(found).astype(jnp.int32))
+    starts = []
+    total = jnp.int32(0)
+    for index in range(members):
+        start = jnp.int32(0)
+        for other in range(members):
+            if other != index:
+                start = start + jnp.where(owners[other] < owners[index], counts[other], 0)
+        starts.append(start)
+        total = total + counts[index]
     begin = (total * me) // members
     finish = (total * (me + 1)) // members
     number = finish - begin
@@ -66,53 +164,36 @@
     flat = flat + column
     near_list = jnp.zeros((slot_rows, LANES), jnp.float32)
     far_list = jnp.zeros((slot_rows, LANES), jnp.float32)
-    for k in range(piece_count):
-        for side in range(2):
-            member = owners[2 * k + side]
-            start = jnp.int32(0)
-            for other in range(members):
-                start = start + jnp.where(other < member, place_ref[2 + other], 0)
-            low = jnp.maximum(start, begin) - begin
-            high = jnp.minimum(start + place_ref[2 + member], finish) - begin
-            shift = jnp.bitwise_and(start - begin, slots - 1)
-            wanted = (flat >= low) & (flat < high)
-
-            def moved(rows):
-                turned = pltpu.roll(rows, shift & (LANES - 1), axis=1)
-                same = pltpu.roll(turned, shift >> 7, axis=0)
-                following = pltpu.roll(turned, (shift >> 7) + 1, axis=0)
-                return jnp.where(column < (shift & (LANES - 1)), following, same)
-
-            near_list = jnp.where(wanted, moved(pieces[k][side, pl.ds(0, slot_rows), :]), near_list)
-            far_list = jnp.where(
-                wanted, moved(pieces[k][side, pl.ds(slot_rows, slot_rows), :]), far_list
-            )
+    for index in range(members):
+        start = starts[index]
+        low = jnp.maximum(start, begin) - begin
+        high = jnp.minimum(start + counts[index], finish) - begin
+        shift = jnp.bitwise_and(start - begin, slots - 1)
+        wanted = (flat >= low) & (flat < high)
+
+        def moved(rows, shift=shift):
+            turned = pltpu.roll(rows, shift & (LANES - 1), axis=1)
+            same = pltpu.roll(turned, shift >> 7, axis=0)
+            following = pltpu.roll(turned, (shift >> 7) + 1, axis=0)
+            return jnp.where(column < (shift & (LANES - 1)), following, same)
+
+        base = index * 2 * slot_rows
+        near_list = jnp.where(wanted, moved(list_ref[pl.ds(base, slot_rows), :]), near_list)
+        far_list = jnp.where(wanted, moved(list_ref[pl.ds(base + slot_rows, slot_rows), :]), far_list)
     word_ref[pl.ds(0, slot_rows), :] = near_list.astype(jnp.int32)
     word_ref[pl.ds(slot_rows, slot_rows), :] = far_list.astype(jnp.int32)
     copy = pltpu.make_async_copy(word_ref, words, sem)
     copy.start()
 
-    def unpack(source, row, first):
-        rows = source[pl.ds(row, 32), :]
-        for sub in range(4):
-            shifted = rows if sub == 0 else pltpu.roll(rows, LANES - 32 * sub, axis=1)
-            table[pl.ds(pl.multiple_of(first + sub * 32, 32), 32), :] = shifted
-
     for k in range(piece_count):
         for side in range(2):
-            base = owners[2 * k + side] * (own_rows * 4)
-
-            def take(part, carry, k=k, side=side, base=base):
-                unpack(
-                    pieces[k].at[side],
-                    pl.multiple_of(head_row + part * 32, 8),
-                    base + part * LANES,
-                )
-                return carry
-
-            lax.fori_loop(0, own_rows // 32, take, 0)
-    for end in range(2):
-        unpack(rim_ref, end * 32, inner_blocks + end * LANES)
+            base = pl.multiple_of(owners[2 * k + side] * own_blocks, LANES)
+            for tile in range(own_blocks // LANES):
+                at = slice(tile * LANES, (tile + 1) * LANES)
+                table[pl.ds(base + tile * LANES, LANES), 0:ROWS] = pieces[k][side, :, at].T
+    below = jnp.where(even, 0, LANES)
+    table[pl.ds(pl.multiple_of(inner_blocks + below, LANES), LANES), 0:ROWS] = across_ref[...].T
+    table[pl.ds(pl.multiple_of(inner_blocks + LANES - below, LANES), LANES), 0:ROWS] = inside_ref[...].T
 
     def clear(turn, carry):
         acc_near[pl.ds(pl.multiple_of(turn * 48, 8), 48), :] = jnp.zeros((48, LANES), jnp.float32)
@@ -124,7 +205,7 @@
     copy.wait()
 
     lane = lax.broadcasted_iota(jnp.int32, (2 * CHUNK, LANES), 1)
-    column_of = jnp.where(lane < LANES // 2, 0, 16)
+    column_of = jnp.where(lane < LANES // 2, 0, PARAMS)
     lane_f = (lane & 7).astype(jnp.float32)
     pick_low = lane < 8
     pick_all = lane < 16
@@ -169,15 +250,19 @@
             )
 
         kind_low = jnp.take_along_axis(
-            packed, jnp.where(pick_low, 12, 28), axis=1, mode="promise_in_bounds"
+            packed, jnp.where(pick_low, 9, PARAMS + 9), axis=1, mode="promise_in_bounds"
         )
         pick = jnp.where(pick_all & (kind_low == lane_f), 1.0, 0.0).astype(jnp.bfloat16)
         offsets = jnp.dot(pick, off_ref[...], preferred_element_type=jnp.float32)
+        turns = [spread(3 + entry) for entry in range(6)]
+        for mode in range(3):
+            after, last = (mode + 1) % 3, (mode + 2) % 3
+            turns.append(turns[after] * turns[3 + last] - turns[last] * turns[3 + after])
         where_at = []
         for axis in range(3):
             value = spread(axis)
             for mode in range(3):
-                value = value + spread(3 + 3 * axis + mode) * offsets[:, mode * LANES : (mode + 1) * LANES]
+                value = value + turns[3 * axis + mode] * offsets[:, mode * LANES : (mode + 1) * LANES]
             where_at.append(value)
         near = [value[:CHUNK] for value in where_at]
         far = [value[CHUNK:] for value in where_at]
@@ -337,25 +422,26 @@
         )
         return (other - mine) * STIFFNESS
 
-    for tiles, start, out in ((inner_blocks // LANES, 0, inner_ref), (2, inner_blocks // LANES, edge_ref)):
-        for half in range(2):
-            rows = [total_of(row, half, tiles, start) for row in range(9)]
-            results = rows[0:3] + [rows[6 + (axis + 2) % 3] - rows[3 + (axis + 1) % 3] for axis in range(3)]
-            for axis in range(6):
-                out[pl.ds(6 * half + axis, tiles, stride=COMPS), :] = results[axis]
-
-
-def neighbour_swap(rows_low, rows_high, axis):
-    count = lax.axis_size(axis)
-    index = lax.axis_index(axis)
-    even = index % 2 == 0
+    def results_of(half, tiles, start):
+        rows = [total_of(row, half, tiles, start) for row in range(9)]
+        return rows[0:3] + [
+            rows[6 + (axis + 2) % 3] - rows[3 + (axis + 1) % 3] for axis in range(3)
+        ]
+
+    inner_tiles = inner_blocks // LANES
+    for half in range(2):
+        for axis, value in enumerate(results_of(half, inner_tiles, 0)):
+            inner_ref[pl.ds(6 * half + axis, inner_tiles, stride=COMPS), :] = value
+        for axis, value in enumerate(results_of(half, 2, inner_tiles)):
+            at = pl.ds(6 * half + axis, 1)
+            edge_in_ref[at, :] = jnp.where(even, value[1:2], value[0:1])
+            edge_over_ref[at, :] = jnp.where(even, value[0:1], value[1:2])
+
+
+def swaps(count):
     inside = [(i, i ^ 1) for i in range(count)]
     across = [(i, (i + 1) % count if i % 2 else (i - 1) % count) for i in range(count)]
-    got_across = lax.ppermute(jnp.where(even, rows_low, rows_high), axis, across)
-    got_inside = lax.ppermute(jnp.where(even, rows_high, rows_low), axis, inside)
-    from_below = jnp.where(even, got_across, got_inside)
-    from_above = jnp.where(even, got_inside, got_across)
-    return from_below, from_above
+    return inside, across
 
 
 def shards(positions, rotations, clump_kind, sub_offsets, pair_blocks, pair_count):
@@ -369,33 +455,18 @@
     slots = pair_blocks.shape[1]
     own_blocks = clumps // 2
     kinds, _, subs = sub_offsets.shape
-    head_row = 2 * slots // LANES
-
-    values = jnp.concatenate(
-        [
-            positions,
-            rotations,
-            clump_kind.astype(jnp.float32)[None],
-            jnp.zeros((3, clumps), jnp.float32),
-        ],
-        0,
-    )
-    values = values.T.reshape(own_blocks, 32)
-    lane = lax.broadcasted_iota(jnp.int32, values.shape, 1)
-    values = jnp.where(lane == 15, pair_count[0].astype(jnp.float32), values)
-    packed = (
-        values.reshape(own_blocks // LANES, 4, 32, 32)
-        .transpose(0, 2, 1, 3)
-        .reshape(own_blocks // 4, LANES)
-    )
-    inner_blocks = own_blocks * members
-    blocks = pair_blocks - group * inner_blocks
-    blocks = jnp.where(
-        blocks < 0,
-        blocks + inner_blocks + RIM,
-        jnp.where(blocks >= inner_blocks, blocks + RIM, blocks),
-    )
-    payload = jnp.concatenate([blocks.astype(jnp.float32).reshape(head_row, LANES), packed], 0)
+    even = group % 2 == 0
+    inside, across = swaps(groups)
+    vmem = pl.BlockSpec(memory_space=pltpu.VMEM)
+    smem = pl.BlockSpec(memory_space=pltpu.SMEM)
+
+    payload = pl.pallas_call(
+        functools.partial(payload_kernel, slots, members),
+        out_shape=jax.ShapeDtypeStruct((ROWS, own_blocks), jnp.float32),
+        in_specs=[vmem] * 4 + [smem],
+        out_specs=vmem,
+        name="payload_kernel",
+    )(positions, rotations, clump_kind.reshape(-1, LANES), pair_blocks, pair_count)
 
     pair_y = [(i, i ^ 1) for i in range(members)]
     both = jnp.stack([payload, lax.ppermute(payload, "dev", pair_y)])
@@ -405,21 +476,20 @@
             lax.ppermute(both, "dev", [(i, (i + 2 * k) % members) for i in range(members)])
         )
 
-    def piece_rows(member, start, count):
+    def piece_columns(member, start):
         z, y = member // 2, member % 2
         found = None
         for k in range(rings):
-            rows = lax.dynamic_slice_in_dim(pieces[k], start, count, 1)
-            side = jnp.where(along_y == y, rows[0], rows[1])
+            part = pieces[k][:, :, start : start + RIM]
+            part = jnp.where(along_y == y, part[0], part[1])
             hit = (along_z - k + rings) % rings == z
-            found = side if found is None else jnp.where(hit, side, found)
+            found = part if found is None else jnp.where(hit, part, found)
         return found
 
-    rim_rows = RIM // 4
-    first_rows = piece_rows(0, head_row, rim_rows)
-    last_rows = piece_rows(members - 1, head_row + packed.shape[0] - rim_rows, rim_rows)
-    from_below, from_above = neighbour_swap(first_rows, last_rows, "grp")
-    rims = jnp.concatenate([from_below, from_above], 0)
+    first = piece_columns(0, 0)
+    last = piece_columns(members - 1, own_blocks - RIM)
+    got_across = lax.ppermute(jnp.where(even, first, last), "grp", across)
+    got_inside = lax.ppermute(jnp.where(even, last, first), "grp", inside)
 
     offset_table = sub_offsets.astype(jnp.float32) * OFFSET_UNIT
     blank = jnp.zeros_like(offset_table)
@@ -434,30 +504,22 @@
         [offset_rows, jnp.zeros((LANES - 2 * kinds, offset_rows.shape[1]), jnp.float32)], 0
     ).astype(jnp.bfloat16)
 
-    counts = jnp.zeros((members,), jnp.float32)
-    for k in range(rings):
-        for side in range(2):
-            member = (along_z - k + rings) % rings * 2 + (along_y if side == 0 else 1 - along_y)
-            counts = counts + jnp.where(
-                jnp.arange(members) == member, pieces[k][side, head_row, 15], 0.0
-            )
-    place = jnp.concatenate(
-        [jnp.stack([along_z, along_y]).astype(jnp.int32), counts.astype(jnp.int32)]
-    )
+    inner_blocks = own_blocks * members
     tiles = inner_blocks // LANES
-    vmem = pl.BlockSpec(memory_space=pltpu.VMEM)
-    inner, edge = pl.pallas_call(
-        functools.partial(pair_kernel, members, slots, head_row),
+    inner, edge_in, edge_over = pl.pallas_call(
+        functools.partial(pair_kernel, members, slots),
         out_shape=(
             jax.ShapeDtypeStruct((tiles * COMPS, LANES), jnp.float32),
-            jax.ShapeDtypeStruct((2 * COMPS, LANES), jnp.float32),
+            jax.ShapeDtypeStruct((COMPS, LANES), jnp.float32),
+            jax.ShapeDtypeStruct((COMPS, LANES), jnp.float32),
         ),
-        in_specs=[pl.BlockSpec(memory_space=pltpu.SMEM)] + [vmem] * (rings + 2),
-        out_specs=(vmem, vmem),
+        in_specs=[vmem] * (rings + 3),
+        out_specs=(vmem, vmem, vmem),
         scratch_shapes=[
             pltpu.VMEM((inner_blocks + 2 * RIM, LANES), jnp.float32),
-            pltpu.VMEM((head_row, LANES), jnp.int32),
-            pltpu.SMEM((head_row, LANES), jnp.int32),
+            pltpu.VMEM((members * 2 * slots // LANES, LANES), jnp.float32),
+            pltpu.VMEM((2 * slots // LANES, LANES), jnp.int32),
+            pltpu.SMEM((2 * slots // LANES, LANES), jnp.int32),
             pltpu.VMEM((2 * CHUNK, LANES), jnp.float32),
             pltpu.VMEM((27 * slots, LANES), jnp.float32),
             pltpu.VMEM((8 * LANES, 2 * LANES), jnp.float32),
@@ -468,11 +530,12 @@
             pltpu.SemaphoreType.DMA,
         ],
         name="pair_kernel",
-    )(place, *pieces, rims, offset_rows)
-
-    below, above = neighbour_swap(edge[:COMPS], edge[COMPS:], "grp")
-    below = jnp.where(group > 0, below, 0.0)
-    above = jnp.where(group < groups - 1, above, 0.0)
+    )(*pieces, got_inside, got_across, offset_rows)
+
+    got_over = lax.ppermute(edge_over, "grp", across)
+    got_in = lax.ppermute(edge_in, "grp", inside)
+    below = jnp.where(group > 0, jnp.where(even, got_over, got_in), 0.0)
+    above = jnp.where(group < groups - 1, jnp.where(even, got_in, got_over), 0.0)
     inner = inner + jnp.concatenate(
         [below, jnp.zeros(((tiles - 2) * COMPS, LANES), jnp.float32), above], 0
     )
@@ -482,15 +545,20 @@
     mine = lax.dynamic_index_in_dim(ranks, along_y, 1, False)
     other = lax.dynamic_index_in_dim(ranks, 1 - along_y, 1, False)
     column = mine + lax.ppermute(other, "dev", pair_y)
-    summed = lax.dynamic_index_in_dim(column, along_z, 0, False)
+    shares = [lax.dynamic_index_in_dim(column, along_z, 0, False)]
     for k in range(1, rings):
         part = lax.dynamic_index_in_dim(column, (along_z + k) % rings, 0, False)
-        summed = summed + lax.ppermute(
-            part, "dev", [(i, (i + 2 * k) % members) for i in range(members)]
-        )
-    summed = summed.reshape(own_blocks // LANES, 2, 6, LANES).transpose(2, 0, 3, 1).reshape(6, clumps)
-    clump_force = summed[0:3]
-    clump_torque = summed[3:6] - cross_axis(positions, clump_force)
+        shares.append(
+            lax.ppermute(part, "dev", [(i, (i + 2 * k) % members) for i in range(members)])
+        )
+    clump_force, clump_torque = pl.pallas_call(
+        finish_kernel,
+        out_shape=(jax.ShapeDtypeStruct((3, clumps), jnp.float32),) * 2,
+        in_specs=[vmem] * (rings + 1),
+        out_specs=(vmem, vmem),
+        scratch_shapes=[pltpu.VMEM((own_rows, LANES), jnp.float32)],
+        name="finish_kernel",
+    )(*shares, positions)
     return (clump_force, clump_torque)
 
 

time: 84.5 us -> 69.4 us (0.82)
  other arithmetic: 11 us -> 1.83 us
  local copies, waits for them, and re-layouts: 7.98 us -> 2.09 us
  Pallas kernels: 22.8 us -> 26.9 us
  starting transfers between devices: 21.7 us -> 18.9 us
    convert_element_type x3 -> x0, other arithmetic: 5.67 us -> none  [the longest x1 4.97 us: shards(): counts.astype(jnp.int32)]
    slice x14 -> x0, local copies, waits for them, and re-layouts: 5.65 us -> none  [the longest x5 3.1 us: shards(): pieces[k][side, head_row, 15]]
    pallas_call x1 -> x3, Pallas kernels: 22.8 us -> 26.9 us  [the longest x1 23.7 us: shards(): pl.pallas_call(functools.partial(pair_kernel, members, slots), out_shape=...]
    ppermute x3, waiting for transfers between devices: 5.87 us -> 4.26 us  [shards(): lax.ppermute(both, 'dev', [(i, (i + 2 * k) % members) for i in range(memb...]
    ppermute x4, starting transfers between devices: 4.92 us -> 3.42 us  [the longest x1 1.7 us: shards(): got_across = lax.ppermute(jnp.where(even, first, last), 'grp', across)]
    ppermute x3, starting transfers between devices: 6.05 us -> 4.66 us  [shards(): lax.ppermute(part, 'dev', [(i, (i + 2 * k) % members) for i in range(memb...]
    concatenate x2 -> x0, other arithmetic: 1.2 us -> none  [the longest x1 0.61 us: shards(): rims = jnp.concatenate([from_below, from_above], 0)]
    ppermute x4, waiting for transfers between devices: 1.29 us -> 2.37 us  [the longest x1 1.62 us: shards(): got_over = lax.ppermute(edge_over, 'grp', across)]
  transfers between devices with their start and end apart: 12 -> 12, of which waited for: 7 -> 9; matrix products, arithmetic and copies ran while one was open for 12% -> 1% of each run, Pallas kernels for 0% -> 0%
where the time goes in v1:
time: 69.4 us; the launch traced here: 69 us
  Pallas kernels  26.9 us (39%)
  starting transfers between devices  18.9 us (27%)
  waiting for transfers between devices  17.9 us (26%)
  local copies, waits for them, and re-layouts  2.09 us (3%)
  other arithmetic  1.83 us (3%)
  between operations  1.47 us (2%)
    pallas_call x1, Pallas kernels, shards(): pl.pallas_call(functools.partial(pair_kernel, members, slots), out_shape=...  23.7 us
    ppermute x3, starting transfers between devices, shards(): lax.ppermute(both, 'dev', [(i, (i + 2 * k) % members) for i in range(memb...  6.07 us
    ppermute x3, waiting for transfers between devices, shards(): lax.ppermute(part, 'dev', [(i, (i + 2 * k) % members) for i in range(memb...  5.62 us
    ppermute x3, starting transfers between devices, shards(): lax.ppermute(part, 'dev', [(i, (i + 2 * k) % members) for i in range(memb...  4.66 us
    ppermute x3, waiting for transfers between devices, shards(): lax.ppermute(both, 'dev', [(i, (i + 2 * k) % members) for i in range(memb...  4.26 us
    ppermute x1, waiting for transfers between devices, shards(): column = mine + lax.ppermute(other, 'dev', pair_y)  3.51 us
    ppermute x1, starting transfers between devices, shards(): both = jnp.stack([payload, lax.ppermute(payload, 'dev', pair_y)])  3 us
    ppermute x1, waiting for transfers between devices, shards(): both = jnp.stack([payload, lax.ppermute(payload, 'dev', pair_y)])  2.11 us
  transfers between devices with their start and end apart: 12, of which 9 were waited for; matrix products, arithmetic and copies ran while one was open for 1% of the time, Pallas kernels for 0%

profile of v1, /device:TPU:0, one launch (start us, length us, event | category | flops | bytes accessed | tf_op | source)
XLA Modules:
  0.0 69.0 jit_solution(4005291466492831556)
XLA Ops:
  1.3 0.0 copy-start.8
  1.3 1.7 %payload_kernel.1 = f32[24,512]{1,0:T(8,128)} custom-call(f32[3,1024]{1,0:T(4,128)} %refs_3_.1, f32[9,1024]{1,0:T(8,128)} %rotation_ref.1, s32[8,128]{1,0:T(8,128)} %bitcast.30, s32[2,1024]{1,0:T(2,128)} %pair_ref.1, s32[1]{0:T(128)S(6)} %copy.8.count_ref), custom_call_target="tpu_custom_call" | custom-call | tf_op jit(solution)/shard_map/payload_kernel/pallas_call | solution.py:463
  2.9 3.0 %collective-permute-start = (f32[24,512]{1,0:T(8,128)}, f32[24,512]{1,0:T(8,128)S(1)}, u32[]{:S(2)}, u32[]{:S(2)}) collective-permute-start(f32[24,512]{1,0:T(8,128)} %payload_kernel.1), channel_id=1, source_target_pairs={{0,1},{1,0},{2,3},{3,2},{4,5},{5,4},{6,7},{7,6},{8,9},{9,8},{10,11... | collective-permute-start | bytes 147464 | tf_op jit(solution)/shard_map/ppermute | solution.py:472
  5.9 0.0 copy-done.8
  5.9 0.0 copy-start.1
  6.0 0.1 pad.9.clone
  6.1 2.1 %collective-permute-done = f32[24,512]{1,0:T(8,128)S(1)} collective-permute-done((f32[24,512]{1,0:T(8,128)}, f32[24,512]{1,0:T(8,128)S(1)}, u32[]{:S(2)}, u32[]{:S(2)}) %collective-permute-start) | collective-permute-done | bytes 49184 | tf_op jit(solution)/shard_map/ppermute | solution.py:472
  8.2 0.0 copy-done.1
  8.2 0.0 copy-start
  8.2 2.1 %collective-permute-start.1 = (f32[2,24,512]{2,1,0:T(8,128)S(1)}, f32[2,24,512]{2,1,0:T(8,128)S(1)}, u32[]{:S(2)}, u32[]{:S(2)}) collective-permute-start(f32[2,24,512]{2,1,0:T(8,128)S(1)} %pad_maximum_fusion.refs_0_), channel_id=1, source_target_pairs={{0,2},{1,3},{2,4},{3,5},{4,6},{5,7},{6,0},{7,1},{8,10},{9,11},{10,... | collective-permute-start | bytes 294920 | tf_op jit(solution)/shard_map/ppermute | solution.py:476
  10.4 2.6 %collective-permute-start.2 = (f32[2,24,512]{2,1,0:T(8,128)S(1)}, f32[2,24,512]{2,1,0:T(8,128)S(1)}, u32[]{:S(2)}, u32[]{:S(2)}) collective-permute-start(f32[2,24,512]{2,1,0:T(8,128)S(1)} %pad_maximum_fusion.refs_0_), channel_id=1, source_target_pairs={{0,4},{1,5},{2,6},{3,7},{4,0},{5,1},{6,2},{7,3},{8,12},{9,13},{10,... | collective-permute-start | bytes 294920 | tf_op jit(solution)/shard_map/ppermute | solution.py:476
  13.0 1.3 %collective-permute-start.3 = (f32[2,24,512]{2,1,0:T(8,128)S(1)}, f32[2,24,512]{2,1,0:T(8,128)S(1)}, u32[]{:S(2)}, u32[]{:S(2)}) collective-permute-start(f32[2,24,512]{2,1,0:T(8,128)S(1)} %pad_maximum_fusion.refs_0_), channel_id=1, source_target_pairs={{0,6},{1,7},{2,0},{3,1},{4,2},{5,3},{6,4},{7,5},{8,14},{9,15},{10,... | collective-permute-start | bytes 294920 | tf_op jit(solution)/shard_map/ppermute | solution.py:476
  14.3 0.1 pad_bitcast_fusion.1
  14.4 1.7 %collective-permute-done.1.refs_1_ = f32[2,24,512]{2,1,0:T(8,128)S(1)} collective-permute-done((f32[2,24,512]{2,1,0:T(8,128)S(1)}, f32[2,24,512]{2,1,0:T(8,128)S(1)}, u32[]{:S(2)}, u32[]{:S(2)}) %collective-permute-start.1) | collective-permute-done | bytes 98336 | tf_op jit(solution)/shard_map/ppermute | solution.py:476
  16.1 0.0 copy-start.2
  16.1 2.5 %collective-permute-done.2.refs_2_ = f32[2,24,512]{2,1,0:T(8,128)S(1)} collective-permute-done((f32[2,24,512]{2,1,0:T(8,128)S(1)}, f32[2,24,512]{2,1,0:T(8,128)S(1)}, u32[]{:S(2)}, u32[]{:S(2)}) %collective-permute-start.2) | collective-permute-done | bytes 98336 | tf_op jit(solution)/shard_map/ppermute | solution.py:476
  18.6 0.0 copy-start.3
  18.6 0.0 collective-permute-done.3.refs_3_
  18.6 0.0 copy-start.4
  18.7 0.0 copy-done
  18.7 0.0 copy-done.2
  18.7 0.1 collective-permute-start.4
  18.8 1.7 %collective-permute-start.5 = (f32[24,128]{1,0:T(8,128)S(1)}, f32[24,128]{1,0:T(8,128)S(1)}, u32[]{:S(2)}, u32[]{:S(2)}) collective-permute-start(f32[24,128]{1,0:T(8,128)S(1)} %get-tuple-element.8), channel_id=1, source_target_pairs={{0,24},{8,16},{16,8},{24,0},{1,25},{9,17},{17,9},{25,1},{2,26},{10... | collective-permute-start | bytes 36872 | tf_op jit(solution)/shard_map/ppermute | solution.py:491
  20.5 0.7 %maximum_maximum_fusion.refs_6_ = bf16[128,384]{1,0:T(8,128)(2,1)} fusion(bf16[8,384]{1,0:T(8,128)(2,1)S(1)} %get-tuple-element.18, bf16[8,384]{1,0:T(8,128)(2,1)S(1)} %get-tuple-element.17, bf16[128]{0:T(256)(128)(2,1)S(1)} %pad.9.clone), kind=kLoop, calls=%fused_computation.2 | loop fusion | flops 294912 | bytes 110848 | tf_op jit(solution)/shard_map/concatenate | solution.py:503
  21.2 0.0 collective-permute-done.4.refs_4_
  21.2 0.0 copy-start.9
  21.2 0.7 %collective-permute-done.5.refs_5_ = f32[24,128]{1,0:T(8,128)S(1)} collective-permute-done((f32[24,128]{1,0:T(8,128)S(1)}, f32[24,128]{1,0:T(8,128)S(1)}, u32[]{:S(2)}, u32[]{:S(2)}) %collective-permute-start.5) | collective-permute-done | bytes 12320 | tf_op jit(solution)/shard_map/ppermute | solution.py:491
  22.0 0.0 copy-done.3
  22.0 0.0 copy-done.4
  22.0 0.0 copy-done.9
  22.0 0.0 copy-start.10
  22.0 0.6 copy-done.10
  22.6 23.7 %pair_kernel.1 = (f32[384,128]{1,0:T(8,128)}, f32[12,128]{1,0:T(8,128)}, f32[12,128]{1,0:T(8,128)}) custom-call(f32[2,24,512]{2,1,0:T(8,128)} %copy-done, f32[2,24,512]{2,1,0:T(8,128)} %copy-done.2, f32[2,24,512]{2,1,0:T(8,128)} %copy-done.3, f32[2,24,512]{2,1,0:T(8,128)} %copy-done.4, f32[24,128]{1,0:T(8,128)} %copy-done.9, f32[24,128]{1,0:T(8,128)} %copy-done.10, ...), custom_call_target="tpu_custom_call" | custom-call | tf_op jit(solution)/shard_map/pair_kernel/pallas_call | solution.py:509
  46.3 1.6 %collective-permute-start.6 = (f32[12,128]{1,0:T(8,128)}, f32[12,128]{1,0:T(8,128)S(1)}, u32[]{:S(2)}, u32[]{:S(2)}) collective-permute-start(f32[12,128]{1,0:T(8,128)} %get-tuple-element.6), channel_id=1, source_target_pairs={{0,24},{8,16},{16,8},{24,0},{1,25},{9,17},{17,9},{25,1},{2,26},{10... | collective-permute-start | bytes 18440 | tf_op jit(solution)/shard_map/ppermute | solution.py:535
  47.9 0.0 collective-permute-start.7
  47.9 0.1 pad.5.clone
  48.0 1.6 %collective-permute-done.6 = f32[12,128]{1,0:T(8,128)S(1)} collective-permute-done((f32[12,128]{1,0:T(8,128)}, f32[12,128]{1,0:T(8,128)S(1)}, u32[]{:S(2)}, u32[]{:S(2)}) %collective-permute-start.6) | collective-permute-done | bytes 6176 | tf_op jit(solution)/shard_map/ppermute | solution.py:535
  49.6 0.0 collective-permute-done.7
  49.6 1.0 %maximum_add_fusion = f32[384,128]{1,0:T(8,128)S(1)} fusion(f32[384,128]{1,0:T(8,128)} %get-tuple-element.5, f32[12,128]{1,0:T(8,128)S(1)} %get-tuple-element.16, f32[12,128]{1,0:T(8,128)S(1)} %get-tuple-element.15, f32[384]{0:T(512)S(1)} %pad.5.clone), kind=kLoop, calls=%fused_computation | loop fusion | flops 147456 | bytes 407040 | tf_op jit(solution)/shard_map/add | solution.py:539
  50.7 1.7 %collective-permute-start.8 = (f32[4,48,128]{2,1,0:T(8,128)S(1)}, f32[4,48,128]{2,1,0:T(8,128)S(1)}, u32[]{:S(2)}, u32[]{:S(2)}) collective-permute-start(f32[4,48,128]{2,1,0:T(8,128)S(1)} %dynamic-slice_bitcast_fusion), channel_id=1, source_target_pairs={{0,1},{1,0},{2,3},{3,2},{4,5},{5,4},{6,7},{7,6},{8,9},{9,8},{10,11... | collective-permute-start | bytes 294920 | tf_op jit(solution)/shard_map/ppermute | solution.py:547
  52.4 3.5 %collective-permute-done.8 = f32[4,48,128]{2,1,0:T(8,128)S(1)} collective-permute-done((f32[4,48,128]{2,1,0:T(8,128)S(1)}, f32[4,48,128]{2,1,0:T(8,128)S(1)}, u32[]{:S(2)}, u32[]{:S(2)}) %collective-permute-start.8) | collective-permute-done | bytes 98336 | tf_op jit(solution)/shard_map/ppermute | solution.py:547
  55.9 0.6 dynamic-slice_bitcast_fusion.1
  56.6 1.3 %collective-permute-start.10 = (f32[48,128]{1,0:T(8,128)S(1)}, f32[48,128]{1,0:T(8,128)S(1)}, u32[]{:S(2)}, u32[]{:S(2)}) collective-permute-start(f32[48,128]{1,0:T(8,128)S(1)} %get-tuple-element.12), channel_id=1, source_target_pairs={{0,4},{1,5},{2,6},{3,7},{4,0},{5,1},{6,2},{7,3},{8,12},{9,13},{10,... | collective-permute-start | bytes 73736 | tf_op jit(solution)/shard_map/ppermute | solution.py:552
  57.9 3.4 %collective-permute-start.11 = (f32[48,128]{1,0:T(8,128)S(1)}, f32[48,128]{1,0:T(8,128)S(1)}, u32[]{:S(2)}, u32[]{:S(2)}) collective-permute-start(f32[48,128]{1,0:T(8,128)S(1)} %get-tuple-element.11), channel_id=1, source_target_pairs={{0,6},{1,7},{2,0},{3,1},{4,2},{5,3},{6,4},{7,5},{8,14},{9,15},{10,... | collective-permute-start | bytes 73736 | tf_op jit(solution)/shard_map/ppermute | solution.py:552
  61.2 0.0 collective-permute-start.9
  61.2 0.1 collective-permute-done.10.refs_1_
  61.3 0.0 copy-start.5
  61.3 1.5 %collective-permute-done.11.refs_2_ = f32[48,128]{1,0:T(8,128)S(1)} collective-permute-done((f32[48,128]{1,0:T(8,128)S(1)}, f32[48,128]{1,0:T(8,128)S(1)}, u32[]{:S(2)}, u32[]{:S(2)}) %collective-permute-start.11) | collective-permute-done | bytes 24608 | tf_op jit(solution)/shard_map/ppermute | solution.py:552
  62.7 0.0 copy-start.6
  62.7 4.1 %collective-permute-done.9.refs_0_ = f32[48,128]{1,0:T(8,128)S(1)} collective-permute-done((f32[48,128]{1,0:T(8,128)S(1)}, f32[48,128]{1,0:T(8,128)S(1)}, u32[]{:S(2)}, u32[]{:S(2)}) %collective-permute-start.9) | collective-permute-done | bytes 24608 | tf_op jit(solution)/shard_map/ppermute | solution.py:552
  66.8 0.0 copy-start.7
  66.8 0.0 copy-done.5
  66.8 0.0 copy-done.6
  66.8 0.6 copy-done.7
  67.4 1.6 %finish_kernel.1 = (f32[3,1024]{1,0:T(4,128)}, f32[3,1024]{1,0:T(4,128)}) custom-call(f32[48,128]{1,0:T(8,128)} %get-tuple-element.14.own_ref, f32[48,128]{1,0:T(8,128)} %copy-done.7, f32[48,128]{1,0:T(8,128)} %copy-done.5, f32[48,128]{1,0:T(8,128)} %copy-done.6, f32[3,1024]{1,0:T(4,128)} %refs_3_.1), custom_call_target="tpu_custom_call" | custom-call | tf_op jit(solution)/shard_map/finish_kernel/pallas_call | solution.py:554
  (9 shorter events, 0.1 us)
Async XLA Ops:
  1.3 4.7 %copy-start.8 = (s32[8,3,64]{2,0,1:T(8,128)S(1)}, s32[8,3,64]{2,0,1:T(8,128)}, u32[]{:S(2)}) copy-start(s32[8,3,64]{2,0,1:T(8,128)} %param.9) | copy-start | bytes 18436
  2.9 5.3 %collective-permute-start = (f32[24,512]{1,0:T(8,128)}, f32[24,512]{1,0:T(8,128)S(1)}, u32[]{:S(2)}, u32[]{:S(2)}) collective-permute-start(f32[24,512]{1,0:T(8,128)} %payload_kernel.1), channel_id=1, source_target_pairs={{0,1},{1,0},{2,3},{3,2},{4,5},{5,4},{6,7},{7,6},{8,9},{9,8},{10,11... | collective-permute-start | bytes 147464 | tf_op jit(solution)/shard_map/ppermute | solution.py:472
  5.9 2.3 %copy-start.1 = (f32[24,512]{1,0:T(8,128)S(1)}, f32[24,512]{1,0:T(8,128)}, u32[]{:S(2)}) copy-start(f32[24,512]{1,0:T(8,128)} %payload_kernel.1) | copy-start | bytes 147460
  8.2 10.4 %copy-start = (f32[2,24,512]{2,1,0:T(8,128)}, f32[2,24,512]{2,1,0:T(8,128)S(1)}, u32[]{:S(2)}) copy-start(f32[2,24,512]{2,1,0:T(8,128)S(1)} %pad_maximum_fusion.refs_0_) | copy-start | bytes 294916
  8.2 7.9 %collective-permute-start.1 = (f32[2,24,512]{2,1,0:T(8,128)S(1)}, f32[2,24,512]{2,1,0:T(8,128)S(1)}, u32[]{:S(2)}, u32[]{:S(2)}) collective-permute-start(f32[2,24,512]{2,1,0:T(8,128)S(1)} %pad_maximum_fusion.refs_0_), channel_id=1, source_target_pairs={{0,2},{1,3},{2,4},{3,5},{4,6},{5,7},{6,0},{7,1},{8,10},{9,11},{10,... | collective-permute-start | bytes 294920 | tf_op jit(solution)/shard_map/ppermute | solution.py:476
  10.4 8.3 %collective-permute-start.2 = (f32[2,24,512]{2,1,0:T(8,128)S(1)}, f32[2,24,512]{2,1,0:T(8,128)S(1)}, u32[]{:S(2)}, u32[]{:S(2)}) collective-permute-start(f32[2,24,512]{2,1,0:T(8,128)S(1)} %pad_maximum_fusion.refs_0_), channel_id=1, source_target_pairs={{0,4},{1,5},{2,6},{3,7},{4,0},{5,1},{6,2},{7,3},{8,12},{9,13},{10,... | collective-permute-start | bytes 294920 | tf_op jit(solution)/shard_map/ppermute | solution.py:476
  13.0 5.7 %collective-permute-start.3 = (f32[2,24,512]{2,1,0:T(8,128)S(1)}, f32[2,24,512]{2,1,0:T(8,128)S(1)}, u32[]{:S(2)}, u32[]{:S(2)}) collective-permute-start(f32[2,24,512]{2,1,0:T(8,128)S(1)} %pad_maximum_fusion.refs_0_), channel_id=1, source_target_pairs={{0,6},{1,7},{2,0},{3,1},{4,2},{5,3},{6,4},{7,5},{8,14},{9,15},{10,... | collective-permute-start | bytes 294920 | tf_op jit(solution)/shard_map/ppermute | solution.py:476
  16.1 2.6 %copy-start.2 = (f32[2,24,512]{2,1,0:T(8,128)}, f32[2,24,512]{2,1,0:T(8,128)S(1)}, u32[]{:S(2)}) copy-start(f32[2,24,512]{2,1,0:T(8,128)S(1)} %collective-permute-done.1.refs_1_) | copy-start | bytes 294916
  18.6 3.3 %copy-start.3 = (f32[2,24,512]{2,1,0:T(8,128)}, f32[2,24,512]{2,1,0:T(8,128)S(1)}, u32[]{:S(2)}) copy-start(f32[2,24,512]{2,1,0:T(8,128)S(1)} %collective-permute-done.2.refs_2_) | copy-start | bytes 294916
  18.6 3.3 %copy-start.4 = (f32[2,24,512]{2,1,0:T(8,128)}, f32[2,24,512]{2,1,0:T(8,128)S(1)}, u32[]{:S(2)}) copy-start(f32[2,24,512]{2,1,0:T(8,128)S(1)} %collective-permute-done.3.refs_3_) | copy-start | bytes 294916
  18.7 2.5 %collective-permute-start.4 = (f32[24,128]{1,0:T(8,128)S(1)}, f32[24,128]{1,0:T(8,128)S(1)}, u32[]{:S(2)}, u32[]{:S(2)}) collective-permute-start(f32[24,128]{1,0:T(8,128)S(1)} %select_bitcast_fusion.1), channel_id=1, source_target_pairs={{0,8},{8,0},{16,24},{24,16},{1,9},{9,1},{17,25},{25,17},{2,10},{10... | collective-permute-start | bytes 36872 | tf_op jit(solution)/shard_map/ppermute | solution.py:492
  18.8 3.2 %collective-permute-start.5 = (f32[24,128]{1,0:T(8,128)S(1)}, f32[24,128]{1,0:T(8,128)S(1)}, u32[]{:S(2)}, u32[]{:S(2)}) collective-permute-start(f32[24,128]{1,0:T(8,128)S(1)} %get-tuple-element.8), channel_id=1, source_target_pairs={{0,24},{8,16},{16,8},{24,0},{1,25},{9,17},{17,9},{25,1},{2,26},{10... | collective-permute-start | bytes 36872 | tf_op jit(solution)/shard_map/ppermute | solution.py:491
  21.2 0.8 %copy-start.9 = (f32[24,128]{1,0:T(8,128)}, f32[24,128]{1,0:T(8,128)S(1)}, u32[]{:S(2)}) copy-start(f32[24,128]{1,0:T(8,128)S(1)} %collective-permute-done.4.refs_4_) | copy-start | bytes 36868
  22.0 0.6 copy-start.10
  46.3 3.4 %collective-permute-start.6 = (f32[12,128]{1,0:T(8,128)}, f32[12,128]{1,0:T(8,128)S(1)}, u32[]{:S(2)}, u32[]{:S(2)}) collective-permute-start(f32[12,128]{1,0:T(8,128)} %get-tuple-element.6), channel_id=1, source_target_pairs={{0,24},{8,16},{16,8},{24,0},{1,25},{9,17},{17,9},{25,1},{2,26},{10... | collective-permute-start | bytes 18440 | tf_op jit(solution)/shard_map/ppermute | solution.py:535
  47.9 1.7 %collective-permute-start.7 = (f32[12,128]{1,0:T(8,128)}, f32[12,128]{1,0:T(8,128)S(1)}, u32[]{:S(2)}, u32[]{:S(2)}) collective-permute-start(f32[12,128]{1,0:T(8,128)} %get-tuple-element.7), channel_id=1, source_target_pairs={{0,8},{8,0},{16,24},{24,16},{1,9},{9,1},{17,25},{25,17},{2,10},{10... | collective-permute-start | bytes 18440 | tf_op jit(solution)/shard_map/ppermute | solution.py:536
  50.7 5.2 %collective-permute-start.8 = (f32[4,48,128]{2,1,0:T(8,128)S(1)}, f32[4,48,128]{2,1,0:T(8,128)S(1)}, u32[]{:S(2)}, u32[]{:S(2)}) collective-permute-start(f32[4,48,128]{2,1,0:T(8,128)S(1)} %dynamic-slice_bitcast_fusion), channel_id=1, source_target_pairs={{0,1},{1,0},{2,3},{3,2},{4,5},{5,4},{6,7},{7,6},{8,9},{9,8},{10,11... | collective-permute-start | bytes 294920 | tf_op jit(solution)/shard_map/ppermute | solution.py:547
  56.6 4.7 %collective-permute-start.10 = (f32[48,128]{1,0:T(8,128)S(1)}, f32[48,128]{1,0:T(8,128)S(1)}, u32[]{:S(2)}, u32[]{:S(2)}) collective-permute-start(f32[48,128]{1,0:T(8,128)S(1)} %get-tuple-element.12), channel_id=1, source_target_pairs={{0,4},{1,5},{2,6},{3,7},{4,0},{5,1},{6,2},{7,3},{8,12},{9,13},{10,... | collective-permute-start | bytes 73736 | tf_op jit(solution)/shard_map/ppermute | solution.py:552
  57.9 4.9 %collective-permute-start.11 = (f32[48,128]{1,0:T(8,128)S(1)}, f32[48,128]{1,0:T(8,128)S(1)}, u32[]{:S(2)}, u32[]{:S(2)}) collective-permute-start(f32[48,128]{1,0:T(8,128)S(1)} %get-tuple-element.11), channel_id=1, source_target_pairs={{0,6},{1,7},{2,0},{3,1},{4,2},{5,3},{6,4},{7,5},{8,14},{9,15},{10,... | collective-permute-start | bytes 73736 | tf_op jit(solution)/shard_map/ppermute | solution.py:552
  61.2 5.6 %collective-permute-start.9 = (f32[48,128]{1,0:T(8,128)S(1)}, f32[48,128]{1,0:T(8,128)S(1)}, u32[]{:S(2)}, u32[]{:S(2)}) collective-permute-start(f32[48,128]{1,0:T(8,128)S(1)} %get-tuple-element.13), channel_id=1, source_target_pairs={{0,2},{1,3},{2,4},{3,5},{4,6},{5,7},{6,0},{7,1},{8,10},{9,11},{10,... | collective-permute-start | bytes 73736 | tf_op jit(solution)/shard_map/ppermute | solution.py:552
  61.3 5.6 %copy-start.5 = (f32[48,128]{1,0:T(8,128)}, f32[48,128]{1,0:T(8,128)S(1)}, u32[]{:S(2)}) copy-start(f32[48,128]{1,0:T(8,128)S(1)} %collective-permute-done.10.refs_1_) | copy-start | bytes 73732
  62.7 4.1 %copy-start.6 = (f32[48,128]{1,0:T(8,128)}, f32[48,128]{1,0:T(8,128)S(1)}, u32[]{:S(2)}) copy-start(f32[48,128]{1,0:T(8,128)S(1)} %collective-permute-done.11.refs_2_) | copy-start | bytes 73732
  66.8 0.6 copy-start.7

commit v2 on v1

--- a/solution.py
+++ b/solution.py
@@ -16,7 +16,7 @@
 COMPS = 12
 PARAMS = 10
 ROWS = 24
-DEPTH = 2
+DEPTH = 4
 
 
 def split3(value):
@@ -24,6 +24,10 @@
     rest = value - high
     middle = rest.astype(jnp.bfloat16).astype(jnp.float32)
     return high, middle, rest - middle
+
+
+def clique_order(count):
+    return [0, count - 1] + list(range(1, count - 1))
 
 
 def payload_kernel(slots, members, position_ref, rotation_ref, kind_ref, pair_ref, count_ref, out_ref):
@@ -123,7 +127,6 @@
     (inside_ref, across_ref, off_ref, inner_ref, edge_in_ref, edge_over_ref, table, list_ref, word_ref,
      words, gathered, parts, reach_ref, sums_ref, folded_ref, acc_near, acc_far, sem) = refs[piece_count:]
     me = lax.axis_index("dev")
-    along_z, along_y = me // 2, lax.rem(me, 2)
     even = lax.rem(lax.axis_index("grp"), 2) == 0
     own_blocks = pieces[0].shape[2]
     inner_blocks = members * own_blocks
@@ -134,10 +137,7 @@
     counts = []
     for k in range(piece_count):
         for side in range(2):
-            owners.append(
-                lax.rem(along_z - k + piece_count, piece_count) * 2
-                + (along_y if side == 0 else 1 - along_y)
-            )
+            owners.append(jnp.bitwise_xor(me, clique_order(piece_count)[k] + side * piece_count))
             base = (2 * k + side) * 2 * slot_rows
             for part in range(2 * slot_rows):
                 line, spot = part // (own_blocks // LANES), part % (own_blocks // LANES)
@@ -225,18 +225,13 @@
     keeps = [jnp.where((row16 & 7) == sub, 1.0, 0.0).astype(jnp.bfloat16) for sub in range(8)]
 
     def fetch(first):
-        def step(turn, carry):
-            row = (first + turn * 8) >> 7
-            base = (first + turn * 8) & (LANES - 1)
-            for sub in range(8):
-                index = turn * 8 + sub
-                near = words[row, base + sub]
-                far = words[slot_rows + row, base + sub]
-                gathered[pl.ds(index, 1), :] = table[pl.ds(near, 1), :]
-                gathered[pl.ds(CHUNK + index, 1), :] = table[pl.ds(far, 1), :]
-            return carry
-
-        lax.fori_loop(0, CHUNK // 8, step, 0)
+        row = first >> 7
+        base = first & (LANES - 1)
+        for index in range(CHUNK):
+            near = words[row, base + index]
+            far = words[slot_rows + row, base + index]
+            gathered[pl.ds(index, 1), :] = table[pl.ds(near, 1), :]
+            gathered[pl.ds(CHUNK + index, 1), :] = table[pl.ds(far, 1), :]
 
     def arrange(first):
         def keep_part(slot, value):
@@ -374,11 +369,11 @@
             )
 
     def chunk(turn, carry):
-        first = pl.multiple_of(turn * CHUNK, CHUNK)
-        fetch(first)
-        arrange(first)
+        arrange(pl.multiple_of(turn * CHUNK, CHUNK))
+        fetch(jnp.minimum((turn + 1) * CHUNK, slots - CHUNK))
         return carry
 
+    fetch(jnp.int32(0))
     lax.fori_loop(0, (number + CHUNK - 1) // CHUNK, chunk, 0)
 
     groups = (number + 7) // 8
@@ -387,6 +382,9 @@
     def octet(turn, slot):
         fresh = 4 * LANES * slot
         stale = 4 * LANES * (1 - slot)
+        ready = prepare(pl.multiple_of(jnp.minimum(turn, groups - 1) * 8, 8))
+        for couple, pair in enumerate(pairs):
+            reach_ref[pl.ds(fresh + LANES * couple, LANES), :] = reach_of(*ready, pair)
         scatter(turn - 3)
         base = jnp.clip(turn - 2, 0, groups - 1) * 8
         terms = [
@@ -396,21 +394,18 @@
         folded_ref[...] = jnp.dot(
             jnp.concatenate(terms, 0), halves, preferred_element_type=jnp.float32
         )
-        ready = prepare(pl.multiple_of(jnp.minimum(turn, groups - 1) * 8, 8))
-        for couple, pair in enumerate(pairs):
-            reach_ref[pl.ds(fresh + LANES * couple, LANES), :] = reach_of(*ready, pair)
         base = jnp.clip(turn - 1, 0, groups - 1) * 8
         for couple, pair in enumerate(pairs):
             sums_ref[pl.ds(64 * couple, 64), :] = sums_of(
                 reach_ref[pl.ds(stale + LANES * couple, LANES), :], base, pair
             )
 
-    def octet_pair(turn, carry):
+    def octets(turn, carry):
         for sub in range(DEPTH):
             octet(DEPTH * turn + sub, sub % 2)
         return carry
 
-    lax.fori_loop(0, (groups + 2 + DEPTH) // DEPTH, octet_pair, 0)
+    lax.fori_loop(0, (groups + 2 + DEPTH) // DEPTH, octets, 0)
 
     def total_of(row, half, tiles, start):
         line = (row // 3) * 8 + row % 3
@@ -449,8 +444,8 @@
     groups = lax.axis_size("grp")
     group = lax.axis_index("grp")
     me = lax.axis_index("dev")
-    along_z, along_y = me // 2, me % 2
     rings = members // 2
+    clique, far = me % rings, me // rings
     clumps = positions.shape[1]
     slots = pair_blocks.shape[1]
     own_blocks = clumps // 2
@@ -468,21 +463,19 @@
         name="payload_kernel",
     )(positions, rotations, clump_kind.reshape(-1, LANES), pair_blocks, pair_count)
 
-    pair_y = [(i, i ^ 1) for i in range(members)]
-    both = jnp.stack([payload, lax.ppermute(payload, "dev", pair_y)])
-    pieces = [both]
-    for k in range(1, rings):
-        pieces.append(
-            lax.ppermute(both, "dev", [(i, (i + 2 * k) % members) for i in range(members)])
-        )
+    def trade(value, k):
+        return lax.ppermute(value, "dev", [(i, i ^ k) for i in range(members)])
+
+    both = jnp.stack([payload, trade(payload, rings)])
+    order = clique_order(rings)
+    pieces = [both] + [trade(both, k) for k in order[1:]]
 
     def piece_columns(member, start):
-        z, y = member // 2, member % 2
         found = None
-        for k in range(rings):
-            part = pieces[k][:, :, start : start + RIM]
-            part = jnp.where(along_y == y, part[0], part[1])
-            hit = (along_z - k + rings) % rings == z
+        for k, piece in zip(order, pieces):
+            part = piece[:, :, start : start + RIM]
+            part = jnp.where(far == member // rings, part[0], part[1])
+            hit = clique ^ k == member % rings
             found = part if found is None else jnp.where(hit, part, found)
         return found
 
@@ -541,20 +534,20 @@
     )
 
     own_rows = tiles * COMPS // members
-    ranks = inner.reshape(rings, 2, own_rows, LANES)
-    mine = lax.dynamic_index_in_dim(ranks, along_y, 1, False)
-    other = lax.dynamic_index_in_dim(ranks, 1 - along_y, 1, False)
-    column = mine + lax.ppermute(other, "dev", pair_y)
-    shares = [lax.dynamic_index_in_dim(column, along_z, 0, False)]
-    for k in range(1, rings):
-        part = lax.dynamic_index_in_dim(column, (along_z + k) % rings, 0, False)
-        shares.append(
-            lax.ppermute(part, "dev", [(i, (i + 2 * k) % members) for i in range(members)])
-        )
+    ranks = inner.reshape(2, rings, own_rows, LANES)
+
+    def share(k):
+        return lax.dynamic_index_in_dim(ranks, clique ^ k, 1, False)
+
+    column = share(0)
+    for k in order[:0:-1]:
+        column = column + trade(share(k), k)
+    kept = lax.dynamic_index_in_dim(column, far, 0, False)
+    shares = [kept, trade(lax.dynamic_index_in_dim(column, 1 - far, 0, False), rings)]
     clump_force, clump_torque = pl.pallas_call(
         finish_kernel,
         out_shape=(jax.ShapeDtypeStruct((3, clumps), jnp.float32),) * 2,
-        in_specs=[vmem] * (rings + 1),
+        in_specs=[vmem] * 3,
         out_specs=(vmem, vmem),
         scratch_shapes=[pltpu.VMEM((own_rows, LANES), jnp.float32)],
         name="finish_kernel",

time: 69.4 us -> 63 us (0.908)
  waiting for transfers between devices: 17.9 us -> 14.2 us
  Pallas kernels: 26.9 us -> 24.2 us
    ppermute x8, waiting for transfers between devices: 15.5 us -> 12.4 us  [trade(): return lax.ppermute(value, 'dev', [(i, i ^ k) for i in range(members)])]
    pallas_call x1, Pallas kernels: 23.7 us -> 21 us  [shards(): pl.pallas_call(functools.partial(pair_kernel, members, slots), out_shape=...]
    ppermute x1, starting transfers between devices: 0.01 us -> 1.59 us  [shards(): got_in = lax.ppermute(edge_in, 'grp', inside)]
    ppermute x1, waiting for transfers between devices: 1.62 us -> 0.11 us  [shards(): got_over = lax.ppermute(edge_over, 'grp', across)]
    ppermute x8, starting transfers between devices: 15.4 us -> 14.2 us  [trade(): return lax.ppermute(value, 'dev', [(i, i ^ k) for i in range(members)])]
    ppermute x1, waiting for transfers between devices: 0.01 us -> 0.85 us  [shards(): got_in = lax.ppermute(edge_in, 'grp', inside)]
  transfers between devices with their start and end apart: 12 -> 12, of which waited for: 9 -> 11; matrix products, arithmetic and copies ran while one was open for 1% -> 2% of each run, Pallas kernels for 0% -> 0%
where the time goes in v2:
time: 63 us; the launch traced here: 62.8 us
  Pallas kernels  24.2 us (38%)
  starting transfers between devices  19 us (30%)
  waiting for transfers between devices  14.2 us (23%)
  local copies, waits for them, and re-layouts  2.11 us (3%)
  other arithmetic  1.83 us (3%)
  between operations  1.46 us (2%)
    pallas_call x1, Pallas kernels, shards(): pl.pallas_call(functools.partial(pair_kernel, members, slots), out_shape=...  21 us
    ppermute x8, starting transfers between devices, trade(): return lax.ppermute(value, 'dev', [(i, i ^ k) for i in range(members)])  14.2 us
    ppermute x8, waiting for transfers between devices, trade(): return lax.ppermute(value, 'dev', [(i, i ^ k) for i in range(members)])  12.4 us
    pallas_call x1, Pallas kernels, shards(): pl.pallas_call(functools.partial(payload_kernel, slots, members), out_sha...  1.65 us
    ppermute x1, starting transfers between devices, shards(): got_across = lax.ppermute(jnp.where(even, first, last), 'grp', across)  1.59 us
    ppermute x1, starting transfers between devices, shards(): got_in = lax.ppermute(edge_in, 'grp', inside)  1.59 us
    ppermute x1, starting transfers between devices, shards(): got_over = lax.ppermute(edge_over, 'grp', across)  1.57 us
    pallas_call x1, Pallas kernels, shards(): pl.pallas_call(finish_kernel, out_shape=(jax.ShapeDtypeStruct((3, clumps)...  1.54 us
  transfers between devices with their start and end apart: 12, of which 11 were waited for; matrix products, arithmetic and copies ran while one was open for 2% of the time, Pallas kernels for 0%

profile of v2, /device:TPU:0, one launch (start us, length us, event | category | flops | bytes accessed | tf_op | source)
XLA Modules:
  0.0 62.8 jit_solution(8241128946817007550)
XLA Ops:
  1.3 0.0 copy-start.6
  1.3 1.7 %payload_kernel.1 = f32[24,512]{1,0:T(8,128)} custom-call(f32[3,1024]{1,0:T(4,128)} %refs_1_.1, f32[9,1024]{1,0:T(8,128)} %rotation_ref.1, s32[8,128]{1,0:T(8,128)} %bitcast.34, s32[2,1024]{1,0:T(2,128)} %pair_ref.1, s32[1]{0:T(128)S(6)} %copy.8.count_ref), custom_call_target="tpu_custom_call" | custom-call | tf_op jit(solution)/shard_map/payload_kernel/pallas_call | solution.py:458
  2.9 4.1 %collective-permute-start = (f32[24,512]{1,0:T(8,128)}, f32[24,512]{1,0:T(8,128)S(1)}, u32[]{:S(2)}, u32[]{:S(2)}) collective-permute-start(f32[24,512]{1,0:T(8,128)} %payload_kernel.1), channel_id=1, source_target_pairs={{0,4},{1,5},{2,6},{3,7},{4,0},{5,1},{6,2},{7,3},{8,12},{9,13},{10,... | collective-permute-start | bytes 147464 | tf_op jit(solution)/shard_map/ppermute | solution.py:467
  7.0 0.0 copy-done.6
  7.0 0.0 copy-start.1
  7.1 0.1 pad.9.clone
  7.2 2.6 %collective-permute-done = f32[24,512]{1,0:T(8,128)S(1)} collective-permute-done((f32[24,512]{1,0:T(8,128)}, f32[24,512]{1,0:T(8,128)S(1)}, u32[]{:S(2)}, u32[]{:S(2)}) %collective-permute-start) | collective-permute-done | bytes 49184 | tf_op jit(solution)/shard_map/ppermute | solution.py:467
  9.8 0.0 copy-done.1
  9.8 0.0 copy-start
  9.8 2.4 %collective-permute-start.1 = (f32[2,24,512]{2,1,0:T(8,128)S(1)}, f32[2,24,512]{2,1,0:T(8,128)S(1)}, u32[]{:S(2)}, u32[]{:S(2)}) collective-permute-start(f32[2,24,512]{2,1,0:T(8,128)S(1)} %pad_maximum_fusion.refs_0_), channel_id=1, source_target_pairs={{0,3},{1,2},{2,1},{3,0},{4,7},{5,6},{6,5},{7,4},{8,11},{9,10},{10,... | collective-permute-start | bytes 294920 | tf_op jit(solution)/shard_map/ppermute | solution.py:467
  12.2 0.5 collective-permute-start.2
  12.7 0.6 %collective-permute-start.3 = (f32[2,24,512]{2,1,0:T(8,128)S(1)}, f32[2,24,512]{2,1,0:T(8,128)S(1)}, u32[]{:S(2)}, u32[]{:S(2)}) collective-permute-start(f32[2,24,512]{2,1,0:T(8,128)S(1)} %pad_maximum_fusion.refs_0_), channel_id=1, source_target_pairs={{0,2},{1,3},{2,0},{3,1},{4,6},{5,7},{6,4},{7,5},{8,10},{9,11},{10,... | collective-permute-start | bytes 294920 | tf_op jit(solution)/shard_map/ppermute | solution.py:467
  13.4 0.1 pad_bitcast_fusion.1
  13.5 2.9 %collective-permute-done.1.refs_1_ = f32[2,24,512]{2,1,0:T(8,128)S(1)} collective-permute-done((f32[2,24,512]{2,1,0:T(8,128)S(1)}, f32[2,24,512]{2,1,0:T(8,128)S(1)}, u32[]{:S(2)}, u32[]{:S(2)}) %collective-permute-start.1) | collective-permute-done | bytes 98336 | tf_op jit(solution)/shard_map/ppermute | solution.py:467
  16.4 0.0 copy-start.2
  16.4 0.8 %collective-permute-done.2.refs_2_ = f32[2,24,512]{2,1,0:T(8,128)S(1)} collective-permute-done((f32[2,24,512]{2,1,0:T(8,128)S(1)}, f32[2,24,512]{2,1,0:T(8,128)S(1)}, u32[]{:S(2)}, u32[]{:S(2)}) %collective-permute-start.2) | collective-permute-done | bytes 98336 | tf_op jit(solution)/shard_map/ppermute | solution.py:467
  17.1 0.0 copy-start.3
  17.1 0.2 collective-permute-done.3.refs_3_
  17.4 0.0 copy-start.4
  17.4 0.0 copy-done
  17.4 0.0 copy-done.2
  17.4 0.1 collective-permute-start.4
  17.5 1.6 %collective-permute-start.5 = (f32[24,128]{1,0:T(8,128)S(1)}, f32[24,128]{1,0:T(8,128)S(1)}, u32[]{:S(2)}, u32[]{:S(2)}) collective-permute-start(f32[24,128]{1,0:T(8,128)S(1)} %get-tuple-element.8), channel_id=1, source_target_pairs={{0,24},{8,16},{16,8},{24,0},{1,25},{9,17},{17,9},{25,1},{2,26},{10... | collective-permute-start | bytes 36872 | tf_op jit(solution)/shard_map/ppermute | solution.py:484
  19.1 0.7 %maximum_maximum_fusion.refs_6_ = bf16[128,384]{1,0:T(8,128)(2,1)} fusion(bf16[8,384]{1,0:T(8,128)(2,1)S(1)} %get-tuple-element.19, bf16[8,384]{1,0:T(8,128)(2,1)S(1)} %get-tuple-element.18, bf16[128]{0:T(256)(128)(2,1)S(1)} %pad.9.clone), kind=kLoop, calls=%fused_computation.2 | loop fusion | flops 294912 | bytes 110848 | tf_op jit(solution)/shard_map/concatenate | solution.py:496
  19.8 0.0 collective-permute-done.4.refs_4_
  19.8 0.0 copy-start.7
  19.8 0.9 %collective-permute-done.5.refs_5_ = f32[24,128]{1,0:T(8,128)S(1)} collective-permute-done((f32[24,128]{1,0:T(8,128)S(1)}, f32[24,128]{1,0:T(8,128)S(1)}, u32[]{:S(2)}, u32[]{:S(2)}) %collective-permute-start.5) | collective-permute-done | bytes 12320 | tf_op jit(solution)/shard_map/ppermute | solution.py:484
  20.7 0.0 copy-done.3
  20.7 0.0 copy-done.4
  20.7 0.0 copy-done.7
  20.7 0.0 copy-start.8
  20.7 0.6 copy-done.8
  21.3 21.0 %pair_kernel.1 = (f32[384,128]{1,0:T(8,128)}, f32[12,128]{1,0:T(8,128)}, f32[12,128]{1,0:T(8,128)}) custom-call(f32[2,24,512]{2,1,0:T(8,128)} %copy-done, f32[2,24,512]{2,1,0:T(8,128)} %copy-done.2, f32[2,24,512]{2,1,0:T(8,128)} %copy-done.3, f32[2,24,512]{2,1,0:T(8,128)} %copy-done.4, f32[24,128]{1,0:T(8,128)} %copy-done.7, f32[24,128]{1,0:T(8,128)} %copy-done.8, ...), custom_call_target="tpu_custom_call" | custom-call | tf_op jit(solution)/shard_map/pair_kernel/pallas_call | solution.py:502
  42.3 1.6 %collective-permute-start.6 = (f32[12,128]{1,0:T(8,128)}, f32[12,128]{1,0:T(8,128)S(1)}, u32[]{:S(2)}, u32[]{:S(2)}) collective-permute-start(f32[12,128]{1,0:T(8,128)} %get-tuple-element.6), channel_id=1, source_target_pairs={{0,24},{8,16},{16,8},{24,0},{1,25},{9,17},{17,9},{25,1},{2,26},{10... | collective-permute-start | bytes 18440 | tf_op jit(solution)/shard_map/ppermute | solution.py:528
  43.9 1.6 %collective-permute-start.7 = (f32[12,128]{1,0:T(8,128)}, f32[12,128]{1,0:T(8,128)S(1)}, u32[]{:S(2)}, u32[]{:S(2)}) collective-permute-start(f32[12,128]{1,0:T(8,128)} %get-tuple-element.7), channel_id=1, source_target_pairs={{0,8},{8,0},{16,24},{24,16},{1,9},{9,1},{17,25},{25,17},{2,10},{10... | collective-permute-start | bytes 18440 | tf_op jit(solution)/shard_map/ppermute | solution.py:529
  45.4 0.1 pad.5.clone
  45.5 0.1 collective-permute-done.6
  45.6 0.8 %collective-permute-done.7 = f32[12,128]{1,0:T(8,128)S(1)} collective-permute-done((f32[12,128]{1,0:T(8,128)}, f32[12,128]{1,0:T(8,128)S(1)}, u32[]{:S(2)}, u32[]{:S(2)}) %collective-permute-start.7) | collective-permute-done | bytes 6176 | tf_op jit(solution)/shard_map/ppermute | solution.py:529
  46.5 1.0 %maximum_add_fusion = f32[384,128]{1,0:T(8,128)S(1)} fusion(f32[384,128]{1,0:T(8,128)} %get-tuple-element.5, f32[12,128]{1,0:T(8,128)S(1)} %get-tuple-element.17, f32[12,128]{1,0:T(8,128)S(1)} %get-tuple-element.16, f32[384]{0:T(512)S(1)} %pad.5.clone), kind=kLoop, calls=%fused_computation | loop fusion | flops 147456 | bytes 407040 | tf_op jit(solution)/shard_map/add | solution.py:532
  47.6 1.9 %collective-permute-start.10 = (f32[2,48,128]{2,1,0:T(8,128)S(1)}, f32[2,48,128]{2,1,0:T(8,128)S(1)}, u32[]{:S(2)}, u32[]{:S(2)}) collective-permute-start(f32[2,48,128]{2,1,0:T(8,128)S(1)} %get-tuple-element.12), channel_id=1, source_target_pairs={{0,3},{1,2},{2,1},{3,0},{4,7},{5,6},{6,5},{7,4},{8,11},{9,10},{10,... | collective-permute-start | bytes 147464 | tf_op jit(solution)/shard_map/ppermute | solution.py:467
  49.4 1.2 %collective-permute-start.8 = (f32[2,48,128]{2,1,0:T(8,128)S(1)}, f32[2,48,128]{2,1,0:T(8,128)S(1)}, u32[]{:S(2)}, u32[]{:S(2)}) collective-permute-start(f32[2,48,128]{2,1,0:T(8,128)S(1)} %get-tuple-element.11), channel_id=1, source_target_pairs={{0,2},{1,3},{2,0},{3,1},{4,6},{5,7},{6,4},{7,5},{8,10},{9,11},{10,... | collective-permute-start | bytes 147464 | tf_op jit(solution)/shard_map/ppermute | solution.py:467
  50.6 0.5 collective-permute-start.9
  51.1 1.5 %collective-permute-done.10 = f32[2,48,128]{2,1,0:T(8,128)S(1)} collective-permute-done((f32[2,48,128]{2,1,0:T(8,128)S(1)}, f32[2,48,128]{2,1,0:T(8,128)S(1)}, u32[]{:S(2)}, u32[]{:S(2)}) %collective-permute-start.10) | collective-permute-done | bytes 49184 | tf_op jit(solution)/shard_map/ppermute | solution.py:467
  52.6 1.1 %collective-permute-done.8 = f32[2,48,128]{2,1,0:T(8,128)S(1)} collective-permute-done((f32[2,48,128]{2,1,0:T(8,128)S(1)}, f32[2,48,128]{2,1,0:T(8,128)S(1)}, u32[]{:S(2)}, u32[]{:S(2)}) %collective-permute-start.8) | collective-permute-done | bytes 49184 | tf_op jit(solution)/shard_map/ppermute | solution.py:467
  53.7 1.0 %collective-permute-done.9 = f32[2,48,128]{2,1,0:T(8,128)S(1)} collective-permute-done((f32[2,48,128]{2,1,0:T(8,128)S(1)}, f32[2,48,128]{2,1,0:T(8,128)S(1)}, u32[]{:S(2)}, u32[]{:S(2)}) %collective-permute-start.9) | collective-permute-done | bytes 49184 | tf_op jit(solution)/shard_map/ppermute | solution.py:467
  54.7 0.6 dynamic-slice_bitcast_fusion.3
  55.3 3.0 %collective-permute-start.11 = (f32[48,128]{1,0:T(8,128)S(1)}, f32[48,128]{1,0:T(8,128)S(1)}, u32[]{:S(2)}, u32[]{:S(2)}) collective-permute-start(f32[48,128]{1,0:T(8,128)S(1)} %get-tuple-element.14), channel_id=1, source_target_pairs={{0,4},{1,5},{2,6},{3,7},{4,0},{5,1},{6,2},{7,3},{8,12},{9,13},{10,... | collective-permute-start | bytes 73736 | tf_op jit(solution)/shard_map/ppermute | solution.py:467
  58.4 2.3 %collective-permute-done.11.refs_0_ = f32[48,128]{1,0:T(8,128)S(1)} collective-permute-done((f32[48,128]{1,0:T(8,128)S(1)}, f32[48,128]{1,0:T(8,128)S(1)}, u32[]{:S(2)}, u32[]{:S(2)}) %collective-permute-start.11) | collective-permute-done | bytes 24608 | tf_op jit(solution)/shard_map/ppermute | solution.py:467
  60.6 0.0 copy-start.5
  60.6 0.6 copy-done.5
  61.2 1.5 %finish_kernel.1 = (f32[3,1024]{1,0:T(4,128)}, f32[3,1024]{1,0:T(4,128)}) custom-call(f32[48,128]{1,0:T(8,128)} %get-tuple-element.15.own_ref, f32[48,128]{1,0:T(8,128)} %copy-done.5, f32[3,1024]{1,0:T(4,128)} %refs_1_.1), custom_call_target="tpu_custom_call" | custom-call | tf_op jit(solution)/shard_map/finish_kernel/pallas_call | solution.py:547
  (9 shorter events, 0.1 us)
Async XLA Ops:
  1.3 5.7 %copy-start.6 = (s32[8,3,64]{2,0,1:T(8,128)S(1)}, s32[8,3,64]{2,0,1:T(8,128)}, u32[]{:S(2)}) copy-start(s32[8,3,64]{2,0,1:T(8,128)} %param.9) | copy-start | bytes 18436
  2.9 6.9 %collective-permute-start = (f32[24,512]{1,0:T(8,128)}, f32[24,512]{1,0:T(8,128)S(1)}, u32[]{:S(2)}, u32[]{:S(2)}) collective-permute-start(f32[24,512]{1,0:T(8,128)} %payload_kernel.1), channel_id=1, source_target_pairs={{0,4},{1,5},{2,6},{3,7},{4,0},{5,1},{6,2},{7,3},{8,12},{9,13},{10,... | collective-permute-start | bytes 147464 | tf_op jit(solution)/shard_map/ppermute | solution.py:467
  7.0 2.8 %copy-start.1 = (f32[24,512]{1,0:T(8,128)S(1)}, f32[24,512]{1,0:T(8,128)}, u32[]{:S(2)}) copy-start(f32[24,512]{1,0:T(8,128)} %payload_kernel.1) | copy-start | bytes 147460
  9.8 7.6 %copy-start = (f32[2,24,512]{2,1,0:T(8,128)}, f32[2,24,512]{2,1,0:T(8,128)S(1)}, u32[]{:S(2)}) copy-start(f32[2,24,512]{2,1,0:T(8,128)S(1)} %pad_maximum_fusion.refs_0_) | copy-start | bytes 294916
  9.8 6.5 %collective-permute-start.1 = (f32[2,24,512]{2,1,0:T(8,128)S(1)}, f32[2,24,512]{2,1,0:T(8,128)S(1)}, u32[]{:S(2)}, u32[]{:S(2)}) collective-permute-start(f32[2,24,512]{2,1,0:T(8,128)S(1)} %pad_maximum_fusion.refs_0_), channel_id=1, source_target_pairs={{0,3},{1,2},{2,1},{3,0},{4,7},{5,6},{6,5},{7,4},{8,11},{9,10},{10,... | collective-permute-start | bytes 294920 | tf_op jit(solution)/shard_map/ppermute | solution.py:467
  12.2 4.9 %collective-permute-start.2 = (f32[2,24,512]{2,1,0:T(8,128)S(1)}, f32[2,24,512]{2,1,0:T(8,128)S(1)}, u32[]{:S(2)}, u32[]{:S(2)}) collective-permute-start(f32[2,24,512]{2,1,0:T(8,128)S(1)} %pad_maximum_fusion.refs_0_), channel_id=1, source_target_pairs={{0,1},{1,0},{2,3},{3,2},{4,5},{5,4},{6,7},{7,6},{8,9},{9,8},{10,11... | collective-permute-start | bytes 294920 | tf_op jit(solution)/shard_map/ppermute | solution.py:467
  12.7 4.6 %collective-permute-start.3 = (f32[2,24,512]{2,1,0:T(8,128)S(1)}, f32[2,24,512]{2,1,0:T(8,128)S(1)}, u32[]{:S(2)}, u32[]{:S(2)}) collective-permute-start(f32[2,24,512]{2,1,0:T(8,128)S(1)} %pad_maximum_fusion.refs_0_), channel_id=1, source_target_pairs={{0,2},{1,3},{2,0},{3,1},{4,6},{5,7},{6,4},{7,5},{8,10},{9,11},{10,... | collective-permute-start | bytes 294920 | tf_op jit(solution)/shard_map/ppermute | solution.py:467
  16.4 1.0 %copy-start.2 = (f32[2,24,512]{2,1,0:T(8,128)}, f32[2,24,512]{2,1,0:T(8,128)S(1)}, u32[]{:S(2)}) copy-start(f32[2,24,512]{2,1,0:T(8,128)S(1)} %collective-permute-done.1.refs_1_) | copy-start | bytes 294916
  17.1 3.6 %copy-start.3 = (f32[2,24,512]{2,1,0:T(8,128)}, f32[2,24,512]{2,1,0:T(8,128)S(1)}, u32[]{:S(2)}) copy-start(f32[2,24,512]{2,1,0:T(8,128)S(1)} %collective-permute-done.2.refs_2_) | copy-start | bytes 294916
  17.4 3.3 %copy-start.4 = (f32[2,24,512]{2,1,0:T(8,128)}, f32[2,24,512]{2,1,0:T(8,128)S(1)}, u32[]{:S(2)}) copy-start(f32[2,24,512]{2,1,0:T(8,128)S(1)} %collective-permute-done.3.refs_3_) | copy-start | bytes 294916
  17.4 2.4 %collective-permute-start.4 = (f32[24,128]{1,0:T(8,128)S(1)}, f32[24,128]{1,0:T(8,128)S(1)}, u32[]{:S(2)}, u32[]{:S(2)}) collective-permute-start(f32[24,128]{1,0:T(8,128)S(1)} %select_bitcast_fusion.1), channel_id=1, source_target_pairs={{0,8},{8,0},{16,24},{24,16},{1,9},{9,1},{17,25},{25,17},{2,10},{10... | collective-permute-start | bytes 36872 | tf_op jit(solution)/shard_map/ppermute | solution.py:485
  17.5 3.2 %collective-permute-start.5 = (f32[24,128]{1,0:T(8,128)S(1)}, f32[24,128]{1,0:T(8,128)S(1)}, u32[]{:S(2)}, u32[]{:S(2)}) collective-permute-start(f32[24,128]{1,0:T(8,128)S(1)} %get-tuple-element.8), channel_id=1, source_target_pairs={{0,24},{8,16},{16,8},{24,0},{1,25},{9,17},{17,9},{25,1},{2,26},{10... | collective-permute-start | bytes 36872 | tf_op jit(solution)/shard_map/ppermute | solution.py:484
  19.8 0.9 %copy-start.7 = (f32[24,128]{1,0:T(8,128)}, f32[24,128]{1,0:T(8,128)S(1)}, u32[]{:S(2)}) copy-start(f32[24,128]{1,0:T(8,128)S(1)} %collective-permute-done.4.refs_4_) | copy-start | bytes 36868
  20.7 0.6 copy-start.8
  42.3 3.4 %collective-permute-start.6 = (f32[12,128]{1,0:T(8,128)}, f32[12,128]{1,0:T(8,128)S(1)}, u32[]{:S(2)}, u32[]{:S(2)}) collective-permute-start(f32[12,128]{1,0:T(8,128)} %get-tuple-element.6), channel_id=1, source_target_pairs={{0,24},{8,16},{16,8},{24,0},{1,25},{9,17},{17,9},{25,1},{2,26},{10... | collective-permute-start | bytes 18440 | tf_op jit(solution)/shard_map/ppermute | solution.py:528
  43.9 2.6 %collective-permute-start.7 = (f32[12,128]{1,0:T(8,128)}, f32[12,128]{1,0:T(8,128)S(1)}, u32[]{:S(2)}, u32[]{:S(2)}) collective-permute-start(f32[12,128]{1,0:T(8,128)} %get-tuple-element.7), channel_id=1, source_target_pairs={{0,8},{8,0},{16,24},{24,16},{1,9},{9,1},{17,25},{25,17},{2,10},{10... | collective-permute-start | bytes 18440 | tf_op jit(solution)/shard_map/ppermute | solution.py:529
  47.6 5.1 %collective-permute-start.10 = (f32[2,48,128]{2,1,0:T(8,128)S(1)}, f32[2,48,128]{2,1,0:T(8,128)S(1)}, u32[]{:S(2)}, u32[]{:S(2)}) collective-permute-start(f32[2,48,128]{2,1,0:T(8,128)S(1)} %get-tuple-element.12), channel_id=1, source_target_pairs={{0,3},{1,2},{2,1},{3,0},{4,7},{5,6},{6,5},{7,4},{8,11},{9,10},{10,... | collective-permute-start | bytes 147464 | tf_op jit(solution)/shard_map/ppermute | solution.py:467
  49.4 4.2 %collective-permute-start.8 = (f32[2,48,128]{2,1,0:T(8,128)S(1)}, f32[2,48,128]{2,1,0:T(8,128)S(1)}, u32[]{:S(2)}, u32[]{:S(2)}) collective-permute-start(f32[2,48,128]{2,1,0:T(8,128)S(1)} %get-tuple-element.11), channel_id=1, source_target_pairs={{0,2},{1,3},{2,0},{3,1},{4,6},{5,7},{6,4},{7,5},{8,10},{9,11},{10,... | collective-permute-start | bytes 147464 | tf_op jit(solution)/shard_map/ppermute | solution.py:467
  50.6 4.1 %collective-permute-start.9 = (f32[2,48,128]{2,1,0:T(8,128)S(1)}, f32[2,48,128]{2,1,0:T(8,128)S(1)}, u32[]{:S(2)}, u32[]{:S(2)}) collective-permute-start(f32[2,48,128]{2,1,0:T(8,128)S(1)} %get-tuple-element.13), channel_id=1, source_target_pairs={{0,1},{1,0},{2,3},{3,2},{4,5},{5,4},{6,7},{7,6},{8,9},{9,8},{10,11... | collective-permute-start | bytes 147464 | tf_op jit(solution)/shard_map/ppermute | solution.py:467
  55.3 5.3 %collective-permute-start.11 = (f32[48,128]{1,0:T(8,128)S(1)}, f32[48,128]{1,0:T(8,128)S(1)}, u32[]{:S(2)}, u32[]{:S(2)}) collective-permute-start(f32[48,128]{1,0:T(8,128)S(1)} %get-tuple-element.14), channel_id=1, source_target_pairs={{0,4},{1,5},{2,6},{3,7},{4,0},{5,1},{6,2},{7,3},{8,12},{9,13},{10,... | collective-permute-start | bytes 73736 | tf_op jit(solution)/shard_map/ppermute | solution.py:467
  60.6 0.6 copy-start.5

commit v3 on v2

--- a/solution.py
+++ b/solution.py
@@ -16,6 +16,7 @@
 COMPS = 12
 PARAMS = 10
 ROWS = 24
+RIM_ROWS = 16
 DEPTH = 4
 
 
@@ -30,7 +31,7 @@
     return [0, count - 1] + list(range(1, count - 1))
 
 
-def payload_kernel(slots, members, position_ref, rotation_ref, kind_ref, pair_ref, count_ref, out_ref):
+def payload_kernel(slots, members, position_ref, rotation_ref, kind_ref, pair_ref, count_ref, out_ref, end_ref):
     clumps = position_ref.shape[1]
     blocks = clumps // 2
     inner_blocks = blocks * members
@@ -76,15 +77,19 @@
             out_ref[pl.ds(2 * PARAMS + which * lists + part, 1), :] = pairs[
                 which : which + 1, part * blocks : (part + 1) * blocks
             ]
-
-
-def finish_kernel(own_ref, *refs):
-    parts = refs[:-4]
-    position_ref, force_ref, torque_ref, total_ref = refs[-4:]
-    total = own_ref[...]
-    for part in parts:
-        total = total + part[...]
-    total_ref[...] = total
+    in_low = lax.axis_index("dev") < members // 2
+    end_ref[...] = jnp.where(in_low, out_ref[:, :RIM], out_ref[:, blocks - RIM :])
+
+
+def finish_kernel(members, groups, own_ref, *refs):
+    other_ref, rim_a_ref, rim_b_ref, position_ref, force_ref, torque_ref, total_ref = refs
+    me, group = lax.axis_index("dev"), lax.axis_index("grp")
+    total_ref[...] = own_ref[...] + other_ref[...]
+    rim = rim_a_ref[0:COMPS] + rim_b_ref[0:COMPS]
+    first = (me == 0) & (group > 0)
+    final = (me == members - 1) & (group < groups - 1)
+    total_ref[0:COMPS] += jnp.where(first, rim, 0.0)
+    total_ref[own_ref.shape[0] - COMPS :] += jnp.where(final, rim, 0.0)
     tiles = own_ref.shape[0] // COMPS
     wide = 2 * LANES
     row = lax.broadcasted_iota(jnp.int32, (wide, wide), 0)
@@ -124,11 +129,13 @@
 def pair_kernel(members, slots, *refs):
     piece_count = members // 2
     pieces = refs[:piece_count]
-    (inside_ref, across_ref, off_ref, inner_ref, edge_in_ref, edge_over_ref, table, list_ref, word_ref,
-     words, gathered, parts, reach_ref, sums_ref, folded_ref, acc_near, acc_far, sem) = refs[piece_count:]
+    off_ref = refs[piece_count]
+    outs = refs[piece_count + 1 : 2 * piece_count + 1]
+    (table, list_ref, word_ref, words, gathered, parts, reach_ref, sums_ref, folded_ref, acc_near,
+     acc_far, sem) = refs[2 * piece_count + 1 :]
     me = lax.axis_index("dev")
-    even = lax.rem(lax.axis_index("grp"), 2) == 0
-    own_blocks = pieces[0].shape[2]
+    clique = lax.rem(me, piece_count)
+    own_blocks = (pieces[0].shape[1] - RIM) // 2
     inner_blocks = members * own_blocks
     slot_rows = slots // LANES
     lists = slots // own_blocks
@@ -141,8 +148,9 @@
             base = (2 * k + side) * 2 * slot_rows
             for part in range(2 * slot_rows):
                 line, spot = part // (own_blocks // LANES), part % (own_blocks // LANES)
+                at = side * own_blocks + spot * LANES
                 list_ref[pl.ds(base + part, 1), :] = pieces[k][
-                    side, pl.ds(2 * PARAMS + line, 1), spot * LANES : (spot + 1) * LANES
+                    pl.ds(2 * PARAMS + line, 1), at : at + LANES
                 ]
             found = jnp.where(list_ref[pl.ds(base, slot_rows), :] >= 0.0, 1.0, 0.0)
             counts.append(jnp.sum(found).astype(jnp.int32))
@@ -189,11 +197,13 @@
         for side in range(2):
             base = pl.multiple_of(owners[2 * k + side] * own_blocks, LANES)
             for tile in range(own_blocks // LANES):
-                at = slice(tile * LANES, (tile + 1) * LANES)
-                table[pl.ds(base + tile * LANES, LANES), 0:ROWS] = pieces[k][side, :, at].T
-    below = jnp.where(even, 0, LANES)
-    table[pl.ds(pl.multiple_of(inner_blocks + below, LANES), LANES), 0:ROWS] = across_ref[...].T
-    table[pl.ds(pl.multiple_of(inner_blocks + LANES - below, LANES), LANES), 0:ROWS] = inside_ref[...].T
+                at = side * own_blocks + tile * LANES
+                table[pl.ds(base + tile * LANES, LANES), 0:ROWS] = pieces[k][:, at : at + LANES].T
+        place = jnp.bitwise_xor(clique, clique_order(piece_count)[k])
+        base = jnp.where(place == 0, RIM, jnp.where(place == piece_count - 1, 0, 2 * RIM))
+        table[pl.ds(pl.multiple_of(inner_blocks + base, RIM), RIM), 0:ROWS] = pieces[k][
+            :, 2 * own_blocks :
+        ].T
 
     def clear(turn, carry):
         acc_near[pl.ds(pl.multiple_of(turn * 48, 8), 48), :] = jnp.zeros((48, LANES), jnp.float32)
@@ -423,20 +433,23 @@
             rows[6 + (axis + 2) % 3] - rows[3 + (axis + 1) % 3] for axis in range(3)
         ]
 
-    inner_tiles = inner_blocks // LANES
-    for half in range(2):
-        for axis, value in enumerate(results_of(half, inner_tiles, 0)):
-            inner_ref[pl.ds(6 * half + axis, inner_tiles, stride=COMPS), :] = value
-        for axis, value in enumerate(results_of(half, 2, inner_tiles)):
-            at = pl.ds(6 * half + axis, 1)
-            edge_in_ref[at, :] = jnp.where(even, value[1:2], value[0:1])
-            edge_over_ref[at, :] = jnp.where(even, value[0:1], value[1:2])
-
-
-def swaps(count):
-    inside = [(i, i ^ 1) for i in range(count)]
-    across = [(i, (i + 1) % count if i % 2 else (i - 1) % count) for i in range(count)]
-    return inside, across
+    own_tiles = own_blocks // LANES
+    own_rows = own_tiles * COMPS
+    edges = [results_of(half, 2, inner_blocks // LANES) for half in range(2)]
+    for k, out in zip(clique_order(piece_count), outs):
+        place = jnp.bitwise_xor(clique, k)
+        for side in range(2):
+            start = (side * piece_count + place) * own_tiles
+            for half in range(2):
+                for axis, value in enumerate(results_of(half, own_tiles, start)):
+                    at = pl.ds(side * own_rows + 6 * half + axis, own_tiles, stride=COMPS)
+                    out[at, :] = value
+        out[pl.ds(2 * own_rows, RIM_ROWS), :] = jnp.zeros((RIM_ROWS, LANES), jnp.float32)
+        for half in range(2):
+            for axis, value in enumerate(edges[half]):
+                rim = jnp.where(place == 0, value[1:2], value[0:1])
+                rim = jnp.where((place == 0) | (place == piece_count - 1), rim, 0.0)
+                out[pl.ds(2 * own_rows + 6 * half + axis, 1), :] = rim
 
 
 def shards(positions, rotations, clump_kind, sub_offsets, pair_blocks, pair_count):
@@ -450,39 +463,40 @@
     slots = pair_blocks.shape[1]
     own_blocks = clumps // 2
     kinds, _, subs = sub_offsets.shape
-    even = group % 2 == 0
-    inside, across = swaps(groups)
     vmem = pl.BlockSpec(memory_space=pltpu.VMEM)
     smem = pl.BlockSpec(memory_space=pltpu.SMEM)
 
-    payload = pl.pallas_call(
+    payload, end = pl.pallas_call(
         functools.partial(payload_kernel, slots, members),
-        out_shape=jax.ShapeDtypeStruct((ROWS, own_blocks), jnp.float32),
+        out_shape=(
+            jax.ShapeDtypeStruct((ROWS, own_blocks), jnp.float32),
+            jax.ShapeDtypeStruct((ROWS, RIM), jnp.float32),
+        ),
         in_specs=[vmem] * 4 + [smem],
-        out_specs=vmem,
+        out_specs=(vmem, vmem),
         name="payload_kernel",
     )(positions, rotations, clump_kind.reshape(-1, LANES), pair_blocks, pair_count)
 
     def trade(value, k):
         return lax.ppermute(value, "dev", [(i, i ^ k) for i in range(members)])
 
-    both = jnp.stack([payload, trade(payload, rings)])
+    def cross(value, step, flip):
+        steps = [
+            (
+                g * members + d,
+                (g + (step if d < rings else -step)) % groups * members + (d ^ flip),
+            )
+            for g in range(groups)
+            for d in range(members)
+        ]
+        return lax.ppermute(value, ("grp", "dev"), steps)
+
+    rim_a, rim_b = cross(end, -1, 0), cross(end, -1, rings)
+    far_payload = trade(payload, rings)
+    rim = jnp.where((clique == 0) == (far == 0), rim_a, rim_b)
+    both = jnp.concatenate([payload, far_payload, rim], 1)
     order = clique_order(rings)
     pieces = [both] + [trade(both, k) for k in order[1:]]
-
-    def piece_columns(member, start):
-        found = None
-        for k, piece in zip(order, pieces):
-            part = piece[:, :, start : start + RIM]
-            part = jnp.where(far == member // rings, part[0], part[1])
-            hit = clique ^ k == member % rings
-            found = part if found is None else jnp.where(hit, part, found)
-        return found
-
-    first = piece_columns(0, 0)
-    last = piece_columns(members - 1, own_blocks - RIM)
-    got_across = lax.ppermute(jnp.where(even, first, last), "grp", across)
-    got_inside = lax.ppermute(jnp.where(even, last, first), "grp", inside)
 
     offset_table = sub_offsets.astype(jnp.float32) * OFFSET_UNIT
     blank = jnp.zeros_like(offset_table)
@@ -499,17 +513,14 @@
 
     inner_blocks = own_blocks * members
     tiles = inner_blocks // LANES
-    inner, edge_in, edge_over = pl.pallas_call(
+    own_rows = own_blocks // LANES * COMPS
+    outs = pl.pallas_call(
         functools.partial(pair_kernel, members, slots),
-        out_shape=(
-            jax.ShapeDtypeStruct((tiles * COMPS, LANES), jnp.float32),
-            jax.ShapeDtypeStruct((COMPS, LANES), jnp.float32),
-            jax.ShapeDtypeStruct((COMPS, LANES), jnp.float32),
-        ),
-        in_specs=[vmem] * (rings + 3),
-        out_specs=(vmem, vmem, vmem),
+        out_shape=(jax.ShapeDtypeStruct((2 * own_rows + RIM_ROWS, LANES), jnp.float32),) * rings,
+        in_specs=[vmem] * (rings + 1),
+        out_specs=(vmem,) * rings,
         scratch_shapes=[
-            pltpu.VMEM((inner_blocks + 2 * RIM, LANES), jnp.float32),
+            pltpu.VMEM((inner_blocks + 3 * RIM, LANES), jnp.float32),
             pltpu.VMEM((members * 2 * slots // LANES, LANES), jnp.float32),
             pltpu.VMEM((2 * slots // LANES, LANES), jnp.int32),
             pltpu.SMEM((2 * slots // LANES, LANES), jnp.int32),
@@ -523,31 +534,21 @@
             pltpu.SemaphoreType.DMA,
         ],
         name="pair_kernel",
-    )(*pieces, got_inside, got_across, offset_rows)
-
-    got_over = lax.ppermute(edge_over, "grp", across)
-    got_in = lax.ppermute(edge_in, "grp", inside)
-    below = jnp.where(group > 0, jnp.where(even, got_over, got_in), 0.0)
-    above = jnp.where(group < groups - 1, jnp.where(even, got_in, got_over), 0.0)
-    inner = inner + jnp.concatenate(
-        [below, jnp.zeros(((tiles - 2) * COMPS, LANES), jnp.float32), above], 0
-    )
-
-    own_rows = tiles * COMPS // members
-    ranks = inner.reshape(2, rings, own_rows, LANES)
-
-    def share(k):
-        return lax.dynamic_index_in_dim(ranks, clique ^ k, 1, False)
-
-    column = share(0)
-    for k in order[:0:-1]:
-        column = column + trade(share(k), k)
-    kept = lax.dynamic_index_in_dim(column, far, 0, False)
-    shares = [kept, trade(lax.dynamic_index_in_dim(column, 1 - far, 0, False), rings)]
+    )(*pieces, offset_rows)
+
+    column = outs[0]
+    for k, out in list(zip(order, outs))[:0:-1]:
+        column = column + trade(out, k)
+    in_low = far == 0
+    low, high = column[:own_rows], column[own_rows : 2 * own_rows]
+    rim = column[2 * own_rows :]
+    rim_a, rim_b = cross(rim, 1, 0), cross(rim, -1, rings)
+    other = trade(jnp.where(in_low, high, low), rings)
+    shares = [jnp.where(in_low, low, high), other, rim_a, rim_b]
     clump_force, clump_torque = pl.pallas_call(
-        finish_kernel,
+        functools.partial(finish_kernel, members, groups),
         out_shape=(jax.ShapeDtypeStruct((3, clumps), jnp.float32),) * 2,
-        in_specs=[vmem] * 3,
+        in_specs=[vmem] * 5,
         out_specs=(vmem, vmem),
         scratch_shapes=[pltpu.VMEM((own_rows, LANES), jnp.float32)],
         name="finish_kernel",

time: 63 us -> 63.4 us (level); the launches traced: 62.8 us -> 62.3 us
  starting transfers between devices: 19 us -> 15.6 us
  waiting for transfers between devices: 14.2 us -> 16.2 us
  Pallas kernels: 24.2 us -> 25.5 us
  local copies, waits for them, and re-layouts: 2.11 us -> 1.43 us
    ppermute x8, starting transfers between devices: 14.2 us -> 9.26 us  [trade(): return lax.ppermute(value, 'dev', [(i, i ^ k) for i in range(members)])]
    ppermute x4, waiting for transfers between devices: 1.81 us -> 5.1 us  [cross(): return lax.ppermute(value, ('grp', 'dev'), steps)]
    ppermute x4, starting transfers between devices: 4.82 us -> 6.33 us  [cross(): return lax.ppermute(value, ('grp', 'dev'), steps)]
    pallas_call x1, Pallas kernels: 21 us -> 22.3 us  [shards(): pl.pallas_call(functools.partial(pair_kernel, members, slots), out_shape=...]
    ppermute x8, waiting for transfers between devices: 12.4 us -> 11.1 us  [trade(): return lax.ppermute(value, 'dev', [(i, i ^ k) for i in range(members)])]
    squeeze x2 -> x0, local copies, waits for them, and re-layouts: 0.65 us -> none  [the longest x1 0.63 us: shards(): lax.dynamic_index_in_dim(column, 1 - far, 0, False)]
  transfers between devices with their start and end apart: 12 -> 12, of which waited for: 11 -> 10; matrix products, arithmetic and copies ran while one was open for 2% -> 1% of each run, Pallas kernels for 0% -> 0%
where the time goes in v3:
time: 63.4 us; the launch traced here: 62.3 us
  Pallas kernels  25.5 us (40%)
  waiting for transfers between devices  16.2 us (26%)
  starting transfers between devices  15.6 us (25%)
  other arithmetic  2.2 us (3%)
  local copies, waits for them, and re-layouts  1.43 us (2%)
  between operations  1.35 us (2%)
    pallas_call x1, Pallas kernels, shards(): pl.pallas_call(functools.partial(pair_kernel, members, slots), out_shape=...  22.3 us
    ppermute x8, waiting for transfers between devices, trade(): return lax.ppermute(value, 'dev', [(i, i ^ k) for i in range(members)])  11.1 us
    ppermute x8, starting transfers between devices, trade(): return lax.ppermute(value, 'dev', [(i, i ^ k) for i in range(members)])  9.26 us
    ppermute x4, starting transfers between devices, cross(): return lax.ppermute(value, ('grp', 'dev'), steps)  6.33 us
    ppermute x4, waiting for transfers between devices, cross(): return lax.ppermute(value, ('grp', 'dev'), steps)  5.1 us
    pallas_call x1, Pallas kernels, shards(): pl.pallas_call(functools.partial(payload_kernel, slots, members), out_sha...  1.67 us
    pallas_call x1, Pallas kernels, shards(): pl.pallas_call(functools.partial(finish_kernel, members, groups), out_sha...  1.57 us
  transfers between devices with their start and end apart: 12, of which 10 were waited for; matrix products, arithmetic and copies ran while one was open for 1% of the time, Pallas kernels for 0%

profile of v3, /device:TPU:0, one launch (start us, length us, event | category | flops | bytes accessed | tf_op | source)
XLA Modules:
  0.0 62.3 jit_solution(904767583776549946)
XLA Ops:
  1.3 0.0 copy-start.6
  1.3 1.7 %payload_kernel.1 = (f32[24,512]{1,0:T(8,128)}, f32[24,128]{1,0:T(8,128)}) custom-call(f32[3,1024]{1,0:T(4,128)} %refs_3_.1, f32[9,1024]{1,0:T(8,128)} %rotation_ref.1, s32[8,128]{1,0:T(8,128)} %bitcast.5, s32[2,1024]{1,0:T(2,128)} %pair_ref.1, s32[1]{0:T(128)S(6)} %copy.8.count_ref), custom_call_target="tpu_custom_call" | custom-call | tf_op jit(solution)/shard_map/payload_kernel/pallas_call | solution.py:469
  3.0 4.4 %collective-permute-start.2 = (f32[24,128]{1,0:T(8,128)}, f32[24,128]{1,0:T(8,128)S(1)}, u32[]{:S(2)}, u32[]{:S(2)}) collective-permute-start(f32[24,128]{1,0:T(8,128)} %get-tuple-element.9), channel_id=1, source_target_pairs={{0,28},{1,29},{2,30},{3,31},{4,8},{5,9},{6,10},{7,11},{8,4},{9,5},... | collective-permute-start | bytes 36872 | tf_op jit(solution)/shard_map/ppermute | solution.py:492
  7.4 0.8 %collective-permute-start.1 = (f32[24,128]{1,0:T(8,128)}, f32[24,128]{1,0:T(8,128)S(1)}, u32[]{:S(2)}, u32[]{:S(2)}) collective-permute-start(f32[24,128]{1,0:T(8,128)} %get-tuple-element.9), channel_id=1, source_target_pairs={{0,24},{1,25},{2,26},{3,27},{4,12},{5,13},{6,14},{7,15},{8,0},{9,1... | collective-permute-start | bytes 36872 | tf_op jit(solution)/shard_map/ppermute | solution.py:492
  8.2 0.2 collective-permute-start
  8.4 0.0 copy-done.6
  8.4 0.1 pad_bitcast_fusion.1
  8.5 0.0 copy-start.4
  8.5 0.1 pad.6.clone
  8.6 0.4 collective-permute-done.2
  9.0 0.8 %collective-permute-done.1 = f32[24,128]{1,0:T(8,128)S(1)} collective-permute-done((f32[24,128]{1,0:T(8,128)}, f32[24,128]{1,0:T(8,128)S(1)}, u32[]{:S(2)}, u32[]{:S(2)}) %collective-permute-start.1) | collective-permute-done | bytes 12320 | tf_op jit(solution)/shard_map/ppermute | solution.py:492
  9.9 3.8 %collective-permute-done = f32[24,512]{1,0:T(8,128)S(1)} collective-permute-done((f32[24,512]{1,0:T(8,128)}, f32[24,512]{1,0:T(8,128)S(1)}, u32[]{:S(2)}, u32[]{:S(2)}) %collective-permute-start) | collective-permute-done | bytes 49184 | tf_op jit(solution)/shard_map/ppermute | solution.py:481
  13.7 0.0 copy-done.4
  13.7 0.0 copy-start
  13.7 1.4 %collective-permute-start.5 = (f32[24,1152]{1,0:T(8,128)S(1)}, f32[24,1152]{1,0:T(8,128)S(1)}, u32[]{:S(2)}, u32[]{:S(2)}) collective-permute-start(f32[24,1152]{1,0:T(8,128)S(1)} %pad_maximum_fusion.refs_0_), channel_id=1, source_target_pairs={{0,2},{1,3},{2,0},{3,1},{4,6},{5,7},{6,4},{7,5},{8,10},{9,11},{10,... | collective-permute-start | bytes 331784 | tf_op jit(solution)/shard_map/ppermute | solution.py:481
  15.1 1.5 %collective-permute-start.4 = (f32[24,1152]{1,0:T(8,128)S(1)}, f32[24,1152]{1,0:T(8,128)S(1)}, u32[]{:S(2)}, u32[]{:S(2)}) collective-permute-start(f32[24,1152]{1,0:T(8,128)S(1)} %pad_maximum_fusion.refs_0_), channel_id=1, source_target_pairs={{0,1},{1,0},{2,3},{3,2},{4,5},{5,4},{6,7},{7,6},{8,9},{9,8},{10,11... | collective-permute-start | bytes 331784 | tf_op jit(solution)/shard_map/ppermute | solution.py:481
  16.6 0.6 %collective-permute-start.3 = (f32[24,1152]{1,0:T(8,128)S(1)}, f32[24,1152]{1,0:T(8,128)S(1)}, u32[]{:S(2)}, u32[]{:S(2)}) collective-permute-start(f32[24,1152]{1,0:T(8,128)S(1)} %pad_maximum_fusion.refs_0_), channel_id=1, source_target_pairs={{0,3},{1,2},{2,1},{3,0},{4,7},{5,6},{6,5},{7,4},{8,11},{9,10},{10,... | collective-permute-start | bytes 331784 | tf_op jit(solution)/shard_map/ppermute | solution.py:481
  17.2 0.7 %maximum_maximum_fusion.refs_4_ = bf16[128,384]{1,0:T(8,128)(2,1)} fusion(bf16[8,384]{1,0:T(8,128)(2,1)S(1)} %get-tuple-element.17, bf16[8,384]{1,0:T(8,128)(2,1)S(1)} %get-tuple-element.16, bf16[128]{0:T(256)(128)(2,1)S(1)} %pad.6.clone), kind=kLoop, calls=%fused_computation.1 | loop fusion | flops 294912 | bytes 110848 | tf_op jit(solution)/shard_map/concatenate | solution.py:510
  18.0 1.5 %collective-permute-done.5.refs_3_ = f32[24,1152]{1,0:T(8,128)S(1)} collective-permute-done((f32[24,1152]{1,0:T(8,128)S(1)}, f32[24,1152]{1,0:T(8,128)S(1)}, u32[]{:S(2)}, u32[]{:S(2)}) %collective-permute-start.5) | collective-permute-done | bytes 110624 | tf_op jit(solution)/shard_map/ppermute | solution.py:481
  19.5 0.0 copy-start.1
  19.5 1.1 %collective-permute-done.4.refs_2_ = f32[24,1152]{1,0:T(8,128)S(1)} collective-permute-done((f32[24,1152]{1,0:T(8,128)S(1)}, f32[24,1152]{1,0:T(8,128)S(1)}, u32[]{:S(2)}, u32[]{:S(2)}) %collective-permute-start.4) | collective-permute-done | bytes 110624 | tf_op jit(solution)/shard_map/ppermute | solution.py:481
  20.7 0.0 copy-start.2
  20.7 1.6 %collective-permute-done.3.refs_1_ = f32[24,1152]{1,0:T(8,128)S(1)} collective-permute-done((f32[24,1152]{1,0:T(8,128)S(1)}, f32[24,1152]{1,0:T(8,128)S(1)}, u32[]{:S(2)}, u32[]{:S(2)}) %collective-permute-start.3) | collective-permute-done | bytes 110624 | tf_op jit(solution)/shard_map/ppermute | solution.py:481
  22.3 0.0 copy-done
  22.3 0.0 copy-done.1
  22.3 0.0 copy-done.2
  22.3 0.0 copy-start.3
  22.3 0.6 %copy-done.3 = f32[24,1152]{1,0:T(8,128)} copy-done((f32[24,1152]{1,0:T(8,128)}, f32[24,1152]{1,0:T(8,128)S(1)}, u32[]{:S(2)}) %copy-start.3) | copy-done | bytes 110616
  22.9 22.3 %pair_kernel.1 = (f32[112,128]{1,0:T(8,128)}, f32[112,128]{1,0:T(8,128)}, f32[112,128]{1,0:T(8,128)}, f32[112,128]{1,0:T(8,128)}) custom-call(f32[24,1152]{1,0:T(8,128)} %copy-done, f32[24,1152]{1,0:T(8,128)} %copy-done.3, f32[24,1152]{1,0:T(8,128)} %copy-done.2, f32[24,1152]{1,0:T(8,128)} %copy-done.1, bf16[128,384]{1,0:T(8,128)(2,1)} %maximum_maximum_fusion.refs_4_), custom_call_target="tpu_custom_call" | custom-call | tf_op jit(solution)/shard_map/pair_kernel/pallas_call | solution.py:517
  45.2 0.7 %collective-permute-start.6 = (f32[112,128]{1,0:T(8,128)}, f32[112,128]{1,0:T(8,128)S(1)}, u32[]{:S(2)}, u32[]{:S(2)}) collective-permute-start(f32[112,128]{1,0:T(8,128)} %get-tuple-element.11), channel_id=1, source_target_pairs={{0,2},{1,3},{2,0},{3,1},{4,6},{5,7},{6,4},{7,5},{8,10},{9,11},{10,... | collective-permute-start | bytes 172040 | tf_op jit(solution)/shard_map/ppermute | solution.py:481
  45.9 0.6 collective-permute-start.7
  46.5 2.3 %collective-permute-start.8 = (f32[112,128]{1,0:T(8,128)}, f32[112,128]{1,0:T(8,128)S(1)}, u32[]{:S(2)}, u32[]{:S(2)}) collective-permute-start(f32[112,128]{1,0:T(8,128)} %get-tuple-element.13), channel_id=1, source_target_pairs={{0,3},{1,2},{2,1},{3,0},{4,7},{5,6},{6,5},{7,4},{8,11},{9,10},{10,... | collective-permute-start | bytes 172040 | tf_op jit(solution)/shard_map/ppermute | solution.py:481
  48.8 0.9 %collective-permute-done.6 = f32[112,128]{1,0:T(8,128)S(1)} collective-permute-done((f32[112,128]{1,0:T(8,128)}, f32[112,128]{1,0:T(8,128)S(1)}, u32[]{:S(2)}, u32[]{:S(2)}) %collective-permute-start.6) | collective-permute-done | bytes 57376 | tf_op jit(solution)/shard_map/ppermute | solution.py:481
  49.7 0.7 %collective-permute-done.7 = f32[112,128]{1,0:T(8,128)S(1)} collective-permute-done((f32[112,128]{1,0:T(8,128)}, f32[112,128]{1,0:T(8,128)S(1)}, u32[]{:S(2)}, u32[]{:S(2)}) %collective-permute-start.7) | collective-permute-done | bytes 57376 | tf_op jit(solution)/shard_map/ppermute | solution.py:481
  50.3 1.5 %collective-permute-done.8 = f32[112,128]{1,0:T(8,128)S(1)} collective-permute-done((f32[112,128]{1,0:T(8,128)}, f32[112,128]{1,0:T(8,128)S(1)}, u32[]{:S(2)}, u32[]{:S(2)}) %collective-permute-start.8) | collective-permute-done | bytes 57376 | tf_op jit(solution)/shard_map/ppermute | solution.py:481
  51.8 0.8 %add_add_fusion = f32[112,128]{1,0:T(8,128)S(1)} fusion(f32[112,128]{1,0:T(8,128)S(1)} %collective-permute-done.8, f32[112,128]{1,0:T(8,128)S(1)} %collective-permute-done.7, f32[112,128]{1,0:T(8,128)} %get-tuple-element.10, f32[112,128]{1,0:T(8,128)S(1)} %collective-permute-done.6), kind=kLoop, calls=%fused_computation.2 | loop fusion | flops 43008 | bytes 286720 | tf_op jit(solution)/shard_map/add | solution.py:541
  52.6 0.6 %slice_select_fusion = (f32[48,128]{1,0:T(8,128)S(1)}, f32[48,128]{1,0:T(8,128)}) fusion(f32[112,128]{1,0:T(8,128)S(1)} %add_add_fusion, pred[]{:T(512)S(6)} %eq.12), kind=kLoop, calls=%fused_computation.3 | loop fusion | flops 12288 | bytes 98305 | tf_op jit(solution)/shard_map/jit(_where)/select_n | solution.py:546
  53.3 2.0 %collective-permute-start.9 = (f32[48,128]{1,0:T(8,128)S(1)}, f32[48,128]{1,0:T(8,128)S(1)}, u32[]{:S(2)}, u32[]{:S(2)}) collective-permute-start(f32[48,128]{1,0:T(8,128)S(1)} %get-tuple-element.14), channel_id=1, source_target_pairs={{0,4},{1,5},{2,6},{3,7},{4,0},{5,1},{6,2},{7,3},{8,12},{9,13},{10,... | collective-permute-start | bytes 73736 | tf_op jit(solution)/shard_map/ppermute | solution.py:481
  55.3 0.0 collective-permute-start.11
  55.3 1.1 %collective-permute-start.10 = (f32[16,128]{1,0:T(8,128)S(1)}, f32[16,128]{1,0:T(8,128)S(1)}, u32[]{:S(2)}, u32[]{:S(2)}) collective-permute-start(f32[16,128]{1,0:T(8,128)S(1)} %slice.14), channel_id=1, source_target_pairs={{0,8},{1,9},{2,10},{3,11},{4,28},{5,29},{6,30},{7,31},{8,16},{9,17... | collective-permute-start | bytes 24584 | tf_op jit(solution)/shard_map/ppermute | solution.py:492
  56.3 3.8 %collective-permute-done.11.refs_2_ = f32[16,128]{1,0:T(8,128)S(1)} collective-permute-done((f32[16,128]{1,0:T(8,128)S(1)}, f32[16,128]{1,0:T(8,128)S(1)}, u32[]{:S(2)}, u32[]{:S(2)}) %collective-permute-start.11) | collective-permute-done | bytes 8224 | tf_op jit(solution)/shard_map/ppermute | solution.py:492
  60.1 0.0 copy-start.7
  60.1 0.0 collective-permute-done.10.refs_1_
  60.1 0.0 copy-start.8
  60.1 0.0 collective-permute-done.9.refs_0_
  60.1 0.0 copy-start.5
  60.2 0.6 copy-done.7
  60.7 0.0 copy-done.8
  60.7 0.0 copy-done.5
  60.8 1.6 %finish_kernel.1 = (f32[3,1024]{1,0:T(4,128)}, f32[3,1024]{1,0:T(4,128)}) custom-call(f32[48,128]{1,0:T(8,128)} %get-tuple-element.15.own_ref, f32[48,128]{1,0:T(8,128)} %copy-done.5, f32[16,128]{1,0:T(8,128)} %copy-done.8, f32[16,128]{1,0:T(8,128)} %copy-done.7, f32[3,1024]{1,0:T(4,128)} %refs_3_.1), custom_call_target="tpu_custom_call" | custom-call | tf_op jit(solution)/shard_map/finish_kernel/pallas_call | solution.py:548
  (5 shorter events, 0.0 us)
Async XLA Ops:
  1.3 7.1 %copy-start.6 = (s32[8,3,64]{2,0,1:T(8,128)S(1)}, s32[8,3,64]{2,0,1:T(8,128)}, u32[]{:S(2)}) copy-start(s32[8,3,64]{2,0,1:T(8,128)} %param.9) | copy-start | bytes 18436
  3.0 6.0 %collective-permute-start.2 = (f32[24,128]{1,0:T(8,128)}, f32[24,128]{1,0:T(8,128)S(1)}, u32[]{:S(2)}, u32[]{:S(2)}) collective-permute-start(f32[24,128]{1,0:T(8,128)} %get-tuple-element.9), channel_id=1, source_target_pairs={{0,28},{1,29},{2,30},{3,31},{4,8},{5,9},{6,10},{7,11},{8,4},{9,5},... | collective-permute-start | bytes 36872 | tf_op jit(solution)/shard_map/ppermute | solution.py:492
  7.4 2.5 %collective-permute-start.1 = (f32[24,128]{1,0:T(8,128)}, f32[24,128]{1,0:T(8,128)S(1)}, u32[]{:S(2)}, u32[]{:S(2)}) collective-permute-start(f32[24,128]{1,0:T(8,128)} %get-tuple-element.9), channel_id=1, source_target_pairs={{0,24},{1,25},{2,26},{3,27},{4,12},{5,13},{6,14},{7,15},{8,0},{9,1... | collective-permute-start | bytes 36872 | tf_op jit(solution)/shard_map/ppermute | solution.py:492
  8.2 5.4 %collective-permute-start = (f32[24,512]{1,0:T(8,128)}, f32[24,512]{1,0:T(8,128)S(1)}, u32[]{:S(2)}, u32[]{:S(2)}) collective-permute-start(f32[24,512]{1,0:T(8,128)} %get-tuple-element.8), channel_id=1, source_target_pairs={{0,4},{1,5},{2,6},{3,7},{4,0},{5,1},{6,2},{7,3},{8,12},{9,13},{10,... | collective-permute-start | bytes 147464 | tf_op jit(solution)/shard_map/ppermute | solution.py:481
  8.5 5.2 %copy-start.4 = (f32[24,512]{1,0:T(8,128)S(1)}, f32[24,512]{1,0:T(8,128)}, u32[]{:S(2)}) copy-start(f32[24,512]{1,0:T(8,128)} %get-tuple-element.8) | copy-start | bytes 147460
  13.7 8.6 %copy-start = (f32[24,1152]{1,0:T(8,128)}, f32[24,1152]{1,0:T(8,128)S(1)}, u32[]{:S(2)}) copy-start(f32[24,1152]{1,0:T(8,128)S(1)} %pad_maximum_fusion.refs_0_) | copy-start | bytes 331780
  13.7 5.8 %collective-permute-start.5 = (f32[24,1152]{1,0:T(8,128)S(1)}, f32[24,1152]{1,0:T(8,128)S(1)}, u32[]{:S(2)}, u32[]{:S(2)}) collective-permute-start(f32[24,1152]{1,0:T(8,128)S(1)} %pad_maximum_fusion.refs_0_), channel_id=1, source_target_pairs={{0,2},{1,3},{2,0},{3,1},{4,6},{5,7},{6,4},{7,5},{8,10},{9,11},{10,... | collective-permute-start | bytes 331784 | tf_op jit(solution)/shard_map/ppermute | solution.py:481
  15.1 5.6 %collective-permute-start.4 = (f32[24,1152]{1,0:T(8,128)S(1)}, f32[24,1152]{1,0:T(8,128)S(1)}, u32[]{:S(2)}, u32[]{:S(2)}) collective-permute-start(f32[24,1152]{1,0:T(8,128)S(1)} %pad_maximum_fusion.refs_0_), channel_id=1, source_target_pairs={{0,1},{1,0},{2,3},{3,2},{4,5},{5,4},{6,7},{7,6},{8,9},{9,8},{10,11... | collective-permute-start | bytes 331784 | tf_op jit(solution)/shard_map/ppermute | solution.py:481
  16.6 5.6 %collective-permute-start.3 = (f32[24,1152]{1,0:T(8,128)S(1)}, f32[24,1152]{1,0:T(8,128)S(1)}, u32[]{:S(2)}, u32[]{:S(2)}) collective-permute-start(f32[24,1152]{1,0:T(8,128)S(1)} %pad_maximum_fusion.refs_0_), channel_id=1, source_target_pairs={{0,3},{1,2},{2,1},{3,0},{4,7},{5,6},{6,5},{7,4},{8,11},{9,10},{10,... | collective-permute-start | bytes 331784 | tf_op jit(solution)/shard_map/ppermute | solution.py:481
  19.5 2.8 %copy-start.1 = (f32[24,1152]{1,0:T(8,128)}, f32[24,1152]{1,0:T(8,128)S(1)}, u32[]{:S(2)}) copy-start(f32[24,1152]{1,0:T(8,128)S(1)} %collective-permute-done.5.refs_3_) | copy-start | bytes 331780
  20.7 1.6 %copy-start.2 = (f32[24,1152]{1,0:T(8,128)}, f32[24,1152]{1,0:T(8,128)S(1)}, u32[]{:S(2)}) copy-start(f32[24,1152]{1,0:T(8,128)S(1)} %collective-permute-done.4.refs_2_) | copy-start | bytes 331780
  22.3 0.6 %copy-start.3 = (f32[24,1152]{1,0:T(8,128)}, f32[24,1152]{1,0:T(8,128)S(1)}, u32[]{:S(2)}) copy-start(f32[24,1152]{1,0:T(8,128)S(1)} %collective-permute-done.3.refs_1_) | copy-start | bytes 331780
  45.2 4.5 %collective-permute-start.6 = (f32[112,128]{1,0:T(8,128)}, f32[112,128]{1,0:T(8,128)S(1)}, u32[]{:S(2)}, u32[]{:S(2)}) collective-permute-start(f32[112,128]{1,0:T(8,128)} %get-tuple-element.11), channel_id=1, source_target_pairs={{0,2},{1,3},{2,0},{3,1},{4,6},{5,7},{6,4},{7,5},{8,10},{9,11},{10,... | collective-permute-start | bytes 172040 | tf_op jit(solution)/shard_map/ppermute | solution.py:481
  45.9 4.4 %collective-permute-start.7 = (f32[112,128]{1,0:T(8,128)}, f32[112,128]{1,0:T(8,128)S(1)}, u32[]{:S(2)}, u32[]{:S(2)}) collective-permute-start(f32[112,128]{1,0:T(8,128)} %get-tuple-element.12), channel_id=1, source_target_pairs={{0,1},{1,0},{2,3},{3,2},{4,5},{5,4},{6,7},{7,6},{8,9},{9,8},{10,11... | collective-permute-start | bytes 172040 | tf_op jit(solution)/shard_map/ppermute | solution.py:481
  46.5 5.3 %collective-permute-start.8 = (f32[112,128]{1,0:T(8,128)}, f32[112,128]{1,0:T(8,128)S(1)}, u32[]{:S(2)}, u32[]{:S(2)}) collective-permute-start(f32[112,128]{1,0:T(8,128)} %get-tuple-element.13), channel_id=1, source_target_pairs={{0,3},{1,2},{2,1},{3,0},{4,7},{5,6},{6,5},{7,4},{8,11},{9,10},{10,... | collective-permute-start | bytes 172040 | tf_op jit(solution)/shard_map/ppermute | solution.py:481
  53.3 6.9 %collective-permute-start.9 = (f32[48,128]{1,0:T(8,128)S(1)}, f32[48,128]{1,0:T(8,128)S(1)}, u32[]{:S(2)}, u32[]{:S(2)}) collective-permute-start(f32[48,128]{1,0:T(8,128)S(1)} %get-tuple-element.14), channel_id=1, source_target_pairs={{0,4},{1,5},{2,6},{3,7},{4,0},{5,1},{6,2},{7,3},{8,12},{9,13},{10,... | collective-permute-start | bytes 73736 | tf_op jit(solution)/shard_map/ppermute | solution.py:481
  55.3 4.9 %collective-permute-start.11 = (f32[16,128]{1,0:T(8,128)S(1)}, f32[16,128]{1,0:T(8,128)S(1)}, u32[]{:S(2)}, u32[]{:S(2)}) collective-permute-start(f32[16,128]{1,0:T(8,128)S(1)} %slice.14), channel_id=1, source_target_pairs={{0,28},{1,29},{2,30},{3,31},{4,8},{5,9},{6,10},{7,11},{8,4},{9,5},... | collective-permute-start | bytes 24584 | tf_op jit(solution)/shard_map/ppermute | solution.py:492
  55.3 4.9 %collective-permute-start.10 = (f32[16,128]{1,0:T(8,128)S(1)}, f32[16,128]{1,0:T(8,128)S(1)}, u32[]{:S(2)}, u32[]{:S(2)}) collective-permute-start(f32[16,128]{1,0:T(8,128)S(1)} %slice.14), channel_id=1, source_target_pairs={{0,8},{1,9},{2,10},{3,11},{4,28},{5,29},{6,30},{7,31},{8,16},{9,17... | collective-permute-start | bytes 24584 | tf_op jit(solution)/shard_map/ppermute | solution.py:492
  60.1 0.6 copy-start.7
  60.1 0.6 copy-start.8
  60.1 0.6 copy-start.5

commit v4 on v3

--- a/solution.py
+++ b/solution.py
@@ -31,7 +31,17 @@
     return [0, count - 1] + list(range(1, count - 1))
 
 
-def payload_kernel(slots, members, position_ref, rotation_ref, kind_ref, pair_ref, count_ref, out_ref, end_ref):
+def payload_kernel(slots, members, *refs):
+    sources, (count_ref, out_ref, end_ref), landed, sems = refs[:4], refs[4:7], refs[7:11], refs[11]
+    copies = [
+        pltpu.make_async_copy(source, target, sems.at[turn])
+        for turn, (source, target) in enumerate(zip(sources, landed))
+    ]
+    for copy in copies:
+        copy.start()
+    for copy in copies:
+        copy.wait()
+    position_ref, rotation_ref, kind_ref, pair_ref = landed
     clumps = position_ref.shape[1]
     blocks = clumps // 2
     inner_blocks = blocks * members
@@ -472,8 +482,16 @@
             jax.ShapeDtypeStruct((ROWS, own_blocks), jnp.float32),
             jax.ShapeDtypeStruct((ROWS, RIM), jnp.float32),
         ),
-        in_specs=[vmem] * 4 + [smem],
+        in_specs=[pl.BlockSpec(memory_space=pltpu.HBM)] * 4 + [smem],
         out_specs=(vmem, vmem),
+        scratch_shapes=[
+            pltpu.VMEM((3, clumps), jnp.float32),
+            pltpu.VMEM((9, clumps), jnp.float32),
+            pltpu.VMEM((clumps // LANES, LANES), jnp.int32),
+            pltpu.VMEM((2, slots), jnp.int32),
+            pltpu.SemaphoreType.DMA((4,)),
+        ],
+        compiler_params=pltpu.CompilerParams(vmem_limit_bytes=4 << 20),
         name="payload_kernel",
     )(positions, rotations, clump_kind.reshape(-1, LANES), pair_blocks, pair_count)
 
@@ -533,6 +551,7 @@
             pltpu.VMEM(((tiles + 2) * 48, LANES), jnp.float32),
             pltpu.SemaphoreType.DMA,
         ],
+        compiler_params=pltpu.CompilerParams(vmem_limit_bytes=32 << 20),
         name="pair_kernel",
     )(*pieces, offset_rows)
 
@@ -551,6 +570,7 @@
         in_specs=[vmem] * 5,
         out_specs=(vmem, vmem),
         scratch_shapes=[pltpu.VMEM((own_rows, LANES), jnp.float32)],
+        compiler_params=pltpu.CompilerParams(vmem_limit_bytes=4 << 20),
         name="finish_kernel",
     )(*shares, positions)
     return (clump_force, clump_torque)

time: 63.4 us -> 55.6 us (0.88); the launches traced: 62.3 us -> 55.9 us
  Pallas kernels: 25.5 us -> 19.7 us
  other arithmetic: 2.2 us -> 0.12 us
  local copies, waits for them, and re-layouts: 1.43 us -> 3.1 us
    pallas_call x1, Pallas kernels: 22.3 us -> 18.6 us  [shards(): pl.pallas_call(functools.partial(pair_kernel, members, slots), out_shape=...]
    unnamed x18 -> x12, local copies, waits for them, and re-layouts: 1.27 us -> 2.94 us
    pallas_call x1, Pallas kernels: 1.67 us -> 0.34 us  [shards(): pl.pallas_call(functools.partial(payload_kernel, slots, members), out_sha...]
    add x1, other arithmetic: 0.84 us -> 0.02 us  [shards(): column = column + trade(out, k)]
    pallas_call x1, Pallas kernels: 1.57 us -> 0.79 us  [shards(): pl.pallas_call(functools.partial(finish_kernel, members, groups), out_sha...]
    ppermute x4, waiting for transfers between devices: 5.1 us -> 4.39 us  [cross(): return lax.ppermute(value, ('grp', 'dev'), steps)]
    concatenate x1, other arithmetic: 0.72 us -> 0.08 us  [shards(): jnp.concatenate([offset_rows, jnp.zeros((LANES - 2 * kinds, offset_rows.s...]
  transfers between devices with their start and end apart: 12 -> 12, of which waited for: 10 -> 10; matrix products, arithmetic and copies ran while one was open for 1% -> 0% of each run, Pallas kernels for 0% -> 0%
where the time goes in v4:
time: 55.6 us; the launch traced here: 55.9 us
  Pallas kernels  19.7 us (35%)
  waiting for transfers between devices  15.9 us (29%)
  starting transfers between devices  15.7 us (28%)
  local copies, waits for them, and re-layouts  3.1 us (6%)
  between operations  1.35 us (2%)
    pallas_call x1, Pallas kernels, shards(): pl.pallas_call(functools.partial(pair_kernel, members, slots), out_shape=...  18.6 us
    ppermute x8, waiting for transfers between devices, trade(): return lax.ppermute(value, 'dev', [(i, i ^ k) for i in range(members)])  11.5 us
    ppermute x8, starting transfers between devices, trade(): return lax.ppermute(value, 'dev', [(i, i ^ k) for i in range(members)])  8.83 us
    ppermute x4, starting transfers between devices, cross(): return lax.ppermute(value, ('grp', 'dev'), steps)  6.89 us
    ppermute x4, waiting for transfers between devices, cross(): return lax.ppermute(value, ('grp', 'dev'), steps)  4.39 us
    unnamed x12, local copies, waits for them, and re-layouts  2.94 us
  transfers between devices with their start and end apart: 12, of which 10 were waited for; matrix products, arithmetic and copies ran while one was open for 0% of the time, Pallas kernels for 0%

profile of v4, /device:TPU:0, one launch (start us, length us, event | category | flops | bytes accessed | tf_op | source)
XLA Modules:
  0.0 55.9 jit_solution(16097717592917833341)
XLA Ops:
  1.3 0.0 copy-start
  1.3 0.8 %copy-done = f32[9,1024]{1,0:T(8,128)S(1)} copy-done((f32[9,1024]{1,0:T(8,128)S(1)}, f32[9,1024]{1,0:T(8,128)}, u32[]{:S(2)}) %copy-start) | copy-done | bytes 36888
  2.1 0.0 copy-start.1
  2.1 0.7 %copy-done.1 = f32[3,1024]{1,0:T(4,128)S(1)} copy-done((f32[3,1024]{1,0:T(4,128)S(1)}, f32[3,1024]{1,0:T(4,128)}, u32[]{:S(2)}) %copy-start.1) | copy-done | bytes 12312
  2.8 0.0 copy-start.3
  2.8 0.7 %copy-done.3 = s32[2,1024]{1,0:T(2,128)S(1)} copy-done((s32[2,1024]{1,0:T(2,128)S(1)}, s32[2,1024]{1,0:T(2,128)}, u32[]{:S(2)}) %copy-start.3) | copy-done | bytes 8216
  3.5 0.0 copy-start.4
  3.5 0.7 %copy-done.4 = s32[1024]{0:T(1024)S(1)} copy-done((s32[1024]{0:T(1024)S(1)}, s32[1024]{0:T(1024)}, u32[]{:S(2)}) %copy-start.4) | copy-done | bytes 4120
  4.2 0.0 copy-start.5
  4.2 0.3 payload_kernel.1
  4.6 4.5 %collective-permute-start.2 = (f32[24,128]{1,0:T(8,128)S(1)}, f32[24,128]{1,0:T(8,128)S(1)}, u32[]{:S(2)}, u32[]{:S(2)}) collective-permute-start(f32[24,128]{1,0:T(8,128)S(1)} %get-tuple-element.9), channel_id=1, source_target_pairs={{0,28},{1,29},{2,30},{3,31},{4,8},{5,9},{6,10},{7,11},{8,4},{9,5},... | collective-permute-start | bytes 36872 | tf_op jit(solution)/shard_map/ppermute | solution.py:510
  9.1 0.8 %collective-permute-start.1 = (f32[24,128]{1,0:T(8,128)S(1)}, f32[24,128]{1,0:T(8,128)S(1)}, u32[]{:S(2)}, u32[]{:S(2)}) collective-permute-start(f32[24,128]{1,0:T(8,128)S(1)} %get-tuple-element.9), channel_id=1, source_target_pairs={{0,24},{1,25},{2,26},{3,27},{4,12},{5,13},{6,14},{7,15},{8,0},{9,1... | collective-permute-start | bytes 36872 | tf_op jit(solution)/shard_map/ppermute | solution.py:510
  9.9 0.2 collective-permute-start
  10.1 0.0 copy-done.5
  10.1 0.1 pad_bitcast_fusion.1
  10.2 0.1 pad.6.clone
  10.3 0.2 collective-permute-done.2
  10.5 0.8 %collective-permute-done.1 = f32[24,128]{1,0:T(8,128)S(1)} collective-permute-done((f32[24,128]{1,0:T(8,128)S(1)}, f32[24,128]{1,0:T(8,128)S(1)}, u32[]{:S(2)}, u32[]{:S(2)}) %collective-permute-start.1) | collective-permute-done | bytes 12320 | tf_op jit(solution)/shard_map/ppermute | solution.py:510
  11.3 3.8 %collective-permute-done = f32[24,512]{1,0:T(8,128)S(1)} collective-permute-done((f32[24,512]{1,0:T(8,128)S(1)}, f32[24,512]{1,0:T(8,128)S(1)}, u32[]{:S(2)}, u32[]{:S(2)}) %collective-permute-start) | collective-permute-done | bytes 49184 | tf_op jit(solution)/shard_map/ppermute | solution.py:499
  15.2 1.4 %collective-permute-start.5 = (f32[24,1152]{1,0:T(8,128)S(1)}, f32[24,1152]{1,0:T(8,128)S(1)}, u32[]{:S(2)}, u32[]{:S(2)}) collective-permute-start(f32[24,1152]{1,0:T(8,128)S(1)} %pad_maximum_fusion.refs_0_), channel_id=1, source_target_pairs={{0,2},{1,3},{2,0},{3,1},{4,6},{5,7},{6,4},{7,5},{8,10},{9,11},{10,... | collective-permute-start | bytes 331784 | tf_op jit(solution)/shard_map/ppermute | solution.py:499
  16.6 1.5 %collective-permute-start.4 = (f32[24,1152]{1,0:T(8,128)S(1)}, f32[24,1152]{1,0:T(8,128)S(1)}, u32[]{:S(2)}, u32[]{:S(2)}) collective-permute-start(f32[24,1152]{1,0:T(8,128)S(1)} %pad_maximum_fusion.refs_0_), channel_id=1, source_target_pairs={{0,1},{1,0},{2,3},{3,2},{4,5},{5,4},{6,7},{7,6},{8,9},{9,8},{10,11... | collective-permute-start | bytes 331784 | tf_op jit(solution)/shard_map/ppermute | solution.py:499
  18.1 0.6 %collective-permute-start.3 = (f32[24,1152]{1,0:T(8,128)S(1)}, f32[24,1152]{1,0:T(8,128)S(1)}, u32[]{:S(2)}, u32[]{:S(2)}) collective-permute-start(f32[24,1152]{1,0:T(8,128)S(1)} %pad_maximum_fusion.refs_0_), channel_id=1, source_target_pairs={{0,3},{1,2},{2,1},{3,0},{4,7},{5,6},{6,5},{7,4},{8,11},{9,10},{10,... | collective-permute-start | bytes 331784 | tf_op jit(solution)/shard_map/ppermute | solution.py:499
  18.7 0.1 maximum_maximum_fusion.refs_4_
  18.8 2.2 %collective-permute-done.5.refs_3_ = f32[24,1152]{1,0:T(8,128)S(1)} collective-permute-done((f32[24,1152]{1,0:T(8,128)S(1)}, f32[24,1152]{1,0:T(8,128)S(1)}, u32[]{:S(2)}, u32[]{:S(2)}) %collective-permute-start.5) | collective-permute-done | bytes 110624 | tf_op jit(solution)/shard_map/ppermute | solution.py:499
  21.0 1.1 %collective-permute-done.4.refs_2_ = f32[24,1152]{1,0:T(8,128)S(1)} collective-permute-done((f32[24,1152]{1,0:T(8,128)S(1)}, f32[24,1152]{1,0:T(8,128)S(1)}, u32[]{:S(2)}, u32[]{:S(2)}) %collective-permute-start.4) | collective-permute-done | bytes 110624 | tf_op jit(solution)/shard_map/ppermute | solution.py:499
  22.1 1.6 %collective-permute-done.3.refs_1_ = f32[24,1152]{1,0:T(8,128)S(1)} collective-permute-done((f32[24,1152]{1,0:T(8,128)S(1)}, f32[24,1152]{1,0:T(8,128)S(1)}, u32[]{:S(2)}, u32[]{:S(2)}) %collective-permute-start.3) | collective-permute-done | bytes 110624 | tf_op jit(solution)/shard_map/ppermute | solution.py:499
  23.7 18.6 %pair_kernel.1 = (f32[112,128]{1,0:T(8,128)S(1)}, f32[112,128]{1,0:T(8,128)S(1)}, f32[112,128]{1,0:T(8,128)S(1)}, f32[112,128]{1,0:T(8,128)S(1)}) custom-call(f32[24,1152]{1,0:T(8,128)S(1)} %pad_maximum_fusion.refs_0_, f32[24,1152]{1,0:T(8,128)S(1)} %collective-permute-done.3.refs_1_, f32[24,1152]{1,0:T(8,128)S(1)} %collective-permute-done.4.refs_2_, ...), custom_call_target="tpu_custom_call" | custom-call | tf_op jit(solution)/shard_map/pair_kernel/pallas_call | solution.py:535
  42.3 0.7 %collective-permute-start.6 = (f32[112,128]{1,0:T(8,128)S(1)}, f32[112,128]{1,0:T(8,128)S(1)}, u32[]{:S(2)}, u32[]{:S(2)}) collective-permute-start(f32[112,128]{1,0:T(8,128)S(1)} %get-tuple-element.11), channel_id=1, source_target_pairs={{0,2},{1,3},{2,0},{3,1},{4,6},{5,7},{6,4},{7,5},{8,10},{9,11},{10,... | collective-permute-start | bytes 172040 | tf_op jit(solution)/shard_map/ppermute | solution.py:499
  43.1 0.5 collective-permute-start.7
  43.6 2.3 %collective-permute-start.8 = (f32[112,128]{1,0:T(8,128)S(1)}, f32[112,128]{1,0:T(8,128)S(1)}, u32[]{:S(2)}, u32[]{:S(2)}) collective-permute-start(f32[112,128]{1,0:T(8,128)S(1)} %get-tuple-element.13), channel_id=1, source_target_pairs={{0,3},{1,2},{2,1},{3,0},{4,7},{5,6},{6,5},{7,4},{8,11},{9,10},{10,... | collective-permute-start | bytes 172040 | tf_op jit(solution)/shard_map/ppermute | solution.py:499
  45.9 0.7 %collective-permute-done.6 = f32[112,128]{1,0:T(8,128)S(1)} collective-permute-done((f32[112,128]{1,0:T(8,128)S(1)}, f32[112,128]{1,0:T(8,128)S(1)}, u32[]{:S(2)}, u32[]{:S(2)}) %collective-permute-start.6) | collective-permute-done | bytes 57376 | tf_op jit(solution)/shard_map/ppermute | solution.py:499
  46.6 0.7 %collective-permute-done.7 = f32[112,128]{1,0:T(8,128)S(1)} collective-permute-done((f32[112,128]{1,0:T(8,128)S(1)}, f32[112,128]{1,0:T(8,128)S(1)}, u32[]{:S(2)}, u32[]{:S(2)}) %collective-permute-start.7) | collective-permute-done | bytes 57376 | tf_op jit(solution)/shard_map/ppermute | solution.py:499
  47.2 1.4 %collective-permute-done.8 = f32[112,128]{1,0:T(8,128)S(1)} collective-permute-done((f32[112,128]{1,0:T(8,128)S(1)}, f32[112,128]{1,0:T(8,128)S(1)}, u32[]{:S(2)}, u32[]{:S(2)}) %collective-permute-start.8) | collective-permute-done | bytes 57376 | tf_op jit(solution)/shard_map/ppermute | solution.py:499
  48.7 0.0 copy-start.2
  48.7 1.6 %collective-permute-start.9 = (f32[48,128]{1,0:T(8,128)S(1)}, f32[48,128]{1,0:T(8,128)S(1)}, u32[]{:S(2)}, u32[]{:S(2)}) collective-permute-start(f32[48,128]{1,0:T(8,128)S(1)} %get-tuple-element.14), channel_id=1, source_target_pairs={{0,4},{1,5},{2,6},{3,7},{4,0},{5,1},{6,2},{7,3},{8,12},{9,13},{10,... | collective-permute-start | bytes 73736 | tf_op jit(solution)/shard_map/ppermute | solution.py:499
  50.3 1.2 %collective-permute-start.11 = (f32[16,128]{1,0:T(8,128)S(1)}, f32[16,128]{1,0:T(8,128)S(1)}, u32[]{:S(2)}, u32[]{:S(2)}) collective-permute-start(f32[16,128]{1,0:T(8,128)S(1)} %slice.14), channel_id=1, source_target_pairs={{0,28},{1,29},{2,30},{3,31},{4,8},{5,9},{6,10},{7,11},{8,4},{9,5},... | collective-permute-start | bytes 24584 | tf_op jit(solution)/shard_map/ppermute | solution.py:510
  51.5 0.3 collective-permute-start.10
  51.8 3.3 %collective-permute-done.11.refs_2_ = f32[16,128]{1,0:T(8,128)S(1)} collective-permute-done((f32[16,128]{1,0:T(8,128)S(1)}, f32[16,128]{1,0:T(8,128)S(1)}, u32[]{:S(2)}, u32[]{:S(2)}) %collective-permute-start.11) | collective-permute-done | bytes 8224 | tf_op jit(solution)/shard_map/ppermute | solution.py:510
  55.1 0.0 collective-permute-done.10.refs_1_
  55.1 0.0 collective-permute-done.9.refs_0_
  55.1 0.0 copy-done.2
  55.2 0.8 %finish_kernel.1 = (f32[3,1024]{1,0:T(4,128)}, f32[3,1024]{1,0:T(4,128)}) custom-call(f32[48,128]{1,0:T(8,128)S(1)} %get-tuple-element.15.own_ref, f32[48,128]{1,0:T(8,128)S(1)} %collective-permute-done.9.refs_0_, f32[16,128]{1,0:T(8,128)S(1)} %collective-permute-done.10.refs_1_, f32[16,128]{1,0:T(8,128)S(1)} %collective-permute-done.11.refs_2_, ...), custom_call_target="tpu_custom_call" | custom-call | tf_op jit(solution)/shard_map/finish_kernel/pallas_call | solution.py:567
  (7 shorter events, 0.0 us)
Async XLA Ops:
  1.3 0.8 %copy-start = (f32[9,1024]{1,0:T(8,128)S(1)}, f32[9,1024]{1,0:T(8,128)}, u32[]{:S(2)}) copy-start(f32[9,1024]{1,0:T(8,128)} %refs_1_.1) | copy-start | bytes 110596
  2.1 0.7 %copy-start.1 = (f32[3,1024]{1,0:T(4,128)S(1)}, f32[3,1024]{1,0:T(4,128)}, u32[]{:S(2)}) copy-start(f32[3,1024]{1,0:T(4,128)} %refs_3_.3) | copy-start | bytes 36868
  2.8 0.7 %copy-start.3 = (s32[2,1024]{1,0:T(2,128)S(1)}, s32[2,1024]{1,0:T(2,128)}, u32[]{:S(2)}) copy-start(s32[2,1024]{1,0:T(2,128)} %refs_3_.2) | copy-start | bytes 24580
  3.5 0.7 %copy-start.4 = (s32[1024]{0:T(1024)S(1)}, s32[1024]{0:T(1024)}, u32[]{:S(2)}) copy-start(s32[1024]{0:T(1024)} %param.8) | copy-start | bytes 12292
  4.2 5.9 %copy-start.5 = (s32[8,3,64]{2,0,1:T(8,128)S(1)}, s32[8,3,64]{2,0,1:T(8,128)}, u32[]{:S(2)}) copy-start(s32[8,3,64]{2,0,1:T(8,128)} %param.9) | copy-start | bytes 18436
  4.6 5.9 %collective-permute-start.2 = (f32[24,128]{1,0:T(8,128)S(1)}, f32[24,128]{1,0:T(8,128)S(1)}, u32[]{:S(2)}, u32[]{:S(2)}) collective-permute-start(f32[24,128]{1,0:T(8,128)S(1)} %get-tuple-element.9), channel_id=1, source_target_pairs={{0,28},{1,29},{2,30},{3,31},{4,8},{5,9},{6,10},{7,11},{8,4},{9,5},... | collective-permute-start | bytes 36872 | tf_op jit(solution)/shard_map/ppermute | solution.py:510
  9.1 2.2 %collective-permute-start.1 = (f32[24,128]{1,0:T(8,128)S(1)}, f32[24,128]{1,0:T(8,128)S(1)}, u32[]{:S(2)}, u32[]{:S(2)}) collective-permute-start(f32[24,128]{1,0:T(8,128)S(1)} %get-tuple-element.9), channel_id=1, source_target_pairs={{0,24},{1,25},{2,26},{3,27},{4,12},{5,13},{6,14},{7,15},{8,0},{9,1... | collective-permute-start | bytes 36872 | tf_op jit(solution)/shard_map/ppermute | solution.py:510
  9.9 5.2 %collective-permute-start = (f32[24,512]{1,0:T(8,128)S(1)}, f32[24,512]{1,0:T(8,128)S(1)}, u32[]{:S(2)}, u32[]{:S(2)}) collective-permute-start(f32[24,512]{1,0:T(8,128)S(1)} %get-tuple-element.8), channel_id=1, source_target_pairs={{0,4},{1,5},{2,6},{3,7},{4,0},{5,1},{6,2},{7,3},{8,12},{9,13},{10,... | collective-permute-start | bytes 147464 | tf_op jit(solution)/shard_map/ppermute | solution.py:499
  15.2 5.8 %collective-permute-start.5 = (f32[24,1152]{1,0:T(8,128)S(1)}, f32[24,1152]{1,0:T(8,128)S(1)}, u32[]{:S(2)}, u32[]{:S(2)}) collective-permute-start(f32[24,1152]{1,0:T(8,128)S(1)} %pad_maximum_fusion.refs_0_), channel_id=1, source_target_pairs={{0,2},{1,3},{2,0},{3,1},{4,6},{5,7},{6,4},{7,5},{8,10},{9,11},{10,... | collective-permute-start | bytes 331784 | tf_op jit(solution)/shard_map/ppermute | solution.py:499
  16.6 5.6 %collective-permute-start.4 = (f32[24,1152]{1,0:T(8,128)S(1)}, f32[24,1152]{1,0:T(8,128)S(1)}, u32[]{:S(2)}, u32[]{:S(2)}) collective-permute-start(f32[24,1152]{1,0:T(8,128)S(1)} %pad_maximum_fusion.refs_0_), channel_id=1, source_target_pairs={{0,1},{1,0},{2,3},{3,2},{4,5},{5,4},{6,7},{7,6},{8,9},{9,8},{10,11... | collective-permute-start | bytes 331784 | tf_op jit(solution)/shard_map/ppermute | solution.py:499
  18.1 5.6 %collective-permute-start.3 = (f32[24,1152]{1,0:T(8,128)S(1)}, f32[24,1152]{1,0:T(8,128)S(1)}, u32[]{:S(2)}, u32[]{:S(2)}) collective-permute-start(f32[24,1152]{1,0:T(8,128)S(1)} %pad_maximum_fusion.refs_0_), channel_id=1, source_target_pairs={{0,3},{1,2},{2,1},{3,0},{4,7},{5,6},{6,5},{7,4},{8,11},{9,10},{10,... | collective-permute-start | bytes 331784 | tf_op jit(solution)/shard_map/ppermute | solution.py:499
  42.3 4.2 %collective-permute-start.6 = (f32[112,128]{1,0:T(8,128)S(1)}, f32[112,128]{1,0:T(8,128)S(1)}, u32[]{:S(2)}, u32[]{:S(2)}) collective-permute-start(f32[112,128]{1,0:T(8,128)S(1)} %get-tuple-element.11), channel_id=1, source_target_pairs={{0,2},{1,3},{2,0},{3,1},{4,6},{5,7},{6,4},{7,5},{8,10},{9,11},{10,... | collective-permute-start | bytes 172040 | tf_op jit(solution)/shard_map/ppermute | solution.py:499
  43.1 4.2 %collective-permute-start.7 = (f32[112,128]{1,0:T(8,128)S(1)}, f32[112,128]{1,0:T(8,128)S(1)}, u32[]{:S(2)}, u32[]{:S(2)}) collective-permute-start(f32[112,128]{1,0:T(8,128)S(1)} %get-tuple-element.12), channel_id=1, source_target_pairs={{0,1},{1,0},{2,3},{3,2},{4,5},{5,4},{6,7},{7,6},{8,9},{9,8},{10,11... | collective-permute-start | bytes 172040 | tf_op jit(solution)/shard_map/ppermute | solution.py:499
  43.6 5.1 %collective-permute-start.8 = (f32[112,128]{1,0:T(8,128)S(1)}, f32[112,128]{1,0:T(8,128)S(1)}, u32[]{:S(2)}, u32[]{:S(2)}) collective-permute-start(f32[112,128]{1,0:T(8,128)S(1)} %get-tuple-element.13), channel_id=1, source_target_pairs={{0,3},{1,2},{2,1},{3,0},{4,7},{5,6},{6,5},{7,4},{8,11},{9,10},{10,... | collective-permute-start | bytes 172040 | tf_op jit(solution)/shard_map/ppermute | solution.py:499
  48.7 6.5 %copy-start.2 = (f32[3,1024]{1,0:T(4,128)S(1)}, f32[3,1024]{1,0:T(4,128)}, u32[]{:S(2)}) copy-start(f32[3,1024]{1,0:T(4,128)} %refs_3_.3) | copy-start | bytes 36868
  48.7 6.4 %collective-permute-start.9 = (f32[48,128]{1,0:T(8,128)S(1)}, f32[48,128]{1,0:T(8,128)S(1)}, u32[]{:S(2)}, u32[]{:S(2)}) collective-permute-start(f32[48,128]{1,0:T(8,128)S(1)} %get-tuple-element.14), channel_id=1, source_target_pairs={{0,4},{1,5},{2,6},{3,7},{4,0},{5,1},{6,2},{7,3},{8,12},{9,13},{10,... | collective-permute-start | bytes 73736 | tf_op jit(solution)/shard_map/ppermute | solution.py:499
  50.3 4.9 %collective-permute-start.11 = (f32[16,128]{1,0:T(8,128)S(1)}, f32[16,128]{1,0:T(8,128)S(1)}, u32[]{:S(2)}, u32[]{:S(2)}) collective-permute-start(f32[16,128]{1,0:T(8,128)S(1)} %slice.14), channel_id=1, source_target_pairs={{0,28},{1,29},{2,30},{3,31},{4,8},{5,9},{6,10},{7,11},{8,4},{9,5},... | collective-permute-start | bytes 24584 | tf_op jit(solution)/shard_map/ppermute | solution.py:510
  51.5 3.6 %collective-permute-start.10 = (f32[16,128]{1,0:T(8,128)S(1)}, f32[16,128]{1,0:T(8,128)S(1)}, u32[]{:S(2)}, u32[]{:S(2)}) collective-permute-start(f32[16,128]{1,0:T(8,128)S(1)} %slice.14), channel_id=1, source_target_pairs={{0,8},{1,9},{2,10},{3,11},{4,28},{5,29},{6,30},{7,31},{8,16},{9,17... | collective-permute-start | bytes 24584 | tf_op jit(solution)/shard_map/ppermute | solution.py:510

commit v5 on v4

--- a/solution.py
+++ b/solution.py
@@ -491,7 +491,6 @@
             pltpu.VMEM((2, slots), jnp.int32),
             pltpu.SemaphoreType.DMA((4,)),
         ],
-        compiler_params=pltpu.CompilerParams(vmem_limit_bytes=4 << 20),
         name="payload_kernel",
     )(positions, rotations, clump_kind.reshape(-1, LANES), pair_blocks, pair_count)
 

time: 55.6 us -> 57 us (1.025); the launches traced: 55.9 us -> 56.5 us
  local copies, waits for them, and re-layouts: 3.1 us -> 0.18 us
  waiting for transfers between devices: 15.9 us -> 18.5 us
  Pallas kernels: 19.7 us -> 20.7 us
    unnamed x12 -> x6, local copies, waits for them, and re-layouts: 2.94 us -> 0.01 us
    ppermute x4, waiting for transfers between devices: 4.39 us -> 6.98 us  [cross(): return lax.ppermute(value, ('grp', 'dev'), steps)]
    pallas_call x1, Pallas kernels: 0.34 us -> 1.72 us  [shards(): pl.pallas_call(functools.partial(payload_kernel, slots, members), out_sha...]
  transfers between devices with their start and end apart: 12 -> 12, of which waited for: 10 -> 11; matrix products, arithmetic and copies ran while one was open for 0% -> 0% of each run, Pallas kernels for 0% -> 0%
where the time goes in v5:
time: 57 us; the launch traced here: 56.5 us
  Pallas kernels  20.7 us (36%)
  waiting for transfers between devices  18.5 us (32%)
  starting transfers between devices  15.7 us (28%)
  between operations  1.35 us (2%)
    pallas_call x1, Pallas kernels, shards(): pl.pallas_call(functools.partial(pair_kernel, members, slots), out_shape=...  18.2 us
    ppermute x8, waiting for transfers between devices, trade(): return lax.ppermute(value, 'dev', [(i, i ^ k) for i in range(members)])  11.5 us
    ppermute x8, starting transfers between devices, trade(): return lax.ppermute(value, 'dev', [(i, i ^ k) for i in range(members)])  8.91 us
    ppermute x4, waiting for transfers between devices, cross(): return lax.ppermute(value, ('grp', 'dev'), steps)  6.98 us
    ppermute x4, starting transfers between devices, cross(): return lax.ppermute(value, ('grp', 'dev'), steps)  6.81 us
    pallas_call x1, Pallas kernels, shards(): pl.pallas_call(functools.partial(payload_kernel, slots, members), out_sha...  1.72 us
  transfers between devices with their start and end apart: 12, of which 11 were waited for; matrix products, arithmetic and copies ran while one was open for 0% of the time, Pallas kernels for 0%

profile of v5, /device:TPU:0, one launch (start us, length us, event | category | flops | bytes accessed | tf_op | source)
XLA Modules:
  0.0 56.5 jit_solution(12509860572158406974)
XLA Ops:
  1.3 0.0 copy-start.2
  1.3 1.7 %payload_kernel.1 = (f32[24,512]{1,0:T(8,128)}, f32[24,128]{1,0:T(8,128)}) custom-call(f32[3,1024]{1,0:T(4,128)} %refs_3_.3, f32[9,1024]{1,0:T(8,128)} %refs_1_.1, s32[8,128]{1,0:T(8,128)} %bitcast.5, s32[2,1024]{1,0:T(2,128)} %refs_3_.2, s32[1]{0:T(128)S(6)} %copy.8.refs_4_), custom_call_target="tpu_custom_call" | custom-call | tf_op jit(solution)/shard_map/payload_kernel/pallas_call | solution.py:479
  3.0 4.5 %collective-permute-start.2 = (f32[24,128]{1,0:T(8,128)}, f32[24,128]{1,0:T(8,128)S(1)}, u32[]{:S(2)}, u32[]{:S(2)}) collective-permute-start(f32[24,128]{1,0:T(8,128)} %get-tuple-element.9), channel_id=1, source_target_pairs={{0,28},{1,29},{2,30},{3,31},{4,8},{5,9},{6,10},{7,11},{8,4},{9,5},... | collective-permute-start | bytes 36872 | tf_op jit(solution)/shard_map/ppermute | solution.py:509
  7.5 0.8 %collective-permute-start.1 = (f32[24,128]{1,0:T(8,128)}, f32[24,128]{1,0:T(8,128)S(1)}, u32[]{:S(2)}, u32[]{:S(2)}) collective-permute-start(f32[24,128]{1,0:T(8,128)} %get-tuple-element.9), channel_id=1, source_target_pairs={{0,24},{1,25},{2,26},{3,27},{4,12},{5,13},{6,14},{7,15},{8,0},{9,1... | collective-permute-start | bytes 36872 | tf_op jit(solution)/shard_map/ppermute | solution.py:509
  8.4 0.2 collective-permute-start
  8.5 0.0 copy-done.2
  8.5 0.1 pad_bitcast_fusion.1
  8.6 0.0 copy-start.1
  8.6 0.1 pad.6.clone
  8.7 0.4 collective-permute-done.2
  9.1 0.8 %collective-permute-done.1 = f32[24,128]{1,0:T(8,128)S(1)} collective-permute-done((f32[24,128]{1,0:T(8,128)}, f32[24,128]{1,0:T(8,128)S(1)}, u32[]{:S(2)}, u32[]{:S(2)}) %collective-permute-start.1) | collective-permute-done | bytes 12320 | tf_op jit(solution)/shard_map/ppermute | solution.py:509
  10.0 3.8 %collective-permute-done = f32[24,512]{1,0:T(8,128)S(1)} collective-permute-done((f32[24,512]{1,0:T(8,128)}, f32[24,512]{1,0:T(8,128)S(1)}, u32[]{:S(2)}, u32[]{:S(2)}) %collective-permute-start) | collective-permute-done | bytes 49184 | tf_op jit(solution)/shard_map/ppermute | solution.py:498
  13.8 0.0 copy-done.1
  13.8 1.4 %collective-permute-start.5 = (f32[24,1152]{1,0:T(8,128)S(1)}, f32[24,1152]{1,0:T(8,128)S(1)}, u32[]{:S(2)}, u32[]{:S(2)}) collective-permute-start(f32[24,1152]{1,0:T(8,128)S(1)} %pad_maximum_fusion.refs_0_), channel_id=1, source_target_pairs={{0,2},{1,3},{2,0},{3,1},{4,6},{5,7},{6,4},{7,5},{8,10},{9,11},{10,... | collective-permute-start | bytes 331784 | tf_op jit(solution)/shard_map/ppermute | solution.py:498
  15.2 1.5 %collective-permute-start.4 = (f32[24,1152]{1,0:T(8,128)S(1)}, f32[24,1152]{1,0:T(8,128)S(1)}, u32[]{:S(2)}, u32[]{:S(2)}) collective-permute-start(f32[24,1152]{1,0:T(8,128)S(1)} %pad_maximum_fusion.refs_0_), channel_id=1, source_target_pairs={{0,1},{1,0},{2,3},{3,2},{4,5},{5,4},{6,7},{7,6},{8,9},{9,8},{10,11... | collective-permute-start | bytes 331784 | tf_op jit(solution)/shard_map/ppermute | solution.py:498
  16.7 0.6 %collective-permute-start.3 = (f32[24,1152]{1,0:T(8,128)S(1)}, f32[24,1152]{1,0:T(8,128)S(1)}, u32[]{:S(2)}, u32[]{:S(2)}) collective-permute-start(f32[24,1152]{1,0:T(8,128)S(1)} %pad_maximum_fusion.refs_0_), channel_id=1, source_target_pairs={{0,3},{1,2},{2,1},{3,0},{4,7},{5,6},{6,5},{7,4},{8,11},{9,10},{10,... | collective-permute-start | bytes 331784 | tf_op jit(solution)/shard_map/ppermute | solution.py:498
  17.4 0.1 maximum_maximum_fusion.refs_4_
  17.5 2.2 %collective-permute-done.5.refs_3_ = f32[24,1152]{1,0:T(8,128)S(1)} collective-permute-done((f32[24,1152]{1,0:T(8,128)S(1)}, f32[24,1152]{1,0:T(8,128)S(1)}, u32[]{:S(2)}, u32[]{:S(2)}) %collective-permute-start.5) | collective-permute-done | bytes 110624 | tf_op jit(solution)/shard_map/ppermute | solution.py:498
  19.6 1.1 %collective-permute-done.4.refs_2_ = f32[24,1152]{1,0:T(8,128)S(1)} collective-permute-done((f32[24,1152]{1,0:T(8,128)S(1)}, f32[24,1152]{1,0:T(8,128)S(1)}, u32[]{:S(2)}, u32[]{:S(2)}) %collective-permute-start.4) | collective-permute-done | bytes 110624 | tf_op jit(solution)/shard_map/ppermute | solution.py:498
  20.8 1.6 %collective-permute-done.3.refs_1_ = f32[24,1152]{1,0:T(8,128)S(1)} collective-permute-done((f32[24,1152]{1,0:T(8,128)S(1)}, f32[24,1152]{1,0:T(8,128)S(1)}, u32[]{:S(2)}, u32[]{:S(2)}) %collective-permute-start.3) | collective-permute-done | bytes 110624 | tf_op jit(solution)/shard_map/ppermute | solution.py:498
  22.4 18.2 %pair_kernel.1 = (f32[112,128]{1,0:T(8,128)S(1)}, f32[112,128]{1,0:T(8,128)S(1)}, f32[112,128]{1,0:T(8,128)S(1)}, f32[112,128]{1,0:T(8,128)S(1)}) custom-call(f32[24,1152]{1,0:T(8,128)S(1)} %pad_maximum_fusion.refs_0_, f32[24,1152]{1,0:T(8,128)S(1)} %collective-permute-done.3.refs_1_, f32[24,1152]{1,0:T(8,128)S(1)} %collective-permute-done.4.refs_2_, ...), custom_call_target="tpu_custom_call" | custom-call | tf_op jit(solution)/shard_map/pair_kernel/pallas_call | solution.py:534
  40.6 0.8 %collective-permute-start.6 = (f32[112,128]{1,0:T(8,128)S(1)}, f32[112,128]{1,0:T(8,128)S(1)}, u32[]{:S(2)}, u32[]{:S(2)}) collective-permute-start(f32[112,128]{1,0:T(8,128)S(1)} %get-tuple-element.11), channel_id=1, source_target_pairs={{0,2},{1,3},{2,0},{3,1},{4,6},{5,7},{6,4},{7,5},{8,10},{9,11},{10,... | collective-permute-start | bytes 172040 | tf_op jit(solution)/shard_map/ppermute | solution.py:498
  41.3 0.5 collective-permute-start.7
  41.8 2.3 %collective-permute-start.8 = (f32[112,128]{1,0:T(8,128)S(1)}, f32[112,128]{1,0:T(8,128)S(1)}, u32[]{:S(2)}, u32[]{:S(2)}) collective-permute-start(f32[112,128]{1,0:T(8,128)S(1)} %get-tuple-element.13), channel_id=1, source_target_pairs={{0,3},{1,2},{2,1},{3,0},{4,7},{5,6},{6,5},{7,4},{8,11},{9,10},{10,... | collective-permute-start | bytes 172040 | tf_op jit(solution)/shard_map/ppermute | solution.py:498
  44.1 0.7 %collective-permute-done.6 = f32[112,128]{1,0:T(8,128)S(1)} collective-permute-done((f32[112,128]{1,0:T(8,128)S(1)}, f32[112,128]{1,0:T(8,128)S(1)}, u32[]{:S(2)}, u32[]{:S(2)}) %collective-permute-start.6) | collective-permute-done | bytes 57376 | tf_op jit(solution)/shard_map/ppermute | solution.py:498
  44.8 0.7 %collective-permute-done.7 = f32[112,128]{1,0:T(8,128)S(1)} collective-permute-done((f32[112,128]{1,0:T(8,128)S(1)}, f32[112,128]{1,0:T(8,128)S(1)}, u32[]{:S(2)}, u32[]{:S(2)}) %collective-permute-start.7) | collective-permute-done | bytes 57376 | tf_op jit(solution)/shard_map/ppermute | solution.py:498
  45.5 1.4 %collective-permute-done.8 = f32[112,128]{1,0:T(8,128)S(1)} collective-permute-done((f32[112,128]{1,0:T(8,128)S(1)}, f32[112,128]{1,0:T(8,128)S(1)}, u32[]{:S(2)}, u32[]{:S(2)}) %collective-permute-start.8) | collective-permute-done | bytes 57376 | tf_op jit(solution)/shard_map/ppermute | solution.py:498
  46.9 0.0 copy-start
  46.9 1.6 %collective-permute-start.9 = (f32[48,128]{1,0:T(8,128)S(1)}, f32[48,128]{1,0:T(8,128)S(1)}, u32[]{:S(2)}, u32[]{:S(2)}) collective-permute-start(f32[48,128]{1,0:T(8,128)S(1)} %get-tuple-element.14), channel_id=1, source_target_pairs={{0,4},{1,5},{2,6},{3,7},{4,0},{5,1},{6,2},{7,3},{8,12},{9,13},{10,... | collective-permute-start | bytes 73736 | tf_op jit(solution)/shard_map/ppermute | solution.py:498
  48.6 0.0 collective-permute-start.11
  48.6 1.5 %collective-permute-start.10 = (f32[16,128]{1,0:T(8,128)S(1)}, f32[16,128]{1,0:T(8,128)S(1)}, u32[]{:S(2)}, u32[]{:S(2)}) collective-permute-start(f32[16,128]{1,0:T(8,128)S(1)} %slice.14), channel_id=1, source_target_pairs={{0,8},{1,9},{2,10},{3,11},{4,28},{5,29},{6,30},{7,31},{8,16},{9,17... | collective-permute-start | bytes 24584 | tf_op jit(solution)/shard_map/ppermute | solution.py:509
  50.0 3.4 %collective-permute-done.11.refs_2_ = f32[16,128]{1,0:T(8,128)S(1)} collective-permute-done((f32[16,128]{1,0:T(8,128)S(1)}, f32[16,128]{1,0:T(8,128)S(1)}, u32[]{:S(2)}, u32[]{:S(2)}) %collective-permute-start.11) | collective-permute-done | bytes 8224 | tf_op jit(solution)/shard_map/ppermute | solution.py:509
  53.4 2.3 %collective-permute-done.10.refs_1_ = f32[16,128]{1,0:T(8,128)S(1)} collective-permute-done((f32[16,128]{1,0:T(8,128)S(1)}, f32[16,128]{1,0:T(8,128)S(1)}, u32[]{:S(2)}, u32[]{:S(2)}) %collective-permute-start.10) | collective-permute-done | bytes 8224 | tf_op jit(solution)/shard_map/ppermute | solution.py:509
  55.7 0.0 collective-permute-done.9.refs_0_
  55.7 0.0 copy-done
  55.7 0.8 %finish_kernel.1 = (f32[3,1024]{1,0:T(4,128)}, f32[3,1024]{1,0:T(4,128)}) custom-call(f32[48,128]{1,0:T(8,128)S(1)} %get-tuple-element.15.own_ref, f32[48,128]{1,0:T(8,128)S(1)} %collective-permute-done.9.refs_0_, f32[16,128]{1,0:T(8,128)S(1)} %collective-permute-done.10.refs_1_, f32[16,128]{1,0:T(8,128)S(1)} %collective-permute-done.11.refs_2_, ...), custom_call_target="tpu_custom_call" | custom-call | tf_op jit(solution)/shard_map/finish_kernel/pallas_call | solution.py:566
  (7 shorter events, 0.0 us)
Async XLA Ops:
  1.3 7.3 %copy-start.2 = (s32[8,3,64]{2,0,1:T(8,128)S(1)}, s32[8,3,64]{2,0,1:T(8,128)}, u32[]{:S(2)}) copy-start(s32[8,3,64]{2,0,1:T(8,128)} %param.9) | copy-start | bytes 18436
  3.0 6.1 %collective-permute-start.2 = (f32[24,128]{1,0:T(8,128)}, f32[24,128]{1,0:T(8,128)S(1)}, u32[]{:S(2)}, u32[]{:S(2)}) collective-permute-start(f32[24,128]{1,0:T(8,128)} %get-tuple-element.9), channel_id=1, source_target_pairs={{0,28},{1,29},{2,30},{3,31},{4,8},{5,9},{6,10},{7,11},{8,4},{9,5},... | collective-permute-start | bytes 36872 | tf_op jit(solution)/shard_map/ppermute | solution.py:509
  7.5 2.5 %collective-permute-start.1 = (f32[24,128]{1,0:T(8,128)}, f32[24,128]{1,0:T(8,128)S(1)}, u32[]{:S(2)}, u32[]{:S(2)}) collective-permute-start(f32[24,128]{1,0:T(8,128)} %get-tuple-element.9), channel_id=1, source_target_pairs={{0,24},{1,25},{2,26},{3,27},{4,12},{5,13},{6,14},{7,15},{8,0},{9,1... | collective-permute-start | bytes 36872 | tf_op jit(solution)/shard_map/ppermute | solution.py:509
  8.4 5.4 %collective-permute-start = (f32[24,512]{1,0:T(8,128)}, f32[24,512]{1,0:T(8,128)S(1)}, u32[]{:S(2)}, u32[]{:S(2)}) collective-permute-start(f32[24,512]{1,0:T(8,128)} %get-tuple-element.8), channel_id=1, source_target_pairs={{0,4},{1,5},{2,6},{3,7},{4,0},{5,1},{6,2},{7,3},{8,12},{9,13},{10,... | collective-permute-start | bytes 147464 | tf_op jit(solution)/shard_map/ppermute | solution.py:498
  8.6 5.2 %copy-start.1 = (f32[24,512]{1,0:T(8,128)S(1)}, f32[24,512]{1,0:T(8,128)}, u32[]{:S(2)}) copy-start(f32[24,512]{1,0:T(8,128)} %get-tuple-element.8) | copy-start | bytes 147460
  13.8 5.8 %collective-permute-start.5 = (f32[24,1152]{1,0:T(8,128)S(1)}, f32[24,1152]{1,0:T(8,128)S(1)}, u32[]{:S(2)}, u32[]{:S(2)}) collective-permute-start(f32[24,1152]{1,0:T(8,128)S(1)} %pad_maximum_fusion.refs_0_), channel_id=1, source_target_pairs={{0,2},{1,3},{2,0},{3,1},{4,6},{5,7},{6,4},{7,5},{8,10},{9,11},{10,... | collective-permute-start | bytes 331784 | tf_op jit(solution)/shard_map/ppermute | solution.py:498
  15.2 5.6 %collective-permute-start.4 = (f32[24,1152]{1,0:T(8,128)S(1)}, f32[24,1152]{1,0:T(8,128)S(1)}, u32[]{:S(2)}, u32[]{:S(2)}) collective-permute-start(f32[24,1152]{1,0:T(8,128)S(1)} %pad_maximum_fusion.refs_0_), channel_id=1, source_target_pairs={{0,1},{1,0},{2,3},{3,2},{4,5},{5,4},{6,7},{7,6},{8,9},{9,8},{10,11... | collective-permute-start | bytes 331784 | tf_op jit(solution)/shard_map/ppermute | solution.py:498
  16.7 5.6 %collective-permute-start.3 = (f32[24,1152]{1,0:T(8,128)S(1)}, f32[24,1152]{1,0:T(8,128)S(1)}, u32[]{:S(2)}, u32[]{:S(2)}) collective-permute-start(f32[24,1152]{1,0:T(8,128)S(1)} %pad_maximum_fusion.refs_0_), channel_id=1, source_target_pairs={{0,3},{1,2},{2,1},{3,0},{4,7},{5,6},{6,5},{7,4},{8,11},{9,10},{10,... | collective-permute-start | bytes 331784 | tf_op jit(solution)/shard_map/ppermute | solution.py:498
  40.6 4.2 %collective-permute-start.6 = (f32[112,128]{1,0:T(8,128)S(1)}, f32[112,128]{1,0:T(8,128)S(1)}, u32[]{:S(2)}, u32[]{:S(2)}) collective-permute-start(f32[112,128]{1,0:T(8,128)S(1)} %get-tuple-element.11), channel_id=1, source_target_pairs={{0,2},{1,3},{2,0},{3,1},{4,6},{5,7},{6,4},{7,5},{8,10},{9,11},{10,... | collective-permute-start | bytes 172040 | tf_op jit(solution)/shard_map/ppermute | solution.py:498
  41.3 4.2 %collective-permute-start.7 = (f32[112,128]{1,0:T(8,128)S(1)}, f32[112,128]{1,0:T(8,128)S(1)}, u32[]{:S(2)}, u32[]{:S(2)}) collective-permute-start(f32[112,128]{1,0:T(8,128)S(1)} %get-tuple-element.12), channel_id=1, source_target_pairs={{0,1},{1,0},{2,3},{3,2},{4,5},{5,4},{6,7},{7,6},{8,9},{9,8},{10,11... | collective-permute-start | bytes 172040 | tf_op jit(solution)/shard_map/ppermute | solution.py:498
  41.8 5.1 %collective-permute-start.8 = (f32[112,128]{1,0:T(8,128)S(1)}, f32[112,128]{1,0:T(8,128)S(1)}, u32[]{:S(2)}, u32[]{:S(2)}) collective-permute-start(f32[112,128]{1,0:T(8,128)S(1)} %get-tuple-element.13), channel_id=1, source_target_pairs={{0,3},{1,2},{2,1},{3,0},{4,7},{5,6},{6,5},{7,4},{8,11},{9,10},{10,... | collective-permute-start | bytes 172040 | tf_op jit(solution)/shard_map/ppermute | solution.py:498
  46.9 8.8 %copy-start = (f32[3,1024]{1,0:T(4,128)S(1)}, f32[3,1024]{1,0:T(4,128)}, u32[]{:S(2)}) copy-start(f32[3,1024]{1,0:T(4,128)} %refs_3_.3) | copy-start | bytes 36868
  46.9 8.8 %collective-permute-start.9 = (f32[48,128]{1,0:T(8,128)S(1)}, f32[48,128]{1,0:T(8,128)S(1)}, u32[]{:S(2)}, u32[]{:S(2)}) collective-permute-start(f32[48,128]{1,0:T(8,128)S(1)} %get-tuple-element.14), channel_id=1, source_target_pairs={{0,4},{1,5},{2,6},{3,7},{4,0},{5,1},{6,2},{7,3},{8,12},{9,13},{10,... | collective-permute-start | bytes 73736 | tf_op jit(solution)/shard_map/ppermute | solution.py:498
  48.6 4.9 %collective-permute-start.11 = (f32[16,128]{1,0:T(8,128)S(1)}, f32[16,128]{1,0:T(8,128)S(1)}, u32[]{:S(2)}, u32[]{:S(2)}) collective-permute-start(f32[16,128]{1,0:T(8,128)S(1)} %slice.14), channel_id=1, source_target_pairs={{0,28},{1,29},{2,30},{3,31},{4,8},{5,9},{6,10},{7,11},{8,4},{9,5},... | collective-permute-start | bytes 24584 | tf_op jit(solution)/shard_map/ppermute | solution.py:509
  48.6 7.2 %collective-permute-start.10 = (f32[16,128]{1,0:T(8,128)S(1)}, f32[16,128]{1,0:T(8,128)S(1)}, u32[]{:S(2)}, u32[]{:S(2)}) collective-permute-start(f32[16,128]{1,0:T(8,128)S(1)} %slice.14), channel_id=1, source_target_pairs={{0,8},{1,9},{2,10},{3,11},{4,28},{5,29},{6,30},{7,31},{8,16},{9,17... | collective-permute-start | bytes 24584 | tf_op jit(solution)/shard_map/ppermute | solution.py:509

commit v6 on v5

--- a/solution.py
+++ b/solution.py
@@ -6,6 +6,7 @@
 from jax.experimental import pallas as pl
 from jax.experimental.pallas import tpu as pltpu
 from jax.sharding import PartitionSpec as P
+
 
 RIM = 128
 LANES = 128
@@ -148,7 +149,6 @@
     own_blocks = (pieces[0].shape[1] - RIM) // 2
     inner_blocks = members * own_blocks
     slot_rows = slots // LANES
-    lists = slots // own_blocks
 
     owners = []
     counts = []
@@ -462,17 +462,16 @@
                 out[pl.ds(2 * own_rows + 6 * half + axis, 1), :] = rim
 
 
-def shards(positions, rotations, clump_kind, sub_offsets, pair_blocks, pair_count):
+def whole_step(positions, rotations, clump_kind, sub_offsets, pair_blocks, pair_count):
     members = lax.axis_size("dev")
     groups = lax.axis_size("grp")
-    group = lax.axis_index("grp")
     me = lax.axis_index("dev")
     rings = members // 2
     clique, far = me % rings, me // rings
     clumps = positions.shape[1]
     slots = pair_blocks.shape[1]
     own_blocks = clumps // 2
-    kinds, _, subs = sub_offsets.shape
+    kinds, _, _ = sub_offsets.shape
     vmem = pl.BlockSpec(memory_space=pltpu.VMEM)
     smem = pl.BlockSpec(memory_space=pltpu.SMEM)
 
@@ -508,8 +507,9 @@
         ]
         return lax.ppermute(value, ("grp", "dev"), steps)
 
-    rim_a, rim_b = cross(end, -1, 0), cross(end, -1, rings)
     far_payload = trade(payload, rings)
+    rim_a = cross(end, -1, 0)
+    rim_b = cross(end, -1, rings)
     rim = jnp.where((clique == 0) == (far == 0), rim_a, rim_b)
     both = jnp.concatenate([payload, far_payload, rim], 1)
     order = clique_order(rings)
@@ -560,8 +560,9 @@
     in_low = far == 0
     low, high = column[:own_rows], column[own_rows : 2 * own_rows]
     rim = column[2 * own_rows :]
-    rim_a, rim_b = cross(rim, 1, 0), cross(rim, -1, rings)
     other = trade(jnp.where(in_low, high, low), rings)
+    rim_a = cross(rim, 1, 0)
+    rim_b = cross(rim, -1, rings)
     shares = [jnp.where(in_low, low, high), other, rim_a, rim_b]
     clump_force, clump_torque = pl.pallas_call(
         functools.partial(finish_kernel, members, groups),
@@ -585,7 +586,7 @@
         P(("grp", "dev")),
     )
     return jax.shard_map(
-        shards,
+        whole_step,
         mesh=mesh,
         in_specs=placed,
         out_specs=(P(None, ("grp", "dev")), P(None, ("grp", "dev"))),

time: 57 us -> 55.9 us (0.981)
  waiting for transfers between devices: 18.5 us -> 16.2 us
  Pallas kernels: 20.7 us -> 22.2 us
    ppermute x4, waiting for transfers between devices: 6.98 us -> 4.69 us  [cross(): return lax.ppermute(value, ('grp', 'dev'), steps)]
    pallas_call x3, Pallas kernels: 20.7 us -> 22.2 us  [the longest x1 19.7 us: whole_step(): pl.pallas_call(functools.partial(pair_kernel, members, slots), out_shape=...]
where the time goes in v6:
time: 55.9 us; the launch traced here: 55.8 us
  Pallas kernels  22.2 us (40%)
  waiting for transfers between devices  16.2 us (29%)
  starting transfers between devices  15.7 us (28%)
  between operations  1.35 us (2%)
    pallas_call x1, Pallas kernels, whole_step(): pl.pallas_call(functools.partial(pair_kernel, members, slots), out_shape=...  19.7 us
    ppermute x8, waiting for transfers between devices, trade(): return lax.ppermute(value, 'dev', [(i, i ^ k) for i in range(members)])  11.5 us
    ppermute x8, starting transfers between devices, trade(): return lax.ppermute(value, 'dev', [(i, i ^ k) for i in range(members)])  8.84 us
    ppermute x4, starting transfers between devices, cross(): return lax.ppermute(value, ('grp', 'dev'), steps)  6.88 us
    ppermute x4, waiting for transfers between devices, cross(): return lax.ppermute(value, ('grp', 'dev'), steps)  4.69 us
    pallas_call x1, Pallas kernels, whole_step(): pl.pallas_call(functools.partial(payload_kernel, slots, members), out_sha...  1.72 us
  transfers between devices with their start and end apart: 12, of which 11 were waited for; matrix products, arithmetic and copies ran while one was open for 0% of the time, Pallas kernels for 0%

profile of v6, /device:TPU:0, one launch (start us, length us, event | category | flops | bytes accessed | tf_op | source)
XLA Modules:
  0.0 55.8 jit_solution(12509860572158406974)
XLA Ops:
  1.3 0.0 copy-start.2
  1.3 1.7 %payload_kernel.1 = (f32[24,512]{1,0:T(8,128)}, f32[24,128]{1,0:T(8,128)}) custom-call(f32[3,1024]{1,0:T(4,128)} %refs_3_.3, f32[9,1024]{1,0:T(8,128)} %refs_1_.1, s32[8,128]{1,0:T(8,128)} %bitcast.5, s32[2,1024]{1,0:T(2,128)} %refs_3_.2, s32[1]{0:T(128)S(6)} %copy.8.refs_4_), custom_call_target="tpu_custom_call" | custom-call | tf_op jit(solution)/shard_map/payload_kernel/pallas_call | solution.py:478
  3.0 4.5 %collective-permute-start.2 = (f32[24,128]{1,0:T(8,128)}, f32[24,128]{1,0:T(8,128)S(1)}, u32[]{:S(2)}, u32[]{:S(2)}) collective-permute-start(f32[24,128]{1,0:T(8,128)} %get-tuple-element.9), channel_id=1, source_target_pairs={{0,28},{1,29},{2,30},{3,31},{4,8},{5,9},{6,10},{7,11},{8,4},{9,5},... | collective-permute-start | bytes 36872 | tf_op jit(solution)/shard_map/ppermute | solution.py:508
  7.5 0.8 %collective-permute-start.1 = (f32[24,128]{1,0:T(8,128)}, f32[24,128]{1,0:T(8,128)S(1)}, u32[]{:S(2)}, u32[]{:S(2)}) collective-permute-start(f32[24,128]{1,0:T(8,128)} %get-tuple-element.9), channel_id=1, source_target_pairs={{0,24},{1,25},{2,26},{3,27},{4,12},{5,13},{6,14},{7,15},{8,0},{9,1... | collective-permute-start | bytes 36872 | tf_op jit(solution)/shard_map/ppermute | solution.py:508
  8.4 0.2 collective-permute-start
  8.5 0.0 copy-done.2
  8.5 0.1 pad_bitcast_fusion.1
  8.6 0.0 copy-start.1
  8.6 0.1 pad.6.clone
  8.7 0.4 collective-permute-done.2
  9.1 0.8 %collective-permute-done.1 = f32[24,128]{1,0:T(8,128)S(1)} collective-permute-done((f32[24,128]{1,0:T(8,128)}, f32[24,128]{1,0:T(8,128)S(1)}, u32[]{:S(2)}, u32[]{:S(2)}) %collective-permute-start.1) | collective-permute-done | bytes 12320 | tf_op jit(solution)/shard_map/ppermute | solution.py:508
  10.0 3.8 %collective-permute-done = f32[24,512]{1,0:T(8,128)S(1)} collective-permute-done((f32[24,512]{1,0:T(8,128)}, f32[24,512]{1,0:T(8,128)S(1)}, u32[]{:S(2)}, u32[]{:S(2)}) %collective-permute-start) | collective-permute-done | bytes 49184 | tf_op jit(solution)/shard_map/ppermute | solution.py:497
  13.8 0.0 copy-done.1
  13.8 1.4 %collective-permute-start.5 = (f32[24,1152]{1,0:T(8,128)S(1)}, f32[24,1152]{1,0:T(8,128)S(1)}, u32[]{:S(2)}, u32[]{:S(2)}) collective-permute-start(f32[24,1152]{1,0:T(8,128)S(1)} %pad_maximum_fusion.refs_0_), channel_id=1, source_target_pairs={{0,2},{1,3},{2,0},{3,1},{4,6},{5,7},{6,4},{7,5},{8,10},{9,11},{10,... | collective-permute-start | bytes 331784 | tf_op jit(solution)/shard_map/ppermute | solution.py:497
  15.2 1.5 %collective-permute-start.4 = (f32[24,1152]{1,0:T(8,128)S(1)}, f32[24,1152]{1,0:T(8,128)S(1)}, u32[]{:S(2)}, u32[]{:S(2)}) collective-permute-start(f32[24,1152]{1,0:T(8,128)S(1)} %pad_maximum_fusion.refs_0_), channel_id=1, source_target_pairs={{0,1},{1,0},{2,3},{3,2},{4,5},{5,4},{6,7},{7,6},{8,9},{9,8},{10,11... | collective-permute-start | bytes 331784 | tf_op jit(solution)/shard_map/ppermute | solution.py:497
  16.7 0.6 %collective-permute-start.3 = (f32[24,1152]{1,0:T(8,128)S(1)}, f32[24,1152]{1,0:T(8,128)S(1)}, u32[]{:S(2)}, u32[]{:S(2)}) collective-permute-start(f32[24,1152]{1,0:T(8,128)S(1)} %pad_maximum_fusion.refs_0_), channel_id=1, source_target_pairs={{0,3},{1,2},{2,1},{3,0},{4,7},{5,6},{6,5},{7,4},{8,11},{9,10},{10,... | collective-permute-start | bytes 331784 | tf_op jit(solution)/shard_map/ppermute | solution.py:497
  17.4 0.1 maximum_maximum_fusion.refs_4_
  17.5 2.2 %collective-permute-done.5.refs_3_ = f32[24,1152]{1,0:T(8,128)S(1)} collective-permute-done((f32[24,1152]{1,0:T(8,128)S(1)}, f32[24,1152]{1,0:T(8,128)S(1)}, u32[]{:S(2)}, u32[]{:S(2)}) %collective-permute-start.5) | collective-permute-done | bytes 110624 | tf_op jit(solution)/shard_map/ppermute | solution.py:497
  19.6 1.1 %collective-permute-done.4.refs_2_ = f32[24,1152]{1,0:T(8,128)S(1)} collective-permute-done((f32[24,1152]{1,0:T(8,128)S(1)}, f32[24,1152]{1,0:T(8,128)S(1)}, u32[]{:S(2)}, u32[]{:S(2)}) %collective-permute-start.4) | collective-permute-done | bytes 110624 | tf_op jit(solution)/shard_map/ppermute | solution.py:497
  20.8 1.6 %collective-permute-done.3.refs_1_ = f32[24,1152]{1,0:T(8,128)S(1)} collective-permute-done((f32[24,1152]{1,0:T(8,128)S(1)}, f32[24,1152]{1,0:T(8,128)S(1)}, u32[]{:S(2)}, u32[]{:S(2)}) %collective-permute-start.3) | collective-permute-done | bytes 110624 | tf_op jit(solution)/shard_map/ppermute | solution.py:497
  22.4 19.7 %pair_kernel.1 = (f32[112,128]{1,0:T(8,128)S(1)}, f32[112,128]{1,0:T(8,128)S(1)}, f32[112,128]{1,0:T(8,128)S(1)}, f32[112,128]{1,0:T(8,128)S(1)}) custom-call(f32[24,1152]{1,0:T(8,128)S(1)} %pad_maximum_fusion.refs_0_, f32[24,1152]{1,0:T(8,128)S(1)} %collective-permute-done.3.refs_1_, f32[24,1152]{1,0:T(8,128)S(1)} %collective-permute-done.4.refs_2_, ...), custom_call_target="tpu_custom_call" | custom-call | tf_op jit(solution)/shard_map/pair_kernel/pallas_call | solution.py:534
  42.1 0.8 %collective-permute-start.6 = (f32[112,128]{1,0:T(8,128)S(1)}, f32[112,128]{1,0:T(8,128)S(1)}, u32[]{:S(2)}, u32[]{:S(2)}) collective-permute-start(f32[112,128]{1,0:T(8,128)S(1)} %get-tuple-element.11), channel_id=1, source_target_pairs={{0,2},{1,3},{2,0},{3,1},{4,6},{5,7},{6,4},{7,5},{8,10},{9,11},{10,... | collective-permute-start | bytes 172040 | tf_op jit(solution)/shard_map/ppermute | solution.py:497
  42.8 0.5 collective-permute-start.7
  43.3 2.3 %collective-permute-start.8 = (f32[112,128]{1,0:T(8,128)S(1)}, f32[112,128]{1,0:T(8,128)S(1)}, u32[]{:S(2)}, u32[]{:S(2)}) collective-permute-start(f32[112,128]{1,0:T(8,128)S(1)} %get-tuple-element.13), channel_id=1, source_target_pairs={{0,3},{1,2},{2,1},{3,0},{4,7},{5,6},{6,5},{7,4},{8,11},{9,10},{10,... | collective-permute-start | bytes 172040 | tf_op jit(solution)/shard_map/ppermute | solution.py:497
  45.6 0.7 %collective-permute-done.6 = f32[112,128]{1,0:T(8,128)S(1)} collective-permute-done((f32[112,128]{1,0:T(8,128)S(1)}, f32[112,128]{1,0:T(8,128)S(1)}, u32[]{:S(2)}, u32[]{:S(2)}) %collective-permute-start.6) | collective-permute-done | bytes 57376 | tf_op jit(solution)/shard_map/ppermute | solution.py:497
  46.3 0.7 %collective-permute-done.7 = f32[112,128]{1,0:T(8,128)S(1)} collective-permute-done((f32[112,128]{1,0:T(8,128)S(1)}, f32[112,128]{1,0:T(8,128)S(1)}, u32[]{:S(2)}, u32[]{:S(2)}) %collective-permute-start.7) | collective-permute-done | bytes 57376 | tf_op jit(solution)/shard_map/ppermute | solution.py:497
  47.0 1.4 %collective-permute-done.8 = f32[112,128]{1,0:T(8,128)S(1)} collective-permute-done((f32[112,128]{1,0:T(8,128)S(1)}, f32[112,128]{1,0:T(8,128)S(1)}, u32[]{:S(2)}, u32[]{:S(2)}) %collective-permute-start.8) | collective-permute-done | bytes 57376 | tf_op jit(solution)/shard_map/ppermute | solution.py:497
  48.4 0.0 copy-start
  48.4 1.6 %collective-permute-start.9 = (f32[48,128]{1,0:T(8,128)S(1)}, f32[48,128]{1,0:T(8,128)S(1)}, u32[]{:S(2)}, u32[]{:S(2)}) collective-permute-start(f32[48,128]{1,0:T(8,128)S(1)} %get-tuple-element.14), channel_id=1, source_target_pairs={{0,4},{1,5},{2,6},{3,7},{4,0},{5,1},{6,2},{7,3},{8,12},{9,13},{10,... | collective-permute-start | bytes 73736 | tf_op jit(solution)/shard_map/ppermute | solution.py:497
  50.0 0.0 collective-permute-start.11
  50.0 1.5 %collective-permute-start.10 = (f32[16,128]{1,0:T(8,128)S(1)}, f32[16,128]{1,0:T(8,128)S(1)}, u32[]{:S(2)}, u32[]{:S(2)}) collective-permute-start(f32[16,128]{1,0:T(8,128)S(1)} %slice.14), channel_id=1, source_target_pairs={{0,8},{1,9},{2,10},{3,11},{4,28},{5,29},{6,30},{7,31},{8,16},{9,17... | collective-permute-start | bytes 24584 | tf_op jit(solution)/shard_map/ppermute | solution.py:508
  51.5 3.4 %collective-permute-done.11.refs_2_ = f32[16,128]{1,0:T(8,128)S(1)} collective-permute-done((f32[16,128]{1,0:T(8,128)S(1)}, f32[16,128]{1,0:T(8,128)S(1)}, u32[]{:S(2)}, u32[]{:S(2)}) %collective-permute-start.11) | collective-permute-done | bytes 8224 | tf_op jit(solution)/shard_map/ppermute | solution.py:508
  54.9 0.1 collective-permute-done.10.refs_1_
  55.0 0.0 collective-permute-done.9.refs_0_
  55.0 0.0 copy-done
  55.0 0.8 %finish_kernel.1 = (f32[3,1024]{1,0:T(4,128)}, f32[3,1024]{1,0:T(4,128)}) custom-call(f32[48,128]{1,0:T(8,128)S(1)} %get-tuple-element.15.own_ref, f32[48,128]{1,0:T(8,128)S(1)} %collective-permute-done.9.refs_0_, f32[16,128]{1,0:T(8,128)S(1)} %collective-permute-done.10.refs_1_, f32[16,128]{1,0:T(8,128)S(1)} %collective-permute-done.11.refs_2_, ...), custom_call_target="tpu_custom_call" | custom-call | tf_op jit(solution)/shard_map/finish_kernel/pallas_call | solution.py:567
  (7 shorter events, 0.0 us)
Async XLA Ops:
  1.3 7.3 %copy-start.2 = (s32[8,3,64]{2,0,1:T(8,128)S(1)}, s32[8,3,64]{2,0,1:T(8,128)}, u32[]{:S(2)}) copy-start(s32[8,3,64]{2,0,1:T(8,128)} %param.9) | copy-start | bytes 18436
  3.0 6.1 %collective-permute-start.2 = (f32[24,128]{1,0:T(8,128)}, f32[24,128]{1,0:T(8,128)S(1)}, u32[]{:S(2)}, u32[]{:S(2)}) collective-permute-start(f32[24,128]{1,0:T(8,128)} %get-tuple-element.9), channel_id=1, source_target_pairs={{0,28},{1,29},{2,30},{3,31},{4,8},{5,9},{6,10},{7,11},{8,4},{9,5},... | collective-permute-start | bytes 36872 | tf_op jit(solution)/shard_map/ppermute | solution.py:508
  7.5 2.5 %collective-permute-start.1 = (f32[24,128]{1,0:T(8,128)}, f32[24,128]{1,0:T(8,128)S(1)}, u32[]{:S(2)}, u32[]{:S(2)}) collective-permute-start(f32[24,128]{1,0:T(8,128)} %get-tuple-element.9), channel_id=1, source_target_pairs={{0,24},{1,25},{2,26},{3,27},{4,12},{5,13},{6,14},{7,15},{8,0},{9,1... | collective-permute-start | bytes 36872 | tf_op jit(solution)/shard_map/ppermute | solution.py:508
  8.4 5.4 %collective-permute-start = (f32[24,512]{1,0:T(8,128)}, f32[24,512]{1,0:T(8,128)S(1)}, u32[]{:S(2)}, u32[]{:S(2)}) collective-permute-start(f32[24,512]{1,0:T(8,128)} %get-tuple-element.8), channel_id=1, source_target_pairs={{0,4},{1,5},{2,6},{3,7},{4,0},{5,1},{6,2},{7,3},{8,12},{9,13},{10,... | collective-permute-start | bytes 147464 | tf_op jit(solution)/shard_map/ppermute | solution.py:497
  8.6 5.2 %copy-start.1 = (f32[24,512]{1,0:T(8,128)S(1)}, f32[24,512]{1,0:T(8,128)}, u32[]{:S(2)}) copy-start(f32[24,512]{1,0:T(8,128)} %get-tuple-element.8) | copy-start | bytes 147460
  13.8 5.8 %collective-permute-start.5 = (f32[24,1152]{1,0:T(8,128)S(1)}, f32[24,1152]{1,0:T(8,128)S(1)}, u32[]{:S(2)}, u32[]{:S(2)}) collective-permute-start(f32[24,1152]{1,0:T(8,128)S(1)} %pad_maximum_fusion.refs_0_), channel_id=1, source_target_pairs={{0,2},{1,3},{2,0},{3,1},{4,6},{5,7},{6,4},{7,5},{8,10},{9,11},{10,... | collective-permute-start | bytes 331784 | tf_op jit(solution)/shard_map/ppermute | solution.py:497
  15.2 5.6 %collective-permute-start.4 = (f32[24,1152]{1,0:T(8,128)S(1)}, f32[24,1152]{1,0:T(8,128)S(1)}, u32[]{:S(2)}, u32[]{:S(2)}) collective-permute-start(f32[24,1152]{1,0:T(8,128)S(1)} %pad_maximum_fusion.refs_0_), channel_id=1, source_target_pairs={{0,1},{1,0},{2,3},{3,2},{4,5},{5,4},{6,7},{7,6},{8,9},{9,8},{10,11... | collective-permute-start | bytes 331784 | tf_op jit(solution)/shard_map/ppermute | solution.py:497
  16.7 5.6 %collective-permute-start.3 = (f32[24,1152]{1,0:T(8,128)S(1)}, f32[24,1152]{1,0:T(8,128)S(1)}, u32[]{:S(2)}, u32[]{:S(2)}) collective-permute-start(f32[24,1152]{1,0:T(8,128)S(1)} %pad_maximum_fusion.refs_0_), channel_id=1, source_target_pairs={{0,3},{1,2},{2,1},{3,0},{4,7},{5,6},{6,5},{7,4},{8,11},{9,10},{10,... | collective-permute-start | bytes 331784 | tf_op jit(solution)/shard_map/ppermute | solution.py:497
  42.1 4.2 %collective-permute-start.6 = (f32[112,128]{1,0:T(8,128)S(1)}, f32[112,128]{1,0:T(8,128)S(1)}, u32[]{:S(2)}, u32[]{:S(2)}) collective-permute-start(f32[112,128]{1,0:T(8,128)S(1)} %get-tuple-element.11), channel_id=1, source_target_pairs={{0,2},{1,3},{2,0},{3,1},{4,6},{5,7},{6,4},{7,5},{8,10},{9,11},{10,... | collective-permute-start | bytes 172040 | tf_op jit(solution)/shard_map/ppermute | solution.py:497
  42.8 4.2 %collective-permute-start.7 = (f32[112,128]{1,0:T(8,128)S(1)}, f32[112,128]{1,0:T(8,128)S(1)}, u32[]{:S(2)}, u32[]{:S(2)}) collective-permute-start(f32[112,128]{1,0:T(8,128)S(1)} %get-tuple-element.12), channel_id=1, source_target_pairs={{0,1},{1,0},{2,3},{3,2},{4,5},{5,4},{6,7},{7,6},{8,9},{9,8},{10,11... | collective-permute-start | bytes 172040 | tf_op jit(solution)/shard_map/ppermute | solution.py:497
  43.3 5.1 %collective-permute-start.8 = (f32[112,128]{1,0:T(8,128)S(1)}, f32[112,128]{1,0:T(8,128)S(1)}, u32[]{:S(2)}, u32[]{:S(2)}) collective-permute-start(f32[112,128]{1,0:T(8,128)S(1)} %get-tuple-element.13), channel_id=1, source_target_pairs={{0,3},{1,2},{2,1},{3,0},{4,7},{5,6},{6,5},{7,4},{8,11},{9,10},{10,... | collective-permute-start | bytes 172040 | tf_op jit(solution)/shard_map/ppermute | solution.py:497
  48.4 6.5 %copy-start = (f32[3,1024]{1,0:T(4,128)S(1)}, f32[3,1024]{1,0:T(4,128)}, u32[]{:S(2)}) copy-start(f32[3,1024]{1,0:T(4,128)} %refs_3_.3) | copy-start | bytes 36868
  48.4 6.5 %collective-permute-start.9 = (f32[48,128]{1,0:T(8,128)S(1)}, f32[48,128]{1,0:T(8,128)S(1)}, u32[]{:S(2)}, u32[]{:S(2)}) collective-permute-start(f32[48,128]{1,0:T(8,128)S(1)} %get-tuple-element.14), channel_id=1, source_target_pairs={{0,4},{1,5},{2,6},{3,7},{4,0},{5,1},{6,2},{7,3},{8,12},{9,13},{10,... | collective-permute-start | bytes 73736 | tf_op jit(solution)/shard_map/ppermute | solution.py:497
  50.0 4.9 %collective-permute-start.11 = (f32[16,128]{1,0:T(8,128)S(1)}, f32[16,128]{1,0:T(8,128)S(1)}, u32[]{:S(2)}, u32[]{:S(2)}) collective-permute-start(f32[16,128]{1,0:T(8,128)S(1)} %slice.14), channel_id=1, source_target_pairs={{0,28},{1,29},{2,30},{3,31},{4,8},{5,9},{6,10},{7,11},{8,4},{9,5},... | collective-permute-start | bytes 24584 | tf_op jit(solution)/shard_map/ppermute | solution.py:508
  50.0 5.0 %collective-permute-start.10 = (f32[16,128]{1,0:T(8,128)S(1)}, f32[16,128]{1,0:T(8,128)S(1)}, u32[]{:S(2)}, u32[]{:S(2)}) collective-permute-start(f32[16,128]{1,0:T(8,128)S(1)} %slice.14), channel_id=1, source_target_pairs={{0,8},{1,9},{2,10},{3,11},{4,28},{5,29},{6,30},{7,31},{8,16},{9,17... | collective-permute-start | bytes 24584 | tf_op jit(solution)/shard_map/ppermute | solution.py:508

commit v7 on v6

--- a/solution.py
+++ b/solution.py
@@ -18,7 +18,7 @@
 PARAMS = 10
 ROWS = 24
 RIM_ROWS = 16
-DEPTH = 4
+DEPTH = 6
 
 
 def split3(value):
@@ -198,8 +198,10 @@
         base = index * 2 * slot_rows
         near_list = jnp.where(wanted, moved(list_ref[pl.ds(base, slot_rows), :]), near_list)
         far_list = jnp.where(wanted, moved(list_ref[pl.ds(base + slot_rows, slot_rows), :]), far_list)
-    word_ref[pl.ds(0, slot_rows), :] = near_list.astype(jnp.int32)
-    word_ref[pl.ds(slot_rows, slot_rows), :] = far_list.astype(jnp.int32)
+    for start, found in ((0, near_list), (2 * slot_rows, far_list)):
+        value = found.astype(jnp.int32)
+        word_ref[pl.ds(start, slot_rows, stride=2), :] = value
+        word_ref[pl.ds(start + 1, slot_rows, stride=2), :] = pltpu.roll(value, CHUNK, axis=1)
     copy = pltpu.make_async_copy(word_ref, words, sem)
     copy.start()
 
@@ -244,12 +246,10 @@
     row16 = lax.broadcasted_iota(jnp.int32, (16, LANES), 0)
     keeps = [jnp.where((row16 & 7) == sub, 1.0, 0.0).astype(jnp.bfloat16) for sub in range(8)]
 
-    def fetch(first):
-        row = first >> 7
-        base = first & (LANES - 1)
+    def fetch(turn):
         for index in range(CHUNK):
-            near = words[row, base + index]
-            far = words[slot_rows + row, base + index]
+            near = words[turn, index]
+            far = words[2 * slot_rows + turn, index]
             gathered[pl.ds(index, 1), :] = table[pl.ds(near, 1), :]
             gathered[pl.ds(CHUNK + index, 1), :] = table[pl.ds(far, 1), :]
 
@@ -371,8 +371,8 @@
 
     def scatter(group):
         base = jnp.clip(group, 0, groups - 1) * 8
-        row = base >> 7
-        spot = base & (LANES - 1)
+        row = base // CHUNK
+        spot = lax.rem(base, CHUNK)
         for sub in range(8):
             lower = folded_ref[pl.ds(24 * sub, 24), :LANES]
             upper = folded_ref[pl.ds(24 * sub, 24), LANES:]
@@ -381,7 +381,7 @@
             here = lane24 == jnp.where(live, block & (LANES - 1), -1)
             at = pl.ds(pl.multiple_of((block >> 7) * 24, 8), 24)
             acc_near[at, :] += jnp.where(here, lower + upper, 0.0)
-            block = words[slot_rows + row, spot + sub]
+            block = words[2 * slot_rows + row, spot + sub]
             here = lane24 == jnp.where(live, block & (LANES - 1), -1)
             at = pl.ds(pl.multiple_of((block >> 7) * 48, 8), 48)
             acc_far[at, :] += jnp.concatenate(
@@ -390,7 +390,7 @@
 
     def chunk(turn, carry):
         arrange(pl.multiple_of(turn * CHUNK, CHUNK))
-        fetch(jnp.minimum((turn + 1) * CHUNK, slots - CHUNK))
+        fetch(jnp.minimum(turn + 1, slots // CHUNK - 1))
         return carry
 
     fetch(jnp.int32(0))
@@ -539,8 +539,8 @@
         scratch_shapes=[
             pltpu.VMEM((inner_blocks + 3 * RIM, LANES), jnp.float32),
             pltpu.VMEM((members * 2 * slots // LANES, LANES), jnp.float32),
-            pltpu.VMEM((2 * slots // LANES, LANES), jnp.int32),
-            pltpu.SMEM((2 * slots // LANES, LANES), jnp.int32),
+            pltpu.VMEM((2 * slots // CHUNK, LANES), jnp.int32),
+            pltpu.SMEM((2 * slots // CHUNK, LANES), jnp.int32),
             pltpu.VMEM((2 * CHUNK, LANES), jnp.float32),
             pltpu.VMEM((27 * slots, LANES), jnp.float32),
             pltpu.VMEM((8 * LANES, 2 * LANES), jnp.float32),

time: 55.9 us -> 55.5 us (level)
  transfers between devices with their start and end apart: 12 -> 12, of which waited for: 11 -> 10; matrix products, arithmetic and copies ran while one was open for 0% -> 0% of each run, Pallas kernels for 0% -> 0%
where the time goes in v7:
time: 55.5 us; the launch traced here: 55.3 us
  Pallas kernels  21.8 us (39%)
  waiting for transfers between devices  16.2 us (29%)
  starting transfers between devices  15.7 us (28%)
  between operations  1.35 us (2%)
    pallas_call x1, Pallas kernels, whole_step(): pl.pallas_call(functools.partial(pair_kernel, members, slots), out_shape=...  19.3 us
    ppermute x8, waiting for transfers between devices, trade(): return lax.ppermute(value, 'dev', [(i, i ^ k) for i in range(members)])  11.5 us
    ppermute x8, starting transfers between devices, trade(): return lax.ppermute(value, 'dev', [(i, i ^ k) for i in range(members)])  8.84 us
    ppermute x4, starting transfers between devices, cross(): return lax.ppermute(value, ('grp', 'dev'), steps)  6.88 us
    ppermute x4, waiting for transfers between devices, cross(): return lax.ppermute(value, ('grp', 'dev'), steps)  4.66 us
    pallas_call x1, Pallas kernels, whole_step(): pl.pallas_call(functools.partial(payload_kernel, slots, members), out_sha...  1.72 us
  transfers between devices with their start and end apart: 12, of which 10 were waited for; matrix products, arithmetic and copies ran while one was open for 0% of the time, Pallas kernels for 0%

profile of v7, /device:TPU:0, one launch (start us, length us, event | category | flops | bytes accessed | tf_op | source)
XLA Modules:
  0.0 55.3 jit_solution(790505638306897361)
XLA Ops:
  1.3 0.0 copy-start.2
  1.3 1.7 %payload_kernel.1 = (f32[24,512]{1,0:T(8,128)}, f32[24,128]{1,0:T(8,128)}) custom-call(f32[3,1024]{1,0:T(4,128)} %refs_3_.3, f32[9,1024]{1,0:T(8,128)} %refs_1_.1, s32[8,128]{1,0:T(8,128)} %bitcast.5, s32[2,1024]{1,0:T(2,128)} %refs_3_.2, s32[1]{0:T(128)S(6)} %copy.8.refs_4_), custom_call_target="tpu_custom_call" | custom-call | tf_op jit(solution)/shard_map/payload_kernel/pallas_call | solution.py:478
  3.0 4.5 %collective-permute-start.2 = (f32[24,128]{1,0:T(8,128)}, f32[24,128]{1,0:T(8,128)S(1)}, u32[]{:S(2)}, u32[]{:S(2)}) collective-permute-start(f32[24,128]{1,0:T(8,128)} %get-tuple-element.9), channel_id=1, source_target_pairs={{0,28},{1,29},{2,30},{3,31},{4,8},{5,9},{6,10},{7,11},{8,4},{9,5},... | collective-permute-start | bytes 36872 | tf_op jit(solution)/shard_map/ppermute | solution.py:508
  7.5 0.8 %collective-permute-start.1 = (f32[24,128]{1,0:T(8,128)}, f32[24,128]{1,0:T(8,128)S(1)}, u32[]{:S(2)}, u32[]{:S(2)}) collective-permute-start(f32[24,128]{1,0:T(8,128)} %get-tuple-element.9), channel_id=1, source_target_pairs={{0,24},{1,25},{2,26},{3,27},{4,12},{5,13},{6,14},{7,15},{8,0},{9,1... | collective-permute-start | bytes 36872 | tf_op jit(solution)/shard_map/ppermute | solution.py:508
  8.4 0.2 collective-permute-start
  8.5 0.0 copy-done.2
  8.5 0.1 pad_bitcast_fusion.1
  8.6 0.0 copy-start.1
  8.6 0.1 pad.6.clone
  8.7 0.4 collective-permute-done.2
  9.1 0.8 %collective-permute-done.1 = f32[24,128]{1,0:T(8,128)S(1)} collective-permute-done((f32[24,128]{1,0:T(8,128)}, f32[24,128]{1,0:T(8,128)S(1)}, u32[]{:S(2)}, u32[]{:S(2)}) %collective-permute-start.1) | collective-permute-done | bytes 12320 | tf_op jit(solution)/shard_map/ppermute | solution.py:508
  10.0 3.8 %collective-permute-done = f32[24,512]{1,0:T(8,128)S(1)} collective-permute-done((f32[24,512]{1,0:T(8,128)}, f32[24,512]{1,0:T(8,128)S(1)}, u32[]{:S(2)}, u32[]{:S(2)}) %collective-permute-start) | collective-permute-done | bytes 49184 | tf_op jit(solution)/shard_map/ppermute | solution.py:497
  13.8 0.0 copy-done.1
  13.8 1.4 %collective-permute-start.5 = (f32[24,1152]{1,0:T(8,128)S(1)}, f32[24,1152]{1,0:T(8,128)S(1)}, u32[]{:S(2)}, u32[]{:S(2)}) collective-permute-start(f32[24,1152]{1,0:T(8,128)S(1)} %pad_maximum_fusion.refs_0_), channel_id=1, source_target_pairs={{0,2},{1,3},{2,0},{3,1},{4,6},{5,7},{6,4},{7,5},{8,10},{9,11},{10,... | collective-permute-start | bytes 331784 | tf_op jit(solution)/shard_map/ppermute | solution.py:497
  15.2 1.5 %collective-permute-start.4 = (f32[24,1152]{1,0:T(8,128)S(1)}, f32[24,1152]{1,0:T(8,128)S(1)}, u32[]{:S(2)}, u32[]{:S(2)}) collective-permute-start(f32[24,1152]{1,0:T(8,128)S(1)} %pad_maximum_fusion.refs_0_), channel_id=1, source_target_pairs={{0,1},{1,0},{2,3},{3,2},{4,5},{5,4},{6,7},{7,6},{8,9},{9,8},{10,11... | collective-permute-start | bytes 331784 | tf_op jit(solution)/shard_map/ppermute | solution.py:497
  16.7 0.6 %collective-permute-start.3 = (f32[24,1152]{1,0:T(8,128)S(1)}, f32[24,1152]{1,0:T(8,128)S(1)}, u32[]{:S(2)}, u32[]{:S(2)}) collective-permute-start(f32[24,1152]{1,0:T(8,128)S(1)} %pad_maximum_fusion.refs_0_), channel_id=1, source_target_pairs={{0,3},{1,2},{2,1},{3,0},{4,7},{5,6},{6,5},{7,4},{8,11},{9,10},{10,... | collective-permute-start | bytes 331784 | tf_op jit(solution)/shard_map/ppermute | solution.py:497
  17.4 0.1 maximum_maximum_fusion.refs_4_
  17.5 2.2 %collective-permute-done.5.refs_3_ = f32[24,1152]{1,0:T(8,128)S(1)} collective-permute-done((f32[24,1152]{1,0:T(8,128)S(1)}, f32[24,1152]{1,0:T(8,128)S(1)}, u32[]{:S(2)}, u32[]{:S(2)}) %collective-permute-start.5) | collective-permute-done | bytes 110624 | tf_op jit(solution)/shard_map/ppermute | solution.py:497
  19.6 1.1 %collective-permute-done.4.refs_2_ = f32[24,1152]{1,0:T(8,128)S(1)} collective-permute-done((f32[24,1152]{1,0:T(8,128)S(1)}, f32[24,1152]{1,0:T(8,128)S(1)}, u32[]{:S(2)}, u32[]{:S(2)}) %collective-permute-start.4) | collective-permute-done | bytes 110624 | tf_op jit(solution)/shard_map/ppermute | solution.py:497
  20.8 1.6 %collective-permute-done.3.refs_1_ = f32[24,1152]{1,0:T(8,128)S(1)} collective-permute-done((f32[24,1152]{1,0:T(8,128)S(1)}, f32[24,1152]{1,0:T(8,128)S(1)}, u32[]{:S(2)}, u32[]{:S(2)}) %collective-permute-start.3) | collective-permute-done | bytes 110624 | tf_op jit(solution)/shard_map/ppermute | solution.py:497
  22.4 19.3 %pair_kernel.1 = (f32[112,128]{1,0:T(8,128)S(1)}, f32[112,128]{1,0:T(8,128)S(1)}, f32[112,128]{1,0:T(8,128)S(1)}, f32[112,128]{1,0:T(8,128)S(1)}) custom-call(f32[24,1152]{1,0:T(8,128)S(1)} %pad_maximum_fusion.refs_0_, f32[24,1152]{1,0:T(8,128)S(1)} %collective-permute-done.3.refs_1_, f32[24,1152]{1,0:T(8,128)S(1)} %collective-permute-done.4.refs_2_, ...), custom_call_target="tpu_custom_call" | custom-call | tf_op jit(solution)/shard_map/pair_kernel/pallas_call | solution.py:534
  41.7 0.7 %collective-permute-start.6 = (f32[112,128]{1,0:T(8,128)S(1)}, f32[112,128]{1,0:T(8,128)S(1)}, u32[]{:S(2)}, u32[]{:S(2)}) collective-permute-start(f32[112,128]{1,0:T(8,128)S(1)} %get-tuple-element.11), channel_id=1, source_target_pairs={{0,2},{1,3},{2,0},{3,1},{4,6},{5,7},{6,4},{7,5},{8,10},{9,11},{10,... | collective-permute-start | bytes 172040 | tf_op jit(solution)/shard_map/ppermute | solution.py:497
  42.4 0.5 collective-permute-start.7
  42.9 2.3 %collective-permute-start.8 = (f32[112,128]{1,0:T(8,128)S(1)}, f32[112,128]{1,0:T(8,128)S(1)}, u32[]{:S(2)}, u32[]{:S(2)}) collective-permute-start(f32[112,128]{1,0:T(8,128)S(1)} %get-tuple-element.13), channel_id=1, source_target_pairs={{0,3},{1,2},{2,1},{3,0},{4,7},{5,6},{6,5},{7,4},{8,11},{9,10},{10,... | collective-permute-start | bytes 172040 | tf_op jit(solution)/shard_map/ppermute | solution.py:497
  45.2 0.7 %collective-permute-done.6 = f32[112,128]{1,0:T(8,128)S(1)} collective-permute-done((f32[112,128]{1,0:T(8,128)S(1)}, f32[112,128]{1,0:T(8,128)S(1)}, u32[]{:S(2)}, u32[]{:S(2)}) %collective-permute-start.6) | collective-permute-done | bytes 57376 | tf_op jit(solution)/shard_map/ppermute | solution.py:497
  45.9 0.7 %collective-permute-done.7 = f32[112,128]{1,0:T(8,128)S(1)} collective-permute-done((f32[112,128]{1,0:T(8,128)S(1)}, f32[112,128]{1,0:T(8,128)S(1)}, u32[]{:S(2)}, u32[]{:S(2)}) %collective-permute-start.7) | collective-permute-done | bytes 57376 | tf_op jit(solution)/shard_map/ppermute | solution.py:497
  46.6 1.4 %collective-permute-done.8 = f32[112,128]{1,0:T(8,128)S(1)} collective-permute-done((f32[112,128]{1,0:T(8,128)S(1)}, f32[112,128]{1,0:T(8,128)S(1)}, u32[]{:S(2)}, u32[]{:S(2)}) %collective-permute-start.8) | collective-permute-done | bytes 57376 | tf_op jit(solution)/shard_map/ppermute | solution.py:497
  48.0 0.0 copy-start
  48.0 1.6 %collective-permute-start.9 = (f32[48,128]{1,0:T(8,128)S(1)}, f32[48,128]{1,0:T(8,128)S(1)}, u32[]{:S(2)}, u32[]{:S(2)}) collective-permute-start(f32[48,128]{1,0:T(8,128)S(1)} %get-tuple-element.14), channel_id=1, source_target_pairs={{0,4},{1,5},{2,6},{3,7},{4,0},{5,1},{6,2},{7,3},{8,12},{9,13},{10,... | collective-permute-start | bytes 73736 | tf_op jit(solution)/shard_map/ppermute | solution.py:497
  49.6 0.0 collective-permute-start.11
  49.6 1.5 %collective-permute-start.10 = (f32[16,128]{1,0:T(8,128)S(1)}, f32[16,128]{1,0:T(8,128)S(1)}, u32[]{:S(2)}, u32[]{:S(2)}) collective-permute-start(f32[16,128]{1,0:T(8,128)S(1)} %slice.14), channel_id=1, source_target_pairs={{0,8},{1,9},{2,10},{3,11},{4,28},{5,29},{6,30},{7,31},{8,16},{9,17... | collective-permute-start | bytes 24584 | tf_op jit(solution)/shard_map/ppermute | solution.py:508
  51.1 3.4 %collective-permute-done.11.refs_2_ = f32[16,128]{1,0:T(8,128)S(1)} collective-permute-done((f32[16,128]{1,0:T(8,128)S(1)}, f32[16,128]{1,0:T(8,128)S(1)}, u32[]{:S(2)}, u32[]{:S(2)}) %collective-permute-start.11) | collective-permute-done | bytes 8224 | tf_op jit(solution)/shard_map/ppermute | solution.py:508
  54.5 0.0 collective-permute-done.10.refs_1_
  54.5 0.0 collective-permute-done.9.refs_0_
  54.5 0.0 copy-done
  54.5 0.8 %finish_kernel.1 = (f32[3,1024]{1,0:T(4,128)}, f32[3,1024]{1,0:T(4,128)}) custom-call(f32[48,128]{1,0:T(8,128)S(1)} %get-tuple-element.15.own_ref, f32[48,128]{1,0:T(8,128)S(1)} %collective-permute-done.9.refs_0_, f32[16,128]{1,0:T(8,128)S(1)} %collective-permute-done.10.refs_1_, f32[16,128]{1,0:T(8,128)S(1)} %collective-permute-done.11.refs_2_, ...), custom_call_target="tpu_custom_call" | custom-call | tf_op jit(solution)/shard_map/finish_kernel/pallas_call | solution.py:567
  (7 shorter events, 0.0 us)
Async XLA Ops:
  1.3 7.3 %copy-start.2 = (s32[8,3,64]{2,0,1:T(8,128)S(1)}, s32[8,3,64]{2,0,1:T(8,128)}, u32[]{:S(2)}) copy-start(s32[8,3,64]{2,0,1:T(8,128)} %param.9) | copy-start | bytes 18436
  3.0 6.1 %collective-permute-start.2 = (f32[24,128]{1,0:T(8,128)}, f32[24,128]{1,0:T(8,128)S(1)}, u32[]{:S(2)}, u32[]{:S(2)}) collective-permute-start(f32[24,128]{1,0:T(8,128)} %get-tuple-element.9), channel_id=1, source_target_pairs={{0,28},{1,29},{2,30},{3,31},{4,8},{5,9},{6,10},{7,11},{8,4},{9,5},... | collective-permute-start | bytes 36872 | tf_op jit(solution)/shard_map/ppermute | solution.py:508
  7.5 2.5 %collective-permute-start.1 = (f32[24,128]{1,0:T(8,128)}, f32[24,128]{1,0:T(8,128)S(1)}, u32[]{:S(2)}, u32[]{:S(2)}) collective-permute-start(f32[24,128]{1,0:T(8,128)} %get-tuple-element.9), channel_id=1, source_target_pairs={{0,24},{1,25},{2,26},{3,27},{4,12},{5,13},{6,14},{7,15},{8,0},{9,1... | collective-permute-start | bytes 36872 | tf_op jit(solution)/shard_map/ppermute | solution.py:508
  8.4 5.4 %collective-permute-start = (f32[24,512]{1,0:T(8,128)}, f32[24,512]{1,0:T(8,128)S(1)}, u32[]{:S(2)}, u32[]{:S(2)}) collective-permute-start(f32[24,512]{1,0:T(8,128)} %get-tuple-element.8), channel_id=1, source_target_pairs={{0,4},{1,5},{2,6},{3,7},{4,0},{5,1},{6,2},{7,3},{8,12},{9,13},{10,... | collective-permute-start | bytes 147464 | tf_op jit(solution)/shard_map/ppermute | solution.py:497
  8.6 5.2 %copy-start.1 = (f32[24,512]{1,0:T(8,128)S(1)}, f32[24,512]{1,0:T(8,128)}, u32[]{:S(2)}) copy-start(f32[24,512]{1,0:T(8,128)} %get-tuple-element.8) | copy-start | bytes 147460
  13.8 5.8 %collective-permute-start.5 = (f32[24,1152]{1,0:T(8,128)S(1)}, f32[24,1152]{1,0:T(8,128)S(1)}, u32[]{:S(2)}, u32[]{:S(2)}) collective-permute-start(f32[24,1152]{1,0:T(8,128)S(1)} %pad_maximum_fusion.refs_0_), channel_id=1, source_target_pairs={{0,2},{1,3},{2,0},{3,1},{4,6},{5,7},{6,4},{7,5},{8,10},{9,11},{10,... | collective-permute-start | bytes 331784 | tf_op jit(solution)/shard_map/ppermute | solution.py:497
  15.2 5.6 %collective-permute-start.4 = (f32[24,1152]{1,0:T(8,128)S(1)}, f32[24,1152]{1,0:T(8,128)S(1)}, u32[]{:S(2)}, u32[]{:S(2)}) collective-permute-start(f32[24,1152]{1,0:T(8,128)S(1)} %pad_maximum_fusion.refs_0_), channel_id=1, source_target_pairs={{0,1},{1,0},{2,3},{3,2},{4,5},{5,4},{6,7},{7,6},{8,9},{9,8},{10,11... | collective-permute-start | bytes 331784 | tf_op jit(solution)/shard_map/ppermute | solution.py:497
  16.7 5.6 %collective-permute-start.3 = (f32[24,1152]{1,0:T(8,128)S(1)}, f32[24,1152]{1,0:T(8,128)S(1)}, u32[]{:S(2)}, u32[]{:S(2)}) collective-permute-start(f32[24,1152]{1,0:T(8,128)S(1)} %pad_maximum_fusion.refs_0_), channel_id=1, source_target_pairs={{0,3},{1,2},{2,1},{3,0},{4,7},{5,6},{6,5},{7,4},{8,11},{9,10},{10,... | collective-permute-start | bytes 331784 | tf_op jit(solution)/shard_map/ppermute | solution.py:497
  41.7 4.2 %collective-permute-start.6 = (f32[112,128]{1,0:T(8,128)S(1)}, f32[112,128]{1,0:T(8,128)S(1)}, u32[]{:S(2)}, u32[]{:S(2)}) collective-permute-start(f32[112,128]{1,0:T(8,128)S(1)} %get-tuple-element.11), channel_id=1, source_target_pairs={{0,2},{1,3},{2,0},{3,1},{4,6},{5,7},{6,4},{7,5},{8,10},{9,11},{10,... | collective-permute-start | bytes 172040 | tf_op jit(solution)/shard_map/ppermute | solution.py:497
  42.4 4.2 %collective-permute-start.7 = (f32[112,128]{1,0:T(8,128)S(1)}, f32[112,128]{1,0:T(8,128)S(1)}, u32[]{:S(2)}, u32[]{:S(2)}) collective-permute-start(f32[112,128]{1,0:T(8,128)S(1)} %get-tuple-element.12), channel_id=1, source_target_pairs={{0,1},{1,0},{2,3},{3,2},{4,5},{5,4},{6,7},{7,6},{8,9},{9,8},{10,11... | collective-permute-start | bytes 172040 | tf_op jit(solution)/shard_map/ppermute | solution.py:497
  42.9 5.1 %collective-permute-start.8 = (f32[112,128]{1,0:T(8,128)S(1)}, f32[112,128]{1,0:T(8,128)S(1)}, u32[]{:S(2)}, u32[]{:S(2)}) collective-permute-start(f32[112,128]{1,0:T(8,128)S(1)} %get-tuple-element.13), channel_id=1, source_target_pairs={{0,3},{1,2},{2,1},{3,0},{4,7},{5,6},{6,5},{7,4},{8,11},{9,10},{10,... | collective-permute-start | bytes 172040 | tf_op jit(solution)/shard_map/ppermute | solution.py:497
  48.0 6.5 %copy-start = (f32[3,1024]{1,0:T(4,128)S(1)}, f32[3,1024]{1,0:T(4,128)}, u32[]{:S(2)}) copy-start(f32[3,1024]{1,0:T(4,128)} %refs_3_.3) | copy-start | bytes 36868
  48.0 6.5 %collective-permute-start.9 = (f32[48,128]{1,0:T(8,128)S(1)}, f32[48,128]{1,0:T(8,128)S(1)}, u32[]{:S(2)}, u32[]{:S(2)}) collective-permute-start(f32[48,128]{1,0:T(8,128)S(1)} %get-tuple-element.14), channel_id=1, source_target_pairs={{0,4},{1,5},{2,6},{3,7},{4,0},{5,1},{6,2},{7,3},{8,12},{9,13},{10,... | collective-permute-start | bytes 73736 | tf_op jit(solution)/shard_map/ppermute | solution.py:497
  49.6 4.9 %collective-permute-start.11 = (f32[16,128]{1,0:T(8,128)S(1)}, f32[16,128]{1,0:T(8,128)S(1)}, u32[]{:S(2)}, u32[]{:S(2)}) collective-permute-start(f32[16,128]{1,0:T(8,128)S(1)} %slice.14), channel_id=1, source_target_pairs={{0,28},{1,29},{2,30},{3,31},{4,8},{5,9},{6,10},{7,11},{8,4},{9,5},... | collective-permute-start | bytes 24584 | tf_op jit(solution)/shard_map/ppermute | solution.py:508
  49.6 4.9 %collective-permute-start.10 = (f32[16,128]{1,0:T(8,128)S(1)}, f32[16,128]{1,0:T(8,128)S(1)}, u32[]{:S(2)}, u32[]{:S(2)}) collective-permute-start(f32[16,128]{1,0:T(8,128)S(1)} %slice.14), channel_id=1, source_target_pairs={{0,8},{1,9},{2,10},{3,11},{4,28},{5,29},{6,30},{7,31},{8,16},{9,17... | collective-permute-start | bytes 24584 | tf_op jit(solution)/shard_map/ppermute | solution.py:508

commit v8 on v7

--- a/solution.py
+++ b/solution.py
@@ -15,8 +15,8 @@
 STIFFNESS = 1.0 / 256.0
 CHUNK = 64
 COMPS = 12
-PARAMS = 10
-ROWS = 24
+PARAMS = 8
+ROWS = 16
 RIM_ROWS = 16
 DEPTH = 6
 
@@ -26,6 +26,38 @@
     rest = value - high
     middle = rest.astype(jnp.bfloat16).astype(jnp.float32)
     return high, middle, rest - middle
+
+
+def quaternion(entries):
+    (xx, xy, xz), (yx, yy, yz), (zx, zy, zz) = entries[0:3], entries[3:6], entries[6:9]
+    squares = [1.0 + xx + yy + zz, 1.0 + xx - yy - zz, 1.0 - xx + yy - zz, 1.0 - xx - yy + zz]
+    forms = [
+        [squares[0], zy - yz, xz - zx, yx - xy],
+        [zy - yz, squares[1], yx + xy, xz + zx],
+        [xz - zx, yx + xy, squares[2], zy + yz],
+        [yx - xy, xz + zx, zy + yz, squares[3]],
+    ]
+    largest, form = squares[0], forms[0]
+    for square, other in zip(squares[1:], forms[1:]):
+        better = square > largest
+        largest = jnp.where(better, square, largest)
+        form = [jnp.where(better, new, old) for new, old in zip(other, form)]
+    scale = 0.5 / jnp.sqrt(largest)
+    return [entry * scale for entry in form]
+
+
+def rotation(real, first, second, third):
+    length = real * real + first * first + second * second + third * third
+    double = 4.0 - 2.0 * length
+    along = [double * first, double * second, double * third]
+    xx, yy, zz = along[0] * first, along[1] * second, along[2] * third
+    xy, xz, yz = along[0] * second, along[0] * third, along[1] * third
+    wx, wy, wz = along[0] * real, along[1] * real, along[2] * real
+    return [
+        1.0 - (yy + zz), xy - wz, xz + wy,
+        xy + wz, 1.0 - (xx + zz), yz - wx,
+        xz - wy, yz + wx, 1.0 - (xx + yy),
+    ]
 
 
 def clique_order(count):
@@ -51,17 +83,15 @@
     column = lax.broadcasted_iota(jnp.int32, (wide, wide), 1)
     source = jnp.where(column < LANES, 2 * column, 2 * column - (wide - 1))
     picked = jnp.where(row == source, 1.0, 0.0).astype(jnp.bfloat16)
+    turned = quaternion([rotation_ref[entry : entry + 1, :] for entry in range(9)])
     parts = []
     for turn in range(clumps // wide):
         at = slice(turn * wide, (turn + 1) * wide)
         kinds = kind_ref[2 * turn : 2 * turn + 2, :].astype(jnp.float32)
         value = jnp.concatenate(
-            [
-                position_ref[:, at],
-                rotation_ref[0:6, at],
-                jnp.concatenate([kinds[0:1], kinds[1:2]], 1),
-                jnp.zeros((16 - PARAMS, wide), jnp.float32),
-            ],
+            [position_ref[:, at]]
+            + [entry[:, at] for entry in turned]
+            + [jnp.concatenate([kinds[0:1], kinds[1:2]], 1)],
             0,
         )
         parts += [piece.astype(jnp.bfloat16) for piece in split3(value)]
@@ -69,11 +99,14 @@
         jnp.concatenate(parts, 0), picked, preferred_element_type=jnp.float32
     )
     for turn in range(clumps // wide):
-        high, middle, low = (sorted_parts[16 * (3 * turn + part) : 16 * (3 * turn + part) + 16] for part in range(3))
+        high, middle, low = (
+            sorted_parts[PARAMS * (3 * turn + part) : PARAMS * (3 * turn + part + 1)]
+            for part in range(3)
+        )
         value = (high + middle) + low
         at = slice(turn * LANES, (turn + 1) * LANES)
-        out_ref[0:PARAMS, at] = value[0:PARAMS, :LANES]
-        out_ref[PARAMS : 2 * PARAMS, at] = value[0:PARAMS, LANES:]
+        out_ref[0:PARAMS, at] = value[:, :LANES]
+        out_ref[PARAMS : 2 * PARAMS, at] = value[:, LANES:]
     pairs = pair_ref[...] - lax.axis_index("grp") * inner_blocks
     pairs = jnp.where(
         pairs < 0,
@@ -82,14 +115,14 @@
     )
     live = lax.broadcasted_iota(jnp.int32, pairs.shape, 1) < count_ref[0]
     pairs = jnp.where(live, pairs, -1).astype(jnp.float32)
-    lists = slots // blocks
+    slot_rows = slots // LANES
     for which in range(2):
-        for part in range(lists):
-            out_ref[pl.ds(2 * PARAMS + which * lists + part, 1), :] = pairs[
-                which : which + 1, part * blocks : (part + 1) * blocks
+        for part in range(slot_rows):
+            out_ref[pl.ds(which * slot_rows + part, 1), blocks:] = pairs[
+                which : which + 1, part * LANES : (part + 1) * LANES
             ]
     in_low = lax.axis_index("dev") < members // 2
-    end_ref[...] = jnp.where(in_low, out_ref[:, :RIM], out_ref[:, blocks - RIM :])
+    end_ref[...] = jnp.where(in_low, out_ref[:, :RIM], out_ref[:, blocks - RIM : blocks])
 
 
 def finish_kernel(members, groups, own_ref, *refs):
@@ -142,27 +175,25 @@
     pieces = refs[:piece_count]
     off_ref = refs[piece_count]
     outs = refs[piece_count + 1 : 2 * piece_count + 1]
-    (table, list_ref, word_ref, words, gathered, parts, reach_ref, sums_ref, folded_ref, acc_near,
+    (table, word_ref, words, gathered, parts, reach_ref, sums_ref, folded_ref, acc_near,
      acc_far, sem) = refs[2 * piece_count + 1 :]
     me = lax.axis_index("dev")
     clique = lax.rem(me, piece_count)
-    own_blocks = (pieces[0].shape[1] - RIM) // 2
+    own_columns = (pieces[0].shape[1] - RIM) // 2
+    own_blocks = own_columns - LANES
     inner_blocks = members * own_blocks
     slot_rows = slots // LANES
 
     owners = []
     counts = []
+    slot_lists = []
     for k in range(piece_count):
         for side in range(2):
             owners.append(jnp.bitwise_xor(me, clique_order(piece_count)[k] + side * piece_count))
-            base = (2 * k + side) * 2 * slot_rows
-            for part in range(2 * slot_rows):
-                line, spot = part // (own_blocks // LANES), part % (own_blocks // LANES)
-                at = side * own_blocks + spot * LANES
-                list_ref[pl.ds(base + part, 1), :] = pieces[k][
-                    pl.ds(2 * PARAMS + line, 1), at : at + LANES
-                ]
-            found = jnp.where(list_ref[pl.ds(base, slot_rows), :] >= 0.0, 1.0, 0.0)
+            at = side * own_columns + own_blocks
+            both_lists = pieces[k][:, at : at + LANES]
+            slot_lists.append((both_lists[0:slot_rows], both_lists[slot_rows : 2 * slot_rows]))
+            found = jnp.where(slot_lists[-1][0] >= 0.0, 1.0, 0.0)
             counts.append(jnp.sum(found).astype(jnp.int32))
     starts = []
     total = jnp.int32(0)
@@ -195,9 +226,8 @@
             following = pltpu.roll(turned, (shift >> 7) + 1, axis=0)
             return jnp.where(column < (shift & (LANES - 1)), following, same)
 
-        base = index * 2 * slot_rows
-        near_list = jnp.where(wanted, moved(list_ref[pl.ds(base, slot_rows), :]), near_list)
-        far_list = jnp.where(wanted, moved(list_ref[pl.ds(base + slot_rows, slot_rows), :]), far_list)
+        near_list = jnp.where(wanted, moved(slot_lists[index][0]), near_list)
+        far_list = jnp.where(wanted, moved(slot_lists[index][1]), far_list)
     for start, found in ((0, near_list), (2 * slot_rows, far_list)):
         value = found.astype(jnp.int32)
         word_ref[pl.ds(start, slot_rows, stride=2), :] = value
@@ -209,12 +239,12 @@
         for side in range(2):
             base = pl.multiple_of(owners[2 * k + side] * own_blocks, LANES)
             for tile in range(own_blocks // LANES):
-                at = side * own_blocks + tile * LANES
+                at = side * own_columns + tile * LANES
                 table[pl.ds(base + tile * LANES, LANES), 0:ROWS] = pieces[k][:, at : at + LANES].T
         place = jnp.bitwise_xor(clique, clique_order(piece_count)[k])
         base = jnp.where(place == 0, RIM, jnp.where(place == piece_count - 1, 0, 2 * RIM))
         table[pl.ds(pl.multiple_of(inner_blocks + base, RIM), RIM), 0:ROWS] = pieces[k][
-            :, 2 * own_blocks :
+            :, 2 * own_columns :
         ].T
 
     def clear(turn, carry):
@@ -265,14 +295,11 @@
             )
 
         kind_low = jnp.take_along_axis(
-            packed, jnp.where(pick_low, 9, PARAMS + 9), axis=1, mode="promise_in_bounds"
+            packed, jnp.where(pick_low, PARAMS - 1, 2 * PARAMS - 1), axis=1, mode="promise_in_bounds"
         )
         pick = jnp.where(pick_all & (kind_low == lane_f), 1.0, 0.0).astype(jnp.bfloat16)
         offsets = jnp.dot(pick, off_ref[...], preferred_element_type=jnp.float32)
-        turns = [spread(3 + entry) for entry in range(6)]
-        for mode in range(3):
-            after, last = (mode + 1) % 3, (mode + 2) % 3
-            turns.append(turns[after] * turns[3 + last] - turns[last] * turns[3 + after])
+        turns = rotation(*[spread(3 + entry) for entry in range(4)])
         where_at = []
         for axis in range(3):
             value = spread(axis)
@@ -379,14 +406,14 @@
             live = (group >= 0) & (group * 8 + sub < number)
             block = words[row, spot + sub]
             here = lane24 == jnp.where(live, block & (LANES - 1), -1)
-            at = pl.ds(pl.multiple_of((block >> 7) * 24, 8), 24)
-            acc_near[at, :] += jnp.where(here, lower + upper, 0.0)
+            target = acc_near.at[pl.ds(pl.multiple_of((block >> 7) * 24, 8), 24), :]
+            pltpu.store(target, target[...] + (lower + upper), mask=here)
             block = words[2 * slot_rows + row, spot + sub]
             here = lane24 == jnp.where(live, block & (LANES - 1), -1)
-            at = pl.ds(pl.multiple_of((block >> 7) * 48, 8), 48)
-            acc_far[at, :] += jnp.concatenate(
-                [jnp.where(here, lower, 0.0), jnp.where(here, upper, 0.0)], 0
-            )
+            for half, value in enumerate((lower, upper)):
+                at = pl.multiple_of((block >> 7) * 48 + 24 * half, 8)
+                target = acc_far.at[pl.ds(at, 24), :]
+                pltpu.store(target, target[...] + value, mask=here)
 
     def chunk(turn, carry):
         arrange(pl.multiple_of(turn * CHUNK, CHUNK))
@@ -478,7 +505,7 @@
     payload, end = pl.pallas_call(
         functools.partial(payload_kernel, slots, members),
         out_shape=(
-            jax.ShapeDtypeStruct((ROWS, own_blocks), jnp.float32),
+            jax.ShapeDtypeStruct((ROWS, own_blocks + LANES), jnp.float32),
             jax.ShapeDtypeStruct((ROWS, RIM), jnp.float32),
         ),
         in_specs=[pl.BlockSpec(memory_space=pltpu.HBM)] * 4 + [smem],
@@ -538,7 +565,6 @@
         out_specs=(vmem,) * rings,
         scratch_shapes=[
             pltpu.VMEM((inner_blocks + 3 * RIM, LANES), jnp.float32),
-            pltpu.VMEM((members * 2 * slots // LANES, LANES), jnp.float32),
             pltpu.VMEM((2 * slots // CHUNK, LANES), jnp.int32),
             pltpu.SMEM((2 * slots // CHUNK, LANES), jnp.int32),
             pltpu.VMEM((2 * CHUNK, LANES), jnp.float32),

time: 55.5 us -> 54 us (0.973)
  waiting for transfers between devices: 16.2 us -> 15 us
    ppermute x4, waiting for transfers between devices: 4.66 us -> 3.76 us  [cross(): return lax.ppermute(value, ('grp', 'dev'), steps)]
    ppermute x8, starting transfers between devices: 8.84 us -> 8.03 us  [trade(): return lax.ppermute(value, 'dev', [(i, i ^ k) for i in range(members)])]
    ppermute x4, starting transfers between devices: 6.88 us -> 7.69 us  [cross(): return lax.ppermute(value, ('grp', 'dev'), steps)]
where the time goes in v8:
time: 54 us; the launch traced here: 53.8 us
  Pallas kernels  21.5 us (40%)
  starting transfers between devices  15.7 us (29%)
  waiting for transfers between devices  15 us (28%)
  between operations  1.35 us (2%)
    pallas_call x1, Pallas kernels, whole_step(): pl.pallas_call(functools.partial(pair_kernel, members, slots), out_shape=...  19 us
    ppermute x8, waiting for transfers between devices, trade(): return lax.ppermute(value, 'dev', [(i, i ^ k) for i in range(members)])  11.2 us
    ppermute x8, starting transfers between devices, trade(): return lax.ppermute(value, 'dev', [(i, i ^ k) for i in range(members)])  8.03 us
    ppermute x4, starting transfers between devices, cross(): return lax.ppermute(value, ('grp', 'dev'), steps)  7.69 us
    ppermute x4, waiting for transfers between devices, cross(): return lax.ppermute(value, ('grp', 'dev'), steps)  3.76 us
    pallas_call x1, Pallas kernels, whole_step(): pl.pallas_call(functools.partial(payload_kernel, slots, members), out_sha...  1.71 us
  transfers between devices with their start and end apart: 12, of which 10 were waited for; matrix products, arithmetic and copies ran while one was open for 0% of the time, Pallas kernels for 0%

profile of v8, /device:TPU:0, one launch (start us, length us, event | category | flops | bytes accessed | tf_op | source)
XLA Modules:
  0.0 53.8 jit_solution(15575967668544914785)
XLA Ops:
  1.3 0.0 copy-start.2
  1.3 1.7 %payload_kernel.1 = (f32[16,640]{1,0:T(8,128)}, f32[16,128]{1,0:T(8,128)}) custom-call(f32[3,1024]{1,0:T(4,128)} %refs_3_.3, f32[9,1024]{1,0:T(8,128)} %refs_1_.1, s32[8,128]{1,0:T(8,128)} %bitcast.5, s32[2,1024]{1,0:T(2,128)} %refs_3_.2, s32[1]{0:T(128)S(6)} %copy.8.refs_4_), custom_call_target="tpu_custom_call" | custom-call | tf_op jit(solution)/shard_map/payload_kernel/pallas_call | solution.py:505
  3.0 4.5 %collective-permute-start.2 = (f32[16,128]{1,0:T(8,128)}, f32[16,128]{1,0:T(8,128)S(1)}, u32[]{:S(2)}, u32[]{:S(2)}) collective-permute-start(f32[16,128]{1,0:T(8,128)} %get-tuple-element.9), channel_id=1, source_target_pairs={{0,28},{1,29},{2,30},{3,31},{4,8},{5,9},{6,10},{7,11},{8,4},{9,5},... | collective-permute-start | bytes 24584 | tf_op jit(solution)/shard_map/ppermute | solution.py:535
  7.5 0.8 %collective-permute-start.1 = (f32[16,128]{1,0:T(8,128)}, f32[16,128]{1,0:T(8,128)S(1)}, u32[]{:S(2)}, u32[]{:S(2)}) collective-permute-start(f32[16,128]{1,0:T(8,128)} %get-tuple-element.9), channel_id=1, source_target_pairs={{0,24},{1,25},{2,26},{3,27},{4,12},{5,13},{6,14},{7,15},{8,0},{9,1... | collective-permute-start | bytes 24584 | tf_op jit(solution)/shard_map/ppermute | solution.py:535
  8.3 0.2 collective-permute-start
  8.5 0.0 copy-done.2
  8.5 0.1 pad_bitcast_fusion.1
  8.6 0.0 copy-start.1
  8.6 0.1 pad.6.clone
  8.7 0.4 collective-permute-done.2
  9.1 0.8 %collective-permute-done.1 = f32[16,128]{1,0:T(8,128)S(1)} collective-permute-done((f32[16,128]{1,0:T(8,128)}, f32[16,128]{1,0:T(8,128)S(1)}, u32[]{:S(2)}, u32[]{:S(2)}) %collective-permute-start.1) | collective-permute-done | bytes 8224 | tf_op jit(solution)/shard_map/ppermute | solution.py:535
  9.9 3.7 %collective-permute-done = f32[16,640]{1,0:T(8,128)S(1)} collective-permute-done((f32[16,640]{1,0:T(8,128)}, f32[16,640]{1,0:T(8,128)S(1)}, u32[]{:S(2)}, u32[]{:S(2)}) %collective-permute-start) | collective-permute-done | bytes 40992 | tf_op jit(solution)/shard_map/ppermute | solution.py:524
  13.6 0.0 copy-done.1
  13.6 1.5 %collective-permute-start.5 = (f32[16,1408]{1,0:T(8,128)S(1)}, f32[16,1408]{1,0:T(8,128)S(1)}, u32[]{:S(2)}, u32[]{:S(2)}) collective-permute-start(f32[16,1408]{1,0:T(8,128)S(1)} %pad_maximum_fusion.refs_0_), channel_id=1, source_target_pairs={{0,2},{1,3},{2,0},{3,1},{4,6},{5,7},{6,4},{7,5},{8,10},{9,11},{10,... | collective-permute-start | bytes 270344 | tf_op jit(solution)/shard_map/ppermute | solution.py:524
  15.1 1.5 %collective-permute-start.4 = (f32[16,1408]{1,0:T(8,128)S(1)}, f32[16,1408]{1,0:T(8,128)S(1)}, u32[]{:S(2)}, u32[]{:S(2)}) collective-permute-start(f32[16,1408]{1,0:T(8,128)S(1)} %pad_maximum_fusion.refs_0_), channel_id=1, source_target_pairs={{0,1},{1,0},{2,3},{3,2},{4,5},{5,4},{6,7},{7,6},{8,9},{9,8},{10,11... | collective-permute-start | bytes 270344 | tf_op jit(solution)/shard_map/ppermute | solution.py:524
  16.6 0.5 %collective-permute-start.3 = (f32[16,1408]{1,0:T(8,128)S(1)}, f32[16,1408]{1,0:T(8,128)S(1)}, u32[]{:S(2)}, u32[]{:S(2)}) collective-permute-start(f32[16,1408]{1,0:T(8,128)S(1)} %pad_maximum_fusion.refs_0_), channel_id=1, source_target_pairs={{0,3},{1,2},{2,1},{3,0},{4,7},{5,6},{6,5},{7,4},{8,11},{9,10},{10,... | collective-permute-start | bytes 270344 | tf_op jit(solution)/shard_map/ppermute | solution.py:524
  17.2 0.1 maximum_maximum_fusion.refs_4_
  17.3 1.8 %collective-permute-done.5.refs_3_ = f32[16,1408]{1,0:T(8,128)S(1)} collective-permute-done((f32[16,1408]{1,0:T(8,128)S(1)}, f32[16,1408]{1,0:T(8,128)S(1)}, u32[]{:S(2)}, u32[]{:S(2)}) %collective-permute-start.5) | collective-permute-done | bytes 90144 | tf_op jit(solution)/shard_map/ppermute | solution.py:524
  19.1 1.2 %collective-permute-done.4.refs_2_ = f32[16,1408]{1,0:T(8,128)S(1)} collective-permute-done((f32[16,1408]{1,0:T(8,128)S(1)}, f32[16,1408]{1,0:T(8,128)S(1)}, u32[]{:S(2)}, u32[]{:S(2)}) %collective-permute-start.4) | collective-permute-done | bytes 90144 | tf_op jit(solution)/shard_map/ppermute | solution.py:524
  20.3 1.8 %collective-permute-done.3.refs_1_ = f32[16,1408]{1,0:T(8,128)S(1)} collective-permute-done((f32[16,1408]{1,0:T(8,128)S(1)}, f32[16,1408]{1,0:T(8,128)S(1)}, u32[]{:S(2)}, u32[]{:S(2)}) %collective-permute-start.3) | collective-permute-done | bytes 90144 | tf_op jit(solution)/shard_map/ppermute | solution.py:524
  22.1 19.0 %pair_kernel.1 = (f32[112,128]{1,0:T(8,128)S(1)}, f32[112,128]{1,0:T(8,128)S(1)}, f32[112,128]{1,0:T(8,128)S(1)}, f32[112,128]{1,0:T(8,128)S(1)}) custom-call(f32[16,1408]{1,0:T(8,128)S(1)} %pad_maximum_fusion.refs_0_, f32[16,1408]{1,0:T(8,128)S(1)} %collective-permute-done.3.refs_1_, f32[16,1408]{1,0:T(8,128)S(1)} %collective-permute-done.4.refs_2_, ...), custom_call_target="tpu_custom_call" | custom-call | tf_op jit(solution)/shard_map/pair_kernel/pallas_call | solution.py:561
  41.1 0.7 %collective-permute-start.6 = (f32[112,128]{1,0:T(8,128)S(1)}, f32[112,128]{1,0:T(8,128)S(1)}, u32[]{:S(2)}, u32[]{:S(2)}) collective-permute-start(f32[112,128]{1,0:T(8,128)S(1)} %get-tuple-element.11), channel_id=1, source_target_pairs={{0,2},{1,3},{2,0},{3,1},{4,6},{5,7},{6,4},{7,5},{8,10},{9,11},{10,... | collective-permute-start | bytes 172040 | tf_op jit(solution)/shard_map/ppermute | solution.py:524
  41.7 0.5 collective-permute-start.7
  42.3 2.4 %collective-permute-start.8 = (f32[112,128]{1,0:T(8,128)S(1)}, f32[112,128]{1,0:T(8,128)S(1)}, u32[]{:S(2)}, u32[]{:S(2)}) collective-permute-start(f32[112,128]{1,0:T(8,128)S(1)} %get-tuple-element.13), channel_id=1, source_target_pairs={{0,3},{1,2},{2,1},{3,0},{4,7},{5,6},{6,5},{7,4},{8,11},{9,10},{10,... | collective-permute-start | bytes 172040 | tf_op jit(solution)/shard_map/ppermute | solution.py:524
  44.6 0.7 %collective-permute-done.6 = f32[112,128]{1,0:T(8,128)S(1)} collective-permute-done((f32[112,128]{1,0:T(8,128)S(1)}, f32[112,128]{1,0:T(8,128)S(1)}, u32[]{:S(2)}, u32[]{:S(2)}) %collective-permute-start.6) | collective-permute-done | bytes 57376 | tf_op jit(solution)/shard_map/ppermute | solution.py:524
  45.3 0.6 %collective-permute-done.7 = f32[112,128]{1,0:T(8,128)S(1)} collective-permute-done((f32[112,128]{1,0:T(8,128)S(1)}, f32[112,128]{1,0:T(8,128)S(1)}, u32[]{:S(2)}, u32[]{:S(2)}) %collective-permute-start.7) | collective-permute-done | bytes 57376 | tf_op jit(solution)/shard_map/ppermute | solution.py:524
  45.9 1.4 %collective-permute-done.8 = f32[112,128]{1,0:T(8,128)S(1)} collective-permute-done((f32[112,128]{1,0:T(8,128)S(1)}, f32[112,128]{1,0:T(8,128)S(1)}, u32[]{:S(2)}, u32[]{:S(2)}) %collective-permute-start.8) | collective-permute-done | bytes 57376 | tf_op jit(solution)/shard_map/ppermute | solution.py:524
  47.4 0.0 copy-start
  47.4 0.8 %collective-permute-start.9 = (f32[48,128]{1,0:T(8,128)S(1)}, f32[48,128]{1,0:T(8,128)S(1)}, u32[]{:S(2)}, u32[]{:S(2)}) collective-permute-start(f32[48,128]{1,0:T(8,128)S(1)} %get-tuple-element.14), channel_id=1, source_target_pairs={{0,4},{1,5},{2,6},{3,7},{4,0},{5,1},{6,2},{7,3},{8,12},{9,13},{10,... | collective-permute-start | bytes 73736 | tf_op jit(solution)/shard_map/ppermute | solution.py:524
  48.1 0.0 collective-permute-start.11
  48.1 2.3 %collective-permute-start.10 = (f32[16,128]{1,0:T(8,128)S(1)}, f32[16,128]{1,0:T(8,128)S(1)}, u32[]{:S(2)}, u32[]{:S(2)}) collective-permute-start(f32[16,128]{1,0:T(8,128)S(1)} %slice.14), channel_id=1, source_target_pairs={{0,8},{1,9},{2,10},{3,11},{4,28},{5,29},{6,30},{7,31},{8,16},{9,17... | collective-permute-start | bytes 24584 | tf_op jit(solution)/shard_map/ppermute | solution.py:535
  50.5 2.5 %collective-permute-done.11.refs_2_ = f32[16,128]{1,0:T(8,128)S(1)} collective-permute-done((f32[16,128]{1,0:T(8,128)S(1)}, f32[16,128]{1,0:T(8,128)S(1)}, u32[]{:S(2)}, u32[]{:S(2)}) %collective-permute-start.11) | collective-permute-done | bytes 8224 | tf_op jit(solution)/shard_map/ppermute | solution.py:535
  53.0 0.0 collective-permute-done.10.refs_1_
  53.0 0.0 collective-permute-done.9.refs_0_
  53.0 0.0 copy-done
  53.0 0.8 %finish_kernel.1 = (f32[3,1024]{1,0:T(4,128)}, f32[3,1024]{1,0:T(4,128)}) custom-call(f32[48,128]{1,0:T(8,128)S(1)} %get-tuple-element.15.own_ref, f32[48,128]{1,0:T(8,128)S(1)} %collective-permute-done.9.refs_0_, f32[16,128]{1,0:T(8,128)S(1)} %collective-permute-done.10.refs_1_, f32[16,128]{1,0:T(8,128)S(1)} %collective-permute-done.11.refs_2_, ...), custom_call_target="tpu_custom_call" | custom-call | tf_op jit(solution)/shard_map/finish_kernel/pallas_call | solution.py:593
  (7 shorter events, 0.0 us)
Async XLA Ops:
  1.3 7.2 %copy-start.2 = (s32[8,3,64]{2,0,1:T(8,128)S(1)}, s32[8,3,64]{2,0,1:T(8,128)}, u32[]{:S(2)}) copy-start(s32[8,3,64]{2,0,1:T(8,128)} %param.9) | copy-start | bytes 18436
  3.0 6.1 %collective-permute-start.2 = (f32[16,128]{1,0:T(8,128)}, f32[16,128]{1,0:T(8,128)S(1)}, u32[]{:S(2)}, u32[]{:S(2)}) collective-permute-start(f32[16,128]{1,0:T(8,128)} %get-tuple-element.9), channel_id=1, source_target_pairs={{0,28},{1,29},{2,30},{3,31},{4,8},{5,9},{6,10},{7,11},{8,4},{9,5},... | collective-permute-start | bytes 24584 | tf_op jit(solution)/shard_map/ppermute | solution.py:535
  7.5 2.4 %collective-permute-start.1 = (f32[16,128]{1,0:T(8,128)}, f32[16,128]{1,0:T(8,128)S(1)}, u32[]{:S(2)}, u32[]{:S(2)}) collective-permute-start(f32[16,128]{1,0:T(8,128)} %get-tuple-element.9), channel_id=1, source_target_pairs={{0,24},{1,25},{2,26},{3,27},{4,12},{5,13},{6,14},{7,15},{8,0},{9,1... | collective-permute-start | bytes 24584 | tf_op jit(solution)/shard_map/ppermute | solution.py:535
  8.3 5.3 %collective-permute-start = (f32[16,640]{1,0:T(8,128)}, f32[16,640]{1,0:T(8,128)S(1)}, u32[]{:S(2)}, u32[]{:S(2)}) collective-permute-start(f32[16,640]{1,0:T(8,128)} %get-tuple-element.8), channel_id=1, source_target_pairs={{0,4},{1,5},{2,6},{3,7},{4,0},{5,1},{6,2},{7,3},{8,12},{9,13},{10,... | collective-permute-start | bytes 122888 | tf_op jit(solution)/shard_map/ppermute | solution.py:524
  8.6 5.0 %copy-start.1 = (f32[16,640]{1,0:T(8,128)S(1)}, f32[16,640]{1,0:T(8,128)}, u32[]{:S(2)}) copy-start(f32[16,640]{1,0:T(8,128)} %get-tuple-element.8) | copy-start | bytes 122884
  13.6 5.4 %collective-permute-start.5 = (f32[16,1408]{1,0:T(8,128)S(1)}, f32[16,1408]{1,0:T(8,128)S(1)}, u32[]{:S(2)}, u32[]{:S(2)}) collective-permute-start(f32[16,1408]{1,0:T(8,128)S(1)} %pad_maximum_fusion.refs_0_), channel_id=1, source_target_pairs={{0,2},{1,3},{2,0},{3,1},{4,6},{5,7},{6,4},{7,5},{8,10},{9,11},{10,... | collective-permute-start | bytes 270344 | tf_op jit(solution)/shard_map/ppermute | solution.py:524
  15.1 5.1 %collective-permute-start.4 = (f32[16,1408]{1,0:T(8,128)S(1)}, f32[16,1408]{1,0:T(8,128)S(1)}, u32[]{:S(2)}, u32[]{:S(2)}) collective-permute-start(f32[16,1408]{1,0:T(8,128)S(1)} %pad_maximum_fusion.refs_0_), channel_id=1, source_target_pairs={{0,1},{1,0},{2,3},{3,2},{4,5},{5,4},{6,7},{7,6},{8,9},{9,8},{10,11... | collective-permute-start | bytes 270344 | tf_op jit(solution)/shard_map/ppermute | solution.py:524
  16.6 5.4 %collective-permute-start.3 = (f32[16,1408]{1,0:T(8,128)S(1)}, f32[16,1408]{1,0:T(8,128)S(1)}, u32[]{:S(2)}, u32[]{:S(2)}) collective-permute-start(f32[16,1408]{1,0:T(8,128)S(1)} %pad_maximum_fusion.refs_0_), channel_id=1, source_target_pairs={{0,3},{1,2},{2,1},{3,0},{4,7},{5,6},{6,5},{7,4},{8,11},{9,10},{10,... | collective-permute-start | bytes 270344 | tf_op jit(solution)/shard_map/ppermute | solution.py:524
  41.1 4.2 %collective-permute-start.6 = (f32[112,128]{1,0:T(8,128)S(1)}, f32[112,128]{1,0:T(8,128)S(1)}, u32[]{:S(2)}, u32[]{:S(2)}) collective-permute-start(f32[112,128]{1,0:T(8,128)S(1)} %get-tuple-element.11), channel_id=1, source_target_pairs={{0,2},{1,3},{2,0},{3,1},{4,6},{5,7},{6,4},{7,5},{8,10},{9,11},{10,... | collective-permute-start | bytes 172040 | tf_op jit(solution)/shard_map/ppermute | solution.py:524
  41.7 4.2 %collective-permute-start.7 = (f32[112,128]{1,0:T(8,128)S(1)}, f32[112,128]{1,0:T(8,128)S(1)}, u32[]{:S(2)}, u32[]{:S(2)}) collective-permute-start(f32[112,128]{1,0:T(8,128)S(1)} %get-tuple-element.12), channel_id=1, source_target_pairs={{0,1},{1,0},{2,3},{3,2},{4,5},{5,4},{6,7},{7,6},{8,9},{9,8},{10,11... | collective-permute-start | bytes 172040 | tf_op jit(solution)/shard_map/ppermute | solution.py:524
  42.3 5.1 %collective-permute-start.8 = (f32[112,128]{1,0:T(8,128)S(1)}, f32[112,128]{1,0:T(8,128)S(1)}, u32[]{:S(2)}, u32[]{:S(2)}) collective-permute-start(f32[112,128]{1,0:T(8,128)S(1)} %get-tuple-element.13), channel_id=1, source_target_pairs={{0,3},{1,2},{2,1},{3,0},{4,7},{5,6},{6,5},{7,4},{8,11},{9,10},{10,... | collective-permute-start | bytes 172040 | tf_op jit(solution)/shard_map/ppermute | solution.py:524
  47.4 5.7 %copy-start = (f32[3,1024]{1,0:T(4,128)S(1)}, f32[3,1024]{1,0:T(4,128)}, u32[]{:S(2)}) copy-start(f32[3,1024]{1,0:T(4,128)} %refs_3_.3) | copy-start | bytes 36868
  47.4 5.6 %collective-permute-start.9 = (f32[48,128]{1,0:T(8,128)S(1)}, f32[48,128]{1,0:T(8,128)S(1)}, u32[]{:S(2)}, u32[]{:S(2)}) collective-permute-start(f32[48,128]{1,0:T(8,128)S(1)} %get-tuple-element.14), channel_id=1, source_target_pairs={{0,4},{1,5},{2,6},{3,7},{4,0},{5,1},{6,2},{7,3},{8,12},{9,13},{10,... | collective-permute-start | bytes 73736 | tf_op jit(solution)/shard_map/ppermute | solution.py:524
  48.1 4.9 %collective-permute-start.11 = (f32[16,128]{1,0:T(8,128)S(1)}, f32[16,128]{1,0:T(8,128)S(1)}, u32[]{:S(2)}, u32[]{:S(2)}) collective-permute-start(f32[16,128]{1,0:T(8,128)S(1)} %slice.14), channel_id=1, source_target_pairs={{0,28},{1,29},{2,30},{3,31},{4,8},{5,9},{6,10},{7,11},{8,4},{9,5},... | collective-permute-start | bytes 24584 | tf_op jit(solution)/shard_map/ppermute | solution.py:535
  48.1 4.9 %collective-permute-start.10 = (f32[16,128]{1,0:T(8,128)S(1)}, f32[16,128]{1,0:T(8,128)S(1)}, u32[]{:S(2)}, u32[]{:S(2)}) collective-permute-start(f32[16,128]{1,0:T(8,128)S(1)} %slice.14), channel_id=1, source_target_pairs={{0,8},{1,9},{2,10},{3,11},{4,28},{5,29},{6,30},{7,31},{8,16},{9,17... | collective-permute-start | bytes 24584 | tf_op jit(solution)/shard_map/ppermute | solution.py:535

commit v9 on v8

--- a/solution.py
+++ b/solution.py
@@ -61,7 +61,7 @@
 
 
 def clique_order(count):
-    return [0, count - 1] + list(range(1, count - 1))
+    return list(range(count))
 
 
 def payload_kernel(slots, members, *refs):
@@ -447,12 +447,18 @@
                 reach_ref[pl.ds(stale + LANES * couple, LANES), :], base, pair
             )
 
-    def octets(turn, carry):
-        for sub in range(DEPTH):
-            octet(DEPTH * turn + sub, sub % 2)
-        return carry
-
-    lax.fori_loop(0, (groups + 2 + DEPTH) // DEPTH, octets, 0)
+    def octets(depth, start):
+        def turn_of(turn, carry):
+            for sub in range(depth):
+                octet(start + depth * turn + sub, sub % 2)
+            return carry
+
+        return turn_of
+
+    turns = groups + 3
+    whole = turns // DEPTH
+    lax.fori_loop(0, whole, octets(DEPTH, 0), 0)
+    lax.fori_loop(0, (turns - whole * DEPTH + 1) // 2, octets(2, whole * DEPTH), 0)
 
     def total_of(row, half, tiles, start):
         line = (row // 3) * 8 + row % 3

time: 54 us -> 52.5 us (0.972)
  Pallas kernels: 21.5 us -> 20.6 us
  waiting for transfers between devices: 15 us -> 14.4 us
    ppermute x8, waiting for transfers between devices: 11.2 us -> 10.2 us  [trade(): return lax.ppermute(value, 'dev', [(i, i ^ k) for i in range(members)])]
    pallas_call x1, Pallas kernels: 19 us -> 18.1 us  [whole_step(): pl.pallas_call(functools.partial(pair_kernel, members, slots), out_shape=...]
  transfers between devices with their start and end apart: 12 -> 12, of which waited for: 10 -> 11; matrix products, arithmetic and copies ran while one was open for 0% -> 0% of each run, Pallas kernels for 0% -> 0%
where the time goes in v9:
time: 52.5 us; the launch traced here: 52.3 us
  Pallas kernels  20.6 us (39%)
  starting transfers between devices  15.7 us (30%)
  waiting for transfers between devices  14.4 us (27%)
  between operations  1.35 us (3%)
    pallas_call x1, Pallas kernels, whole_step(): pl.pallas_call(functools.partial(pair_kernel, members, slots), out_shape=...  18.1 us
    ppermute x8, waiting for transfers between devices, trade(): return lax.ppermute(value, 'dev', [(i, i ^ k) for i in range(members)])  10.2 us
    ppermute x8, starting transfers between devices, trade(): return lax.ppermute(value, 'dev', [(i, i ^ k) for i in range(members)])  8.2 us
    ppermute x4, starting transfers between devices, cross(): return lax.ppermute(value, ('grp', 'dev'), steps)  7.52 us
    ppermute x4, waiting for transfers between devices, cross(): return lax.ppermute(value, ('grp', 'dev'), steps)  4.13 us
    pallas_call x1, Pallas kernels, whole_step(): pl.pallas_call(functools.partial(payload_kernel, slots, members), out_sha...  1.71 us
  transfers between devices with their start and end apart: 12, of which 11 were waited for; matrix products, arithmetic and copies ran while one was open for 0% of the time, Pallas kernels for 0%

profile of v9, /device:TPU:0, one launch (start us, length us, event | category | flops | bytes accessed | tf_op | source)
XLA Modules:
  0.0 52.3 jit_solution(1539344360892153265)
XLA Ops:
  1.3 0.0 copy-start.2
  1.3 1.7 %payload_kernel.1 = (f32[16,640]{1,0:T(8,128)}, f32[16,128]{1,0:T(8,128)}) custom-call(f32[3,1024]{1,0:T(4,128)} %refs_3_.3, f32[9,1024]{1,0:T(8,128)} %refs_1_.1, s32[8,128]{1,0:T(8,128)} %bitcast.5, s32[2,1024]{1,0:T(2,128)} %refs_3_.2, s32[1]{0:T(128)S(6)} %copy.8.refs_4_), custom_call_target="tpu_custom_call" | custom-call | tf_op jit(solution)/shard_map/payload_kernel/pallas_call | solution.py:511
  3.0 4.5 %collective-permute-start.2 = (f32[16,128]{1,0:T(8,128)}, f32[16,128]{1,0:T(8,128)S(1)}, u32[]{:S(2)}, u32[]{:S(2)}) collective-permute-start(f32[16,128]{1,0:T(8,128)} %get-tuple-element.9), channel_id=1, source_target_pairs={{0,28},{1,29},{2,30},{3,31},{4,8},{5,9},{6,10},{7,11},{8,4},{9,5},... | collective-permute-start | bytes 24584 | tf_op jit(solution)/shard_map/ppermute | solution.py:541
  7.5 0.8 %collective-permute-start.1 = (f32[16,128]{1,0:T(8,128)}, f32[16,128]{1,0:T(8,128)S(1)}, u32[]{:S(2)}, u32[]{:S(2)}) collective-permute-start(f32[16,128]{1,0:T(8,128)} %get-tuple-element.9), channel_id=1, source_target_pairs={{0,24},{1,25},{2,26},{3,27},{4,12},{5,13},{6,14},{7,15},{8,0},{9,1... | collective-permute-start | bytes 24584 | tf_op jit(solution)/shard_map/ppermute | solution.py:541
  8.3 0.2 collective-permute-start
  8.5 0.0 copy-done.2
  8.5 0.1 pad_bitcast_fusion.1
  8.6 0.0 copy-start.1
  8.6 0.1 pad.6.clone
  8.7 0.4 collective-permute-done.2
  9.1 0.8 %collective-permute-done.1 = f32[16,128]{1,0:T(8,128)S(1)} collective-permute-done((f32[16,128]{1,0:T(8,128)}, f32[16,128]{1,0:T(8,128)S(1)}, u32[]{:S(2)}, u32[]{:S(2)}) %collective-permute-start.1) | collective-permute-done | bytes 8224 | tf_op jit(solution)/shard_map/ppermute | solution.py:541
  9.9 3.7 %collective-permute-done = f32[16,640]{1,0:T(8,128)S(1)} collective-permute-done((f32[16,640]{1,0:T(8,128)}, f32[16,640]{1,0:T(8,128)S(1)}, u32[]{:S(2)}, u32[]{:S(2)}) %collective-permute-start) | collective-permute-done | bytes 40992 | tf_op jit(solution)/shard_map/ppermute | solution.py:530
  13.6 0.0 copy-done.1
  13.6 2.4 %collective-permute-start.5 = (f32[16,1408]{1,0:T(8,128)S(1)}, f32[16,1408]{1,0:T(8,128)S(1)}, u32[]{:S(2)}, u32[]{:S(2)}) collective-permute-start(f32[16,1408]{1,0:T(8,128)S(1)} %pad_maximum_fusion.refs_0_), channel_id=1, source_target_pairs={{0,3},{1,2},{2,1},{3,0},{4,7},{5,6},{6,5},{7,4},{8,11},{9,10},{10,... | collective-permute-start | bytes 270344 | tf_op jit(solution)/shard_map/ppermute | solution.py:530
  16.1 0.6 %collective-permute-start.4 = (f32[16,1408]{1,0:T(8,128)S(1)}, f32[16,1408]{1,0:T(8,128)S(1)}, u32[]{:S(2)}, u32[]{:S(2)}) collective-permute-start(f32[16,1408]{1,0:T(8,128)S(1)} %pad_maximum_fusion.refs_0_), channel_id=1, source_target_pairs={{0,2},{1,3},{2,0},{3,1},{4,6},{5,7},{6,4},{7,5},{8,10},{9,11},{10,... | collective-permute-start | bytes 270344 | tf_op jit(solution)/shard_map/ppermute | solution.py:530
  16.7 0.5 collective-permute-start.3
  17.2 0.1 maximum_maximum_fusion.refs_4_
  17.3 1.9 %collective-permute-done.5.refs_3_ = f32[16,1408]{1,0:T(8,128)S(1)} collective-permute-done((f32[16,1408]{1,0:T(8,128)S(1)}, f32[16,1408]{1,0:T(8,128)S(1)}, u32[]{:S(2)}, u32[]{:S(2)}) %collective-permute-start.5) | collective-permute-done | bytes 90144 | tf_op jit(solution)/shard_map/ppermute | solution.py:530
  19.1 1.5 %collective-permute-done.4.refs_2_ = f32[16,1408]{1,0:T(8,128)S(1)} collective-permute-done((f32[16,1408]{1,0:T(8,128)S(1)}, f32[16,1408]{1,0:T(8,128)S(1)}, u32[]{:S(2)}, u32[]{:S(2)}) %collective-permute-start.4) | collective-permute-done | bytes 90144 | tf_op jit(solution)/shard_map/ppermute | solution.py:530
  20.6 0.6 %collective-permute-done.3.refs_1_ = f32[16,1408]{1,0:T(8,128)S(1)} collective-permute-done((f32[16,1408]{1,0:T(8,128)S(1)}, f32[16,1408]{1,0:T(8,128)S(1)}, u32[]{:S(2)}, u32[]{:S(2)}) %collective-permute-start.3) | collective-permute-done | bytes 90144 | tf_op jit(solution)/shard_map/ppermute | solution.py:530
  21.2 18.1 %pair_kernel.1 = (f32[112,128]{1,0:T(8,128)S(1)}, f32[112,128]{1,0:T(8,128)S(1)}, f32[112,128]{1,0:T(8,128)S(1)}, f32[112,128]{1,0:T(8,128)S(1)}) custom-call(f32[16,1408]{1,0:T(8,128)S(1)} %pad_maximum_fusion.refs_0_, f32[16,1408]{1,0:T(8,128)S(1)} %collective-permute-done.3.refs_1_, f32[16,1408]{1,0:T(8,128)S(1)} %collective-permute-done.4.refs_2_, ...), custom_call_target="tpu_custom_call" | custom-call | tf_op jit(solution)/shard_map/pair_kernel/pallas_call | solution.py:567
  39.3 1.5 %collective-permute-start.6 = (f32[112,128]{1,0:T(8,128)S(1)}, f32[112,128]{1,0:T(8,128)S(1)}, u32[]{:S(2)}, u32[]{:S(2)}) collective-permute-start(f32[112,128]{1,0:T(8,128)S(1)} %get-tuple-element.11), channel_id=1, source_target_pairs={{0,3},{1,2},{2,1},{3,0},{4,7},{5,6},{6,5},{7,4},{8,11},{9,10},{10,... | collective-permute-start | bytes 172040 | tf_op jit(solution)/shard_map/ppermute | solution.py:530
  40.7 0.5 %collective-permute-start.7 = (f32[112,128]{1,0:T(8,128)S(1)}, f32[112,128]{1,0:T(8,128)S(1)}, u32[]{:S(2)}, u32[]{:S(2)}) collective-permute-start(f32[112,128]{1,0:T(8,128)S(1)} %get-tuple-element.12), channel_id=1, source_target_pairs={{0,2},{1,3},{2,0},{3,1},{4,6},{5,7},{6,4},{7,5},{8,10},{9,11},{10,... | collective-permute-start | bytes 172040 | tf_op jit(solution)/shard_map/ppermute | solution.py:530
  41.3 1.5 %collective-permute-start.8 = (f32[112,128]{1,0:T(8,128)S(1)}, f32[112,128]{1,0:T(8,128)S(1)}, u32[]{:S(2)}, u32[]{:S(2)}) collective-permute-start(f32[112,128]{1,0:T(8,128)S(1)} %get-tuple-element.13), channel_id=1, source_target_pairs={{0,1},{1,0},{2,3},{3,2},{4,5},{5,4},{6,7},{7,6},{8,9},{9,8},{10,11... | collective-permute-start | bytes 172040 | tf_op jit(solution)/shard_map/ppermute | solution.py:530
  42.8 1.6 %collective-permute-done.6 = f32[112,128]{1,0:T(8,128)S(1)} collective-permute-done((f32[112,128]{1,0:T(8,128)S(1)}, f32[112,128]{1,0:T(8,128)S(1)}, u32[]{:S(2)}, u32[]{:S(2)}) %collective-permute-start.6) | collective-permute-done | bytes 57376 | tf_op jit(solution)/shard_map/ppermute | solution.py:530
  44.4 0.5 collective-permute-done.7
  44.9 0.5 %collective-permute-done.8 = f32[112,128]{1,0:T(8,128)S(1)} collective-permute-done((f32[112,128]{1,0:T(8,128)S(1)}, f32[112,128]{1,0:T(8,128)S(1)}, u32[]{:S(2)}, u32[]{:S(2)}) %collective-permute-start.8) | collective-permute-done | bytes 57376 | tf_op jit(solution)/shard_map/ppermute | solution.py:530
  45.5 0.0 copy-start
  45.5 0.9 %collective-permute-start.9 = (f32[48,128]{1,0:T(8,128)S(1)}, f32[48,128]{1,0:T(8,128)S(1)}, u32[]{:S(2)}, u32[]{:S(2)}) collective-permute-start(f32[48,128]{1,0:T(8,128)S(1)} %get-tuple-element.14), channel_id=1, source_target_pairs={{0,4},{1,5},{2,6},{3,7},{4,0},{5,1},{6,2},{7,3},{8,12},{9,13},{10,... | collective-permute-start | bytes 73736 | tf_op jit(solution)/shard_map/ppermute | solution.py:530
  46.4 0.0 collective-permute-start.11
  46.4 2.2 %collective-permute-start.10 = (f32[16,128]{1,0:T(8,128)S(1)}, f32[16,128]{1,0:T(8,128)S(1)}, u32[]{:S(2)}, u32[]{:S(2)}) collective-permute-start(f32[16,128]{1,0:T(8,128)S(1)} %slice.14), channel_id=1, source_target_pairs={{0,8},{1,9},{2,10},{3,11},{4,28},{5,29},{6,30},{7,31},{8,16},{9,17... | collective-permute-start | bytes 24584 | tf_op jit(solution)/shard_map/ppermute | solution.py:541
  48.6 2.7 %collective-permute-done.11.refs_2_ = f32[16,128]{1,0:T(8,128)S(1)} collective-permute-done((f32[16,128]{1,0:T(8,128)S(1)}, f32[16,128]{1,0:T(8,128)S(1)}, u32[]{:S(2)}, u32[]{:S(2)}) %collective-permute-start.11) | collective-permute-done | bytes 8224 | tf_op jit(solution)/shard_map/ppermute | solution.py:541
  51.3 0.2 collective-permute-done.10.refs_1_
  51.5 0.0 collective-permute-done.9.refs_0_
  51.5 0.0 copy-done
  51.5 0.8 %finish_kernel.1 = (f32[3,1024]{1,0:T(4,128)}, f32[3,1024]{1,0:T(4,128)}) custom-call(f32[48,128]{1,0:T(8,128)S(1)} %get-tuple-element.15.own_ref, f32[48,128]{1,0:T(8,128)S(1)} %collective-permute-done.9.refs_0_, f32[16,128]{1,0:T(8,128)S(1)} %collective-permute-done.10.refs_1_, f32[16,128]{1,0:T(8,128)S(1)} %collective-permute-done.11.refs_2_, ...), custom_call_target="tpu_custom_call" | custom-call | tf_op jit(solution)/shard_map/finish_kernel/pallas_call | solution.py:599
  (7 shorter events, 0.0 us)
Async XLA Ops:
  1.3 7.2 %copy-start.2 = (s32[8,3,64]{2,0,1:T(8,128)S(1)}, s32[8,3,64]{2,0,1:T(8,128)}, u32[]{:S(2)}) copy-start(s32[8,3,64]{2,0,1:T(8,128)} %param.9) | copy-start | bytes 18436
  3.0 6.1 %collective-permute-start.2 = (f32[16,128]{1,0:T(8,128)}, f32[16,128]{1,0:T(8,128)S(1)}, u32[]{:S(2)}, u32[]{:S(2)}) collective-permute-start(f32[16,128]{1,0:T(8,128)} %get-tuple-element.9), channel_id=1, source_target_pairs={{0,28},{1,29},{2,30},{3,31},{4,8},{5,9},{6,10},{7,11},{8,4},{9,5},... | collective-permute-start | bytes 24584 | tf_op jit(solution)/shard_map/ppermute | solution.py:541
  7.5 2.4 %collective-permute-start.1 = (f32[16,128]{1,0:T(8,128)}, f32[16,128]{1,0:T(8,128)S(1)}, u32[]{:S(2)}, u32[]{:S(2)}) collective-permute-start(f32[16,128]{1,0:T(8,128)} %get-tuple-element.9), channel_id=1, source_target_pairs={{0,24},{1,25},{2,26},{3,27},{4,12},{5,13},{6,14},{7,15},{8,0},{9,1... | collective-permute-start | bytes 24584 | tf_op jit(solution)/shard_map/ppermute | solution.py:541
  8.3 5.3 %collective-permute-start = (f32[16,640]{1,0:T(8,128)}, f32[16,640]{1,0:T(8,128)S(1)}, u32[]{:S(2)}, u32[]{:S(2)}) collective-permute-start(f32[16,640]{1,0:T(8,128)} %get-tuple-element.8), channel_id=1, source_target_pairs={{0,4},{1,5},{2,6},{3,7},{4,0},{5,1},{6,2},{7,3},{8,12},{9,13},{10,... | collective-permute-start | bytes 122888 | tf_op jit(solution)/shard_map/ppermute | solution.py:530
  8.6 5.0 %copy-start.1 = (f32[16,640]{1,0:T(8,128)S(1)}, f32[16,640]{1,0:T(8,128)}, u32[]{:S(2)}) copy-start(f32[16,640]{1,0:T(8,128)} %get-tuple-element.8) | copy-start | bytes 122884
  13.6 5.5 %collective-permute-start.5 = (f32[16,1408]{1,0:T(8,128)S(1)}, f32[16,1408]{1,0:T(8,128)S(1)}, u32[]{:S(2)}, u32[]{:S(2)}) collective-permute-start(f32[16,1408]{1,0:T(8,128)S(1)} %pad_maximum_fusion.refs_0_), channel_id=1, source_target_pairs={{0,3},{1,2},{2,1},{3,0},{4,7},{5,6},{6,5},{7,4},{8,11},{9,10},{10,... | collective-permute-start | bytes 270344 | tf_op jit(solution)/shard_map/ppermute | solution.py:530
  16.1 4.5 %collective-permute-start.4 = (f32[16,1408]{1,0:T(8,128)S(1)}, f32[16,1408]{1,0:T(8,128)S(1)}, u32[]{:S(2)}, u32[]{:S(2)}) collective-permute-start(f32[16,1408]{1,0:T(8,128)S(1)} %pad_maximum_fusion.refs_0_), channel_id=1, source_target_pairs={{0,2},{1,3},{2,0},{3,1},{4,6},{5,7},{6,4},{7,5},{8,10},{9,11},{10,... | collective-permute-start | bytes 270344 | tf_op jit(solution)/shard_map/ppermute | solution.py:530
  16.7 4.5 %collective-permute-start.3 = (f32[16,1408]{1,0:T(8,128)S(1)}, f32[16,1408]{1,0:T(8,128)S(1)}, u32[]{:S(2)}, u32[]{:S(2)}) collective-permute-start(f32[16,1408]{1,0:T(8,128)S(1)} %pad_maximum_fusion.refs_0_), channel_id=1, source_target_pairs={{0,1},{1,0},{2,3},{3,2},{4,5},{5,4},{6,7},{7,6},{8,9},{9,8},{10,11... | collective-permute-start | bytes 270344 | tf_op jit(solution)/shard_map/ppermute | solution.py:530
  39.3 5.1 %collective-permute-start.6 = (f32[112,128]{1,0:T(8,128)S(1)}, f32[112,128]{1,0:T(8,128)S(1)}, u32[]{:S(2)}, u32[]{:S(2)}) collective-permute-start(f32[112,128]{1,0:T(8,128)S(1)} %get-tuple-element.11), channel_id=1, source_target_pairs={{0,3},{1,2},{2,1},{3,0},{4,7},{5,6},{6,5},{7,4},{8,11},{9,10},{10,... | collective-permute-start | bytes 172040 | tf_op jit(solution)/shard_map/ppermute | solution.py:530
  40.7 4.2 %collective-permute-start.7 = (f32[112,128]{1,0:T(8,128)S(1)}, f32[112,128]{1,0:T(8,128)S(1)}, u32[]{:S(2)}, u32[]{:S(2)}) collective-permute-start(f32[112,128]{1,0:T(8,128)S(1)} %get-tuple-element.12), channel_id=1, source_target_pairs={{0,2},{1,3},{2,0},{3,1},{4,6},{5,7},{6,4},{7,5},{8,10},{9,11},{10,... | collective-permute-start | bytes 172040 | tf_op jit(solution)/shard_map/ppermute | solution.py:530
  41.3 4.2 %collective-permute-start.8 = (f32[112,128]{1,0:T(8,128)S(1)}, f32[112,128]{1,0:T(8,128)S(1)}, u32[]{:S(2)}, u32[]{:S(2)}) collective-permute-start(f32[112,128]{1,0:T(8,128)S(1)} %get-tuple-element.13), channel_id=1, source_target_pairs={{0,1},{1,0},{2,3},{3,2},{4,5},{5,4},{6,7},{7,6},{8,9},{9,8},{10,11... | collective-permute-start | bytes 172040 | tf_op jit(solution)/shard_map/ppermute | solution.py:530
  45.5 6.0 %copy-start = (f32[3,1024]{1,0:T(4,128)S(1)}, f32[3,1024]{1,0:T(4,128)}, u32[]{:S(2)}) copy-start(f32[3,1024]{1,0:T(4,128)} %refs_3_.3) | copy-start | bytes 36868
  45.5 6.0 %collective-permute-start.9 = (f32[48,128]{1,0:T(8,128)S(1)}, f32[48,128]{1,0:T(8,128)S(1)}, u32[]{:S(2)}, u32[]{:S(2)}) collective-permute-start(f32[48,128]{1,0:T(8,128)S(1)} %get-tuple-element.14), channel_id=1, source_target_pairs={{0,4},{1,5},{2,6},{3,7},{4,0},{5,1},{6,2},{7,3},{8,12},{9,13},{10,... | collective-permute-start | bytes 73736 | tf_op jit(solution)/shard_map/ppermute | solution.py:530
  46.4 4.9 %collective-permute-start.11 = (f32[16,128]{1,0:T(8,128)S(1)}, f32[16,128]{1,0:T(8,128)S(1)}, u32[]{:S(2)}, u32[]{:S(2)}) collective-permute-start(f32[16,128]{1,0:T(8,128)S(1)} %slice.14), channel_id=1, source_target_pairs={{0,28},{1,29},{2,30},{3,31},{4,8},{5,9},{6,10},{7,11},{8,4},{9,5},... | collective-permute-start | bytes 24584 | tf_op jit(solution)/shard_map/ppermute | solution.py:541
  46.4 5.1 %collective-permute-start.10 = (f32[16,128]{1,0:T(8,128)S(1)}, f32[16,128]{1,0:T(8,128)S(1)}, u32[]{:S(2)}, u32[]{:S(2)}) collective-permute-start(f32[16,128]{1,0:T(8,128)S(1)} %slice.14), channel_id=1, source_target_pairs={{0,8},{1,9},{2,10},{3,11},{4,28},{5,29},{6,30},{7,31},{8,16},{9,17... | collective-permute-start | bytes 24584 | tf_op jit(solution)/shard_map/ppermute | solution.py:541

commit v10 on v9

--- a/solution.py
+++ b/solution.py
@@ -18,7 +18,7 @@
 PARAMS = 8
 ROWS = 16
 RIM_ROWS = 16
-DEPTH = 6
+DEPTH = 8
 
 
 def split3(value):
@@ -223,7 +223,7 @@
         def moved(rows, shift=shift):
             turned = pltpu.roll(rows, shift & (LANES - 1), axis=1)
             same = pltpu.roll(turned, shift >> 7, axis=0)
-            following = pltpu.roll(turned, (shift >> 7) + 1, axis=0)
+            following = pltpu.roll(turned, ((shift >> 7) + 1) & (slot_rows - 1), axis=0)
             return jnp.where(column < (shift & (LANES - 1)), following, same)
 
         near_list = jnp.where(wanted, moved(slot_lists[index][0]), near_list)
@@ -574,12 +574,12 @@
             pltpu.VMEM((2 * slots // CHUNK, LANES), jnp.int32),
             pltpu.SMEM((2 * slots // CHUNK, LANES), jnp.int32),
             pltpu.VMEM((2 * CHUNK, LANES), jnp.float32),
-            pltpu.VMEM((27 * slots, LANES), jnp.float32),
+            pltpu.VMEM((27 * slots + 8, LANES), jnp.float32),
             pltpu.VMEM((8 * LANES, 2 * LANES), jnp.float32),
             pltpu.VMEM((4 * 64, 2 * LANES), jnp.float32),
             pltpu.VMEM((192, 2 * LANES), jnp.float32),
-            pltpu.VMEM(((tiles + 2) * 24, LANES), jnp.float32),
-            pltpu.VMEM(((tiles + 2) * 48, LANES), jnp.float32),
+            pltpu.VMEM(((tiles + 3) * 24, LANES), jnp.float32),
+            pltpu.VMEM(((tiles + 3) * 48, LANES), jnp.float32),
             pltpu.SemaphoreType.DMA,
         ],
         compiler_params=pltpu.CompilerParams(vmem_limit_bytes=32 << 20),

time: 52.5 us -> 52.4 us (level)
  transfers between devices with their start and end apart: 12 -> 12, of which waited for: 11 -> 10; matrix products, arithmetic and copies ran while one was open for 0% -> 0% of each run, Pallas kernels for 0% -> 0%
where the time goes in v10:
time: 52.4 us; the launch traced here: 52.2 us
  Pallas kernels  20.6 us (39%)
  starting transfers between devices  15.7 us (30%)
  waiting for transfers between devices  14.2 us (27%)
  between operations  1.35 us (3%)
    pallas_call x1, Pallas kernels, whole_step(): pl.pallas_call(functools.partial(pair_kernel, members, slots), out_shape=...  18.1 us
    ppermute x8, waiting for transfers between devices, trade(): return lax.ppermute(value, 'dev', [(i, i ^ k) for i in range(members)])  10.2 us
    ppermute x8, starting transfers between devices, trade(): return lax.ppermute(value, 'dev', [(i, i ^ k) for i in range(members)])  8.17 us
    ppermute x4, starting transfers between devices, cross(): return lax.ppermute(value, ('grp', 'dev'), steps)  7.55 us
    ppermute x4, waiting for transfers between devices, cross(): return lax.ppermute(value, ('grp', 'dev'), steps)  3.98 us
    pallas_call x1, Pallas kernels, whole_step(): pl.pallas_call(functools.partial(payload_kernel, slots, members), out_sha...  1.71 us
  transfers between devices with their start and end apart: 12, of which 10 were waited for; matrix products, arithmetic and copies ran while one was open for 0% of the time, Pallas kernels for 0%

profile of v10, /device:TPU:0, one launch (start us, length us, event | category | flops | bytes accessed | tf_op | source)
XLA Modules:
  0.0 52.2 jit_solution(1143072096354963876)
XLA Ops:
  1.3 0.0 copy-start.2
  1.3 1.7 %payload_kernel.1 = (f32[16,640]{1,0:T(8,128)}, f32[16,128]{1,0:T(8,128)}) custom-call(f32[3,1024]{1,0:T(4,128)} %refs_3_.3, f32[9,1024]{1,0:T(8,128)} %refs_1_.1, s32[8,128]{1,0:T(8,128)} %bitcast.5, s32[2,1024]{1,0:T(2,128)} %refs_3_.2, s32[1]{0:T(128)S(6)} %copy.8.refs_4_), custom_call_target="tpu_custom_call" | custom-call | tf_op jit(solution)/shard_map/payload_kernel/pallas_call | solution.py:511
  3.0 4.5 %collective-permute-start.2 = (f32[16,128]{1,0:T(8,128)}, f32[16,128]{1,0:T(8,128)S(1)}, u32[]{:S(2)}, u32[]{:S(2)}) collective-permute-start(f32[16,128]{1,0:T(8,128)} %get-tuple-element.9), channel_id=1, source_target_pairs={{0,28},{1,29},{2,30},{3,31},{4,8},{5,9},{6,10},{7,11},{8,4},{9,5},... | collective-permute-start | bytes 24584 | tf_op jit(solution)/shard_map/ppermute | solution.py:541
  7.5 0.8 %collective-permute-start.1 = (f32[16,128]{1,0:T(8,128)}, f32[16,128]{1,0:T(8,128)S(1)}, u32[]{:S(2)}, u32[]{:S(2)}) collective-permute-start(f32[16,128]{1,0:T(8,128)} %get-tuple-element.9), channel_id=1, source_target_pairs={{0,24},{1,25},{2,26},{3,27},{4,12},{5,13},{6,14},{7,15},{8,0},{9,1... | collective-permute-start | bytes 24584 | tf_op jit(solution)/shard_map/ppermute | solution.py:541
  8.3 0.2 collective-permute-start
  8.5 0.0 copy-done.2
  8.5 0.1 pad_bitcast_fusion.1
  8.6 0.0 copy-start.1
  8.6 0.1 pad.6.clone
  8.7 0.4 collective-permute-done.2
  9.1 0.8 %collective-permute-done.1 = f32[16,128]{1,0:T(8,128)S(1)} collective-permute-done((f32[16,128]{1,0:T(8,128)}, f32[16,128]{1,0:T(8,128)S(1)}, u32[]{:S(2)}, u32[]{:S(2)}) %collective-permute-start.1) | collective-permute-done | bytes 8224 | tf_op jit(solution)/shard_map/ppermute | solution.py:541
  9.9 3.7 %collective-permute-done = f32[16,640]{1,0:T(8,128)S(1)} collective-permute-done((f32[16,640]{1,0:T(8,128)}, f32[16,640]{1,0:T(8,128)S(1)}, u32[]{:S(2)}, u32[]{:S(2)}) %collective-permute-start) | collective-permute-done | bytes 40992 | tf_op jit(solution)/shard_map/ppermute | solution.py:530
  13.6 0.0 copy-done.1
  13.6 2.4 %collective-permute-start.5 = (f32[16,1408]{1,0:T(8,128)S(1)}, f32[16,1408]{1,0:T(8,128)S(1)}, u32[]{:S(2)}, u32[]{:S(2)}) collective-permute-start(f32[16,1408]{1,0:T(8,128)S(1)} %pad_maximum_fusion.refs_0_), channel_id=1, source_target_pairs={{0,3},{1,2},{2,1},{3,0},{4,7},{5,6},{6,5},{7,4},{8,11},{9,10},{10,... | collective-permute-start | bytes 270344 | tf_op jit(solution)/shard_map/ppermute | solution.py:530
  16.1 0.6 %collective-permute-start.4 = (f32[16,1408]{1,0:T(8,128)S(1)}, f32[16,1408]{1,0:T(8,128)S(1)}, u32[]{:S(2)}, u32[]{:S(2)}) collective-permute-start(f32[16,1408]{1,0:T(8,128)S(1)} %pad_maximum_fusion.refs_0_), channel_id=1, source_target_pairs={{0,2},{1,3},{2,0},{3,1},{4,6},{5,7},{6,4},{7,5},{8,10},{9,11},{10,... | collective-permute-start | bytes 270344 | tf_op jit(solution)/shard_map/ppermute | solution.py:530
  16.7 0.5 collective-permute-start.3
  17.2 0.1 maximum_maximum_fusion.refs_4_
  17.3 1.9 %collective-permute-done.5.refs_3_ = f32[16,1408]{1,0:T(8,128)S(1)} collective-permute-done((f32[16,1408]{1,0:T(8,128)S(1)}, f32[16,1408]{1,0:T(8,128)S(1)}, u32[]{:S(2)}, u32[]{:S(2)}) %collective-permute-start.5) | collective-permute-done | bytes 90144 | tf_op jit(solution)/shard_map/ppermute | solution.py:530
  19.1 1.5 %collective-permute-done.4.refs_2_ = f32[16,1408]{1,0:T(8,128)S(1)} collective-permute-done((f32[16,1408]{1,0:T(8,128)S(1)}, f32[16,1408]{1,0:T(8,128)S(1)}, u32[]{:S(2)}, u32[]{:S(2)}) %collective-permute-start.4) | collective-permute-done | bytes 90144 | tf_op jit(solution)/shard_map/ppermute | solution.py:530
  20.6 0.6 %collective-permute-done.3.refs_1_ = f32[16,1408]{1,0:T(8,128)S(1)} collective-permute-done((f32[16,1408]{1,0:T(8,128)S(1)}, f32[16,1408]{1,0:T(8,128)S(1)}, u32[]{:S(2)}, u32[]{:S(2)}) %collective-permute-start.3) | collective-permute-done | bytes 90144 | tf_op jit(solution)/shard_map/ppermute | solution.py:530
  21.2 18.1 %pair_kernel.1 = (f32[112,128]{1,0:T(8,128)S(1)}, f32[112,128]{1,0:T(8,128)S(1)}, f32[112,128]{1,0:T(8,128)S(1)}, f32[112,128]{1,0:T(8,128)S(1)}) custom-call(f32[16,1408]{1,0:T(8,128)S(1)} %pad_maximum_fusion.refs_0_, f32[16,1408]{1,0:T(8,128)S(1)} %collective-permute-done.3.refs_1_, f32[16,1408]{1,0:T(8,128)S(1)} %collective-permute-done.4.refs_2_, ...), custom_call_target="tpu_custom_call" | custom-call | tf_op jit(solution)/shard_map/pair_kernel/pallas_call | solution.py:567
  39.3 1.4 %collective-permute-start.6 = (f32[112,128]{1,0:T(8,128)S(1)}, f32[112,128]{1,0:T(8,128)S(1)}, u32[]{:S(2)}, u32[]{:S(2)}) collective-permute-start(f32[112,128]{1,0:T(8,128)S(1)} %get-tuple-element.11), channel_id=1, source_target_pairs={{0,3},{1,2},{2,1},{3,0},{4,7},{5,6},{6,5},{7,4},{8,11},{9,10},{10,... | collective-permute-start | bytes 172040 | tf_op jit(solution)/shard_map/ppermute | solution.py:530
  40.7 0.6 %collective-permute-start.7 = (f32[112,128]{1,0:T(8,128)S(1)}, f32[112,128]{1,0:T(8,128)S(1)}, u32[]{:S(2)}, u32[]{:S(2)}) collective-permute-start(f32[112,128]{1,0:T(8,128)S(1)} %get-tuple-element.12), channel_id=1, source_target_pairs={{0,2},{1,3},{2,0},{3,1},{4,6},{5,7},{6,4},{7,5},{8,10},{9,11},{10,... | collective-permute-start | bytes 172040 | tf_op jit(solution)/shard_map/ppermute | solution.py:530
  41.3 1.5 %collective-permute-start.8 = (f32[112,128]{1,0:T(8,128)S(1)}, f32[112,128]{1,0:T(8,128)S(1)}, u32[]{:S(2)}, u32[]{:S(2)}) collective-permute-start(f32[112,128]{1,0:T(8,128)S(1)} %get-tuple-element.13), channel_id=1, source_target_pairs={{0,1},{1,0},{2,3},{3,2},{4,5},{5,4},{6,7},{7,6},{8,9},{9,8},{10,11... | collective-permute-start | bytes 172040 | tf_op jit(solution)/shard_map/ppermute | solution.py:530
  42.8 1.6 %collective-permute-done.6 = f32[112,128]{1,0:T(8,128)S(1)} collective-permute-done((f32[112,128]{1,0:T(8,128)S(1)}, f32[112,128]{1,0:T(8,128)S(1)}, u32[]{:S(2)}, u32[]{:S(2)}) %collective-permute-start.6) | collective-permute-done | bytes 57376 | tf_op jit(solution)/shard_map/ppermute | solution.py:530
  44.4 0.4 collective-permute-done.7
  44.8 0.6 %collective-permute-done.8 = f32[112,128]{1,0:T(8,128)S(1)} collective-permute-done((f32[112,128]{1,0:T(8,128)S(1)}, f32[112,128]{1,0:T(8,128)S(1)}, u32[]{:S(2)}, u32[]{:S(2)}) %collective-permute-start.8) | collective-permute-done | bytes 57376 | tf_op jit(solution)/shard_map/ppermute | solution.py:530
  45.5 0.0 copy-start
  45.5 0.9 %collective-permute-start.9 = (f32[48,128]{1,0:T(8,128)S(1)}, f32[48,128]{1,0:T(8,128)S(1)}, u32[]{:S(2)}, u32[]{:S(2)}) collective-permute-start(f32[48,128]{1,0:T(8,128)S(1)} %get-tuple-element.14), channel_id=1, source_target_pairs={{0,4},{1,5},{2,6},{3,7},{4,0},{5,1},{6,2},{7,3},{8,12},{9,13},{10,... | collective-permute-start | bytes 73736 | tf_op jit(solution)/shard_map/ppermute | solution.py:530
  46.4 0.0 collective-permute-start.11
  46.4 2.2 %collective-permute-start.10 = (f32[16,128]{1,0:T(8,128)S(1)}, f32[16,128]{1,0:T(8,128)S(1)}, u32[]{:S(2)}, u32[]{:S(2)}) collective-permute-start(f32[16,128]{1,0:T(8,128)S(1)} %slice.14), channel_id=1, source_target_pairs={{0,8},{1,9},{2,10},{3,11},{4,28},{5,29},{6,30},{7,31},{8,16},{9,17... | collective-permute-start | bytes 24584 | tf_op jit(solution)/shard_map/ppermute | solution.py:541
  48.6 2.7 %collective-permute-done.11.refs_2_ = f32[16,128]{1,0:T(8,128)S(1)} collective-permute-done((f32[16,128]{1,0:T(8,128)S(1)}, f32[16,128]{1,0:T(8,128)S(1)}, u32[]{:S(2)}, u32[]{:S(2)}) %collective-permute-start.11) | collective-permute-done | bytes 8224 | tf_op jit(solution)/shard_map/ppermute | solution.py:541
  51.4 0.0 collective-permute-done.10.refs_1_
  51.4 0.0 collective-permute-done.9.refs_0_
  51.4 0.0 copy-done
  51.4 0.8 %finish_kernel.1 = (f32[3,1024]{1,0:T(4,128)}, f32[3,1024]{1,0:T(4,128)}) custom-call(f32[48,128]{1,0:T(8,128)S(1)} %get-tuple-element.15.own_ref, f32[48,128]{1,0:T(8,128)S(1)} %collective-permute-done.9.refs_0_, f32[16,128]{1,0:T(8,128)S(1)} %collective-permute-done.10.refs_1_, f32[16,128]{1,0:T(8,128)S(1)} %collective-permute-done.11.refs_2_, ...), custom_call_target="tpu_custom_call" | custom-call | tf_op jit(solution)/shard_map/finish_kernel/pallas_call | solution.py:599
  (7 shorter events, 0.0 us)
Async XLA Ops:
  1.3 7.2 %copy-start.2 = (s32[8,3,64]{2,0,1:T(8,128)S(1)}, s32[8,3,64]{2,0,1:T(8,128)}, u32[]{:S(2)}) copy-start(s32[8,3,64]{2,0,1:T(8,128)} %param.9) | copy-start | bytes 18436
  3.0 6.1 %collective-permute-start.2 = (f32[16,128]{1,0:T(8,128)}, f32[16,128]{1,0:T(8,128)S(1)}, u32[]{:S(2)}, u32[]{:S(2)}) collective-permute-start(f32[16,128]{1,0:T(8,128)} %get-tuple-element.9), channel_id=1, source_target_pairs={{0,28},{1,29},{2,30},{3,31},{4,8},{5,9},{6,10},{7,11},{8,4},{9,5},... | collective-permute-start | bytes 24584 | tf_op jit(solution)/shard_map/ppermute | solution.py:541
  7.5 2.4 %collective-permute-start.1 = (f32[16,128]{1,0:T(8,128)}, f32[16,128]{1,0:T(8,128)S(1)}, u32[]{:S(2)}, u32[]{:S(2)}) collective-permute-start(f32[16,128]{1,0:T(8,128)} %get-tuple-element.9), channel_id=1, source_target_pairs={{0,24},{1,25},{2,26},{3,27},{4,12},{5,13},{6,14},{7,15},{8,0},{9,1... | collective-permute-start | bytes 24584 | tf_op jit(solution)/shard_map/ppermute | solution.py:541
  8.3 5.3 %collective-permute-start = (f32[16,640]{1,0:T(8,128)}, f32[16,640]{1,0:T(8,128)S(1)}, u32[]{:S(2)}, u32[]{:S(2)}) collective-permute-start(f32[16,640]{1,0:T(8,128)} %get-tuple-element.8), channel_id=1, source_target_pairs={{0,4},{1,5},{2,6},{3,7},{4,0},{5,1},{6,2},{7,3},{8,12},{9,13},{10,... | collective-permute-start | bytes 122888 | tf_op jit(solution)/shard_map/ppermute | solution.py:530
  8.6 5.0 %copy-start.1 = (f32[16,640]{1,0:T(8,128)S(1)}, f32[16,640]{1,0:T(8,128)}, u32[]{:S(2)}) copy-start(f32[16,640]{1,0:T(8,128)} %get-tuple-element.8) | copy-start | bytes 122884
  13.6 5.5 %collective-permute-start.5 = (f32[16,1408]{1,0:T(8,128)S(1)}, f32[16,1408]{1,0:T(8,128)S(1)}, u32[]{:S(2)}, u32[]{:S(2)}) collective-permute-start(f32[16,1408]{1,0:T(8,128)S(1)} %pad_maximum_fusion.refs_0_), channel_id=1, source_target_pairs={{0,3},{1,2},{2,1},{3,0},{4,7},{5,6},{6,5},{7,4},{8,11},{9,10},{10,... | collective-permute-start | bytes 270344 | tf_op jit(solution)/shard_map/ppermute | solution.py:530
  16.1 4.5 %collective-permute-start.4 = (f32[16,1408]{1,0:T(8,128)S(1)}, f32[16,1408]{1,0:T(8,128)S(1)}, u32[]{:S(2)}, u32[]{:S(2)}) collective-permute-start(f32[16,1408]{1,0:T(8,128)S(1)} %pad_maximum_fusion.refs_0_), channel_id=1, source_target_pairs={{0,2},{1,3},{2,0},{3,1},{4,6},{5,7},{6,4},{7,5},{8,10},{9,11},{10,... | collective-permute-start | bytes 270344 | tf_op jit(solution)/shard_map/ppermute | solution.py:530
  16.7 4.5 %collective-permute-start.3 = (f32[16,1408]{1,0:T(8,128)S(1)}, f32[16,1408]{1,0:T(8,128)S(1)}, u32[]{:S(2)}, u32[]{:S(2)}) collective-permute-start(f32[16,1408]{1,0:T(8,128)S(1)} %pad_maximum_fusion.refs_0_), channel_id=1, source_target_pairs={{0,1},{1,0},{2,3},{3,2},{4,5},{5,4},{6,7},{7,6},{8,9},{9,8},{10,11... | collective-permute-start | bytes 270344 | tf_op jit(solution)/shard_map/ppermute | solution.py:530
  39.3 5.1 %collective-permute-start.6 = (f32[112,128]{1,0:T(8,128)S(1)}, f32[112,128]{1,0:T(8,128)S(1)}, u32[]{:S(2)}, u32[]{:S(2)}) collective-permute-start(f32[112,128]{1,0:T(8,128)S(1)} %get-tuple-element.11), channel_id=1, source_target_pairs={{0,3},{1,2},{2,1},{3,0},{4,7},{5,6},{6,5},{7,4},{8,11},{9,10},{10,... | collective-permute-start | bytes 172040 | tf_op jit(solution)/shard_map/ppermute | solution.py:530
  40.7 4.2 %collective-permute-start.7 = (f32[112,128]{1,0:T(8,128)S(1)}, f32[112,128]{1,0:T(8,128)S(1)}, u32[]{:S(2)}, u32[]{:S(2)}) collective-permute-start(f32[112,128]{1,0:T(8,128)S(1)} %get-tuple-element.12), channel_id=1, source_target_pairs={{0,2},{1,3},{2,0},{3,1},{4,6},{5,7},{6,4},{7,5},{8,10},{9,11},{10,... | collective-permute-start | bytes 172040 | tf_op jit(solution)/shard_map/ppermute | solution.py:530
  41.3 4.2 %collective-permute-start.8 = (f32[112,128]{1,0:T(8,128)S(1)}, f32[112,128]{1,0:T(8,128)S(1)}, u32[]{:S(2)}, u32[]{:S(2)}) collective-permute-start(f32[112,128]{1,0:T(8,128)S(1)} %get-tuple-element.13), channel_id=1, source_target_pairs={{0,1},{1,0},{2,3},{3,2},{4,5},{5,4},{6,7},{7,6},{8,9},{9,8},{10,11... | collective-permute-start | bytes 172040 | tf_op jit(solution)/shard_map/ppermute | solution.py:530
  45.5 5.9 %copy-start = (f32[3,1024]{1,0:T(4,128)S(1)}, f32[3,1024]{1,0:T(4,128)}, u32[]{:S(2)}) copy-start(f32[3,1024]{1,0:T(4,128)} %refs_3_.3) | copy-start | bytes 36868
  45.5 5.9 %collective-permute-start.9 = (f32[48,128]{1,0:T(8,128)S(1)}, f32[48,128]{1,0:T(8,128)S(1)}, u32[]{:S(2)}, u32[]{:S(2)}) collective-permute-start(f32[48,128]{1,0:T(8,128)S(1)} %get-tuple-element.14), channel_id=1, source_target_pairs={{0,4},{1,5},{2,6},{3,7},{4,0},{5,1},{6,2},{7,3},{8,12},{9,13},{10,... | collective-permute-start | bytes 73736 | tf_op jit(solution)/shard_map/ppermute | solution.py:530
  46.4 5.0 %collective-permute-start.11 = (f32[16,128]{1,0:T(8,128)S(1)}, f32[16,128]{1,0:T(8,128)S(1)}, u32[]{:S(2)}, u32[]{:S(2)}) collective-permute-start(f32[16,128]{1,0:T(8,128)S(1)} %slice.14), channel_id=1, source_target_pairs={{0,28},{1,29},{2,30},{3,31},{4,8},{5,9},{6,10},{7,11},{8,4},{9,5},... | collective-permute-start | bytes 24584 | tf_op jit(solution)/shard_map/ppermute | solution.py:541
  46.4 5.0 %collective-permute-start.10 = (f32[16,128]{1,0:T(8,128)S(1)}, f32[16,128]{1,0:T(8,128)S(1)}, u32[]{:S(2)}, u32[]{:S(2)}) collective-permute-start(f32[16,128]{1,0:T(8,128)S(1)} %slice.14), channel_id=1, source_target_pairs={{0,8},{1,9},{2,10},{3,11},{4,28},{5,29},{6,30},{7,31},{8,16},{9,17... | collective-permute-start | bytes 24584 | tf_op jit(solution)/shard_map/ppermute | solution.py:541
